TPU v7x, 32 devices: a whole 2x2x4 slice. The times are simulated.
32 devices in a mesh: patch: 2 (over x), epoch: 16 (over z, y, core).
Axes of the slice: x: 2, y: 2, z: 4, core: 2. Of those that a mesh axis runs over, the one named last changes fastest.
Arguments:
- epoch_images: float32 [32, 64, 4096], P(('patch', 'epoch')), parts along dimension 0, may hold values from -8 to 8
- mask_words: int32 [32, 1, 128], P(('patch', 'epoch')), parts along dimension 0, may hold values from -2147483648 to 2147483647, as said below
- coefficients: float32 [32, 49, 3], P('patch'), parts along dimension 0, may hold values from -2 to 2
- epoch_order: int32 [32], P('patch'), parts along dimension 0, may hold values from 0 to 15, each once
Outputs:
- difference: float32 [32, 32, 4096], P(('patch', 'epoch')), parts along dimension 0
There are 2 independent parts, one for each index of `patch`. A program takes and returns all parts, laid end to end along the dimension named above; each array names one. Nothing has to cross between parts.
Inputs may be any that keep to these rules, and one draw needn't show every extreme that they name: `mask_words`: bit b of word w in band n of an epoch marks column 32 w + b of rows n * 64 to (n + 1) * 64 - 1 of that epoch valid (1) or masked (0), bit 31 being the sign bit; some cells are masked in every epoch. A permutation: image slot e uses the coefficients of catalog epoch epoch_order[e].
All inputs are finite; a program needn't handle non-finite values.
Results may differ from a plain program's by a relative error of at most 0.000057.
Values sent between devices are 32-bit elements; how exact they have to be, the bound alone decides.
No kernel may reach another device: no remote copies, remote signals or barrier semaphores. Data moves between devices by JAX's collectives and lax.ppermute only.
A program may use at most 64 MiB of HBM per device.

v0:
```python
import math

import jax
import jax.numpy as jnp
import numpy as np
from jax import lax
from jax.sharding import PartitionSpec as P

HALF = 15
MARGIN = 16
BAND = 64


gauss_widths = (1.5, 3.0, 6.0)
gauss_degrees = (6, 4, 2)


def extended(cells, sides, width):
    for axis, dim in sides:
        count = lax.axis_size(axis)
        ends = count - 1
        head = lax.slice_in_dim(cells, 0, width, axis=dim)
        tail = lax.slice_in_dim(cells, cells.shape[dim] - width, cells.shape[dim], axis=dim)
        cells = jnp.concatenate(
            [
                lax.ppermute(tail, axis, [(i, (i + 1) % count) for i in range(ends)]),
                cells,
                lax.ppermute(head, axis, [((i + 1) % count, i) for i in range(ends)]),
            ],
            axis=dim,
        )
    return cells


def basis_filters(half_width):
    offsets = jnp.arange(-half_width, half_width + 1).astype(jnp.float32)
    result = []
    for spread_width, degree in zip(gauss_widths, gauss_degrees):
        envelope = jnp.exp(-offsets * offsets / (2.0 * spread_width * spread_width)) / (
            math.sqrt(2.0 * math.pi) * spread_width
        )
        for vert_power in range(degree + 1):
            result.append(envelope * (offsets / spread_width) ** vert_power)
    return jnp.stack(result)


def kernel_pairs():
    result = []
    first_index = 0
    for degree in gauss_degrees:
        for vert_power in range(degree + 1):
            for horiz_power in range(degree + 1 - vert_power):
                result.append((first_index + vert_power, first_index + horiz_power))
        first_index = first_index + degree + 1
    return result


def unpack_valid(mask_words):
    bit_places = jnp.arange(32, dtype=jnp.int32)
    bit_values = jnp.right_shift(mask_words[..., None], bit_places) & 1
    word_shape = mask_words.shape
    return bit_values.reshape(word_shape[0], word_shape[1], word_shape[2] * 32).astype(jnp.float32)


def shift_table(tap_count, inner_cols, outer_cols):
    taps_axis = jnp.arange(tap_count)[:, None, None]
    inner_axis = jnp.arange(inner_cols)[None, :, None]
    outer_axis = jnp.arange(outer_cols)[None, None, :]
    return (inner_axis - outer_axis == taps_axis).astype(jnp.float32)


def vertical_matrices(filters, rows_out, padded_rows):
    tap_count = filters.shape[1]
    out_rows = jnp.arange(rows_out)[:, None]
    in_rows = jnp.arange(padded_rows)[None, :]
    places = in_rows - out_rows - MARGIN + HALF
    one_hot = (places[None] == jnp.arange(tap_count)[:, None, None]).astype(jnp.float32)
    return jnp.einsum("jd,drt->jrt", filters, one_hot, precision=lax.Precision.HIGHEST)


def spatial_terms(col_start, col_count, total_columns, rows_out):
    columns = (
        2.0 * (col_start + jnp.arange(col_count)).astype(jnp.float32) + 1.0
    ) / total_columns - 1.0
    row_pos = (2.0 * jnp.arange(rows_out).astype(jnp.float32) + 1.0) / rows_out - 1.0
    return jnp.stack(
        [
            jnp.ones((rows_out, col_count), jnp.float32),
            jnp.broadcast_to(columns[None, :], (rows_out, col_count)),
            jnp.broadcast_to(row_pos[:, None], (rows_out, col_count)),
        ]
    )


def shards(epoch_images, mask_words, coefficients, epoch_order):
    slot_count, padded_rows, total_columns = epoch_images.shape
    rows_out = padded_rows - 2 * MARGIN
    band_valid = unpack_valid(mask_words)
    valid_mask = jnp.repeat(band_valid, BAND, axis=1)
    part_total = jnp.sum(valid_mask * epoch_images, axis=0)
    part_count = jnp.sum(band_valid, axis=0)
    filters = basis_filters(HALF)
    pair_list = kernel_pairs()
    vert_table = np.zeros((len(pair_list), filters.shape[0]), np.float32)
    horiz_table = np.zeros((len(pair_list), filters.shape[0]), np.float32)
    for kernel_index, pair_value in enumerate(pair_list):
        vert_table[kernel_index, pair_value[0]] = 1.0
        horiz_table[kernel_index, pair_value[1]] = 1.0
    vert_pick = jnp.asarray(vert_table)
    horiz_filters = jnp.dot(jnp.asarray(horiz_table), filters, precision=lax.Precision.HIGHEST)
    vert_mats = vertical_matrices(filters, rows_out, padded_rows)
    full_sum, full_count = (
        lax.psum_scatter(part_total, "epoch", scatter_dimension=1, tiled=True),
        lax.psum_scatter(part_count, "epoch", scatter_dimension=1, tiled=True),
    )
    template = full_sum / jnp.maximum(jnp.repeat(full_count, BAND, axis=0), 1.0)
    slab_cols = template.shape[1]
    rimmed = extended(template, (("epoch", 1),), HALF)
    vertical = jnp.einsum("jrt,tc->jrc", vert_mats, rimmed, precision=lax.Precision.HIGHEST)
    picked = jnp.einsum("kj,jrc->krc", vert_pick, vertical, precision=lax.Precision.HIGHEST)
    horiz_mats = jnp.einsum(
        "kd,dso->kso",
        horiz_filters,
        shift_table(horiz_filters.shape[1], slab_cols + 2 * HALF, slab_cols),
        precision=lax.Precision.HIGHEST,
    )
    convolved = jnp.einsum("krs,kso->kro", picked, horiz_mats, precision=lax.Precision.HIGHEST)
    spatial = spatial_terms(lax.axis_index("epoch") * slab_cols, slab_cols, total_columns, rows_out)
    term_count = coefficients.shape[1] * coefficients.shape[2]
    basis_images = (convolved[:, None] * spatial[None]).reshape(term_count, rows_out * slab_cols)
    coef_table = coefficients[epoch_order].reshape(coefficients.shape[0], term_count)
    models = jnp.dot(
        coef_table,
        basis_images,
        precision=lax.Precision.HIGHEST,
        preferred_element_type=jnp.float32,
    ).reshape(coefficients.shape[0], rows_out, slab_cols)
    model_image = lax.all_to_all(models, "epoch", split_axis=0, concat_axis=2, tiled=True)
    centre = epoch_images[:, MARGIN : MARGIN + rows_out]
    return valid_mask[:, MARGIN : MARGIN + rows_out] * (centre - model_image)


def solution(mesh):
    placed = (
        P(("patch", "epoch"), None, None),
        P(("patch", "epoch"), None, None),
        P("patch", None, None),
        P("patch"),
    )
    return jax.shard_map(
        shards,
        mesh=mesh,
        in_specs=placed,
        out_specs=P(("patch", "epoch"), None, None),
        check_vma=False,
    )
```

profile of v0, /device:TPU:0, one launch (start us, length us, event | category | flops | bytes accessed | tf_op | source)
XLA Modules:
  0.0 205.0 jit_solution(17101479756316634492)
XLA Ops:
  6.8 0.8 shift_right_arithmetic.37
  7.6 0.1 shift_right_arithmetic.42
  7.9 2.0 copy.29
  10.1 1.1 multiply_bitcast_fusion
  11.8 0.3 fusion.9
  12.2 9.9 %fusion.2 = f32[49,286,256]{2,0,1:T(8,128)} fusion(s32[286,256]{1,0:T(8,128)S(1)} %iota_subtract_fusion, f32[49]{0:T(128)S(1)} %copy-done.3, f32[31]{0:T(128)S(1)} %fusion.70, f32[49]{0:T(128)S(1)} %copy-done.17, f32[31]{0:T(128)S(1)} %get-tuple-element.15, f32[49]{0:T(128)S(1)} %copy-done.16, f32[31]{0:T(128)S(1)} %get-tuple-element.9, ...), kind=kOutput, calls=%fused_computation.4 | convolution fusion | flops 1336894976 | bytes 14648000 | tf_op jit(solution)/shard_map/kd,dso->kso/dot_general | solution.py:121
  22.1 53.7 %reduce-scatter.7.cloned.1.call-done = f32[256,1]{1,0:T(8,128)} async-done(((f32[4096,1]{1,0:T(8,128)}), f32[256,1]{1,0:T(8,128)}) %reduce-scatter.7.cloned.1.call-update) | async-done | bytes 1040
  75.8 0.9 maximum_bitcast_fusion
  76.8 59.1 %reduce-scatter.5.cloned.1.call-done = f32[64,256]{1,0:T(8,128)} async-done(((f32[64,4096]{1,0:T(8,128)}), f32[64,256]{1,0:T(8,128)}) %reduce-scatter.5.cloned.1.call-update) | async-done | bytes 65552 | tf_op jit(solution)/shard_map/reduce_scatter | solution.py:113
  135.9 0.8 broadcast_divide_fusion
  136.8 1.3 collective-permute-start
  138.1 1.3 collective-permute-start.1
  139.5 0.6 gather_fusion
  140.0 0.1 copy.18
  140.2 2.6 %collective-permute-done.1 = f32[64,15]{1,0:T(8,128)S(1)} collective-permute-done((f32[64,15]{1,0:T(8,128)S(1)}, f32[64,15]{1,0:T(8,128)S(1)}, u32[]{:S(2)}, u32[]{:S(2)}) %collective-permute-start.1) | collective-permute-done | bytes 3872 | tf_op jit(solution)/shard_map/ppermute | solution.py:28
  142.8 0.8 fusion.11
  143.6 2.5 %fusion.7 = f32[49,32,286]{2,0,1:T(8,128)S(1)} fusion(f32[49,15,1]{0,1,2:T(8,128)S(1)} %copy-done.2, f32[15,32,286]{2,1,0:T(8,128)S(1)} %fusion.11), kind=kOutput, calls=%fused_computation.12 | convolution fusion | flops 80720640 | bytes 2345852 | tf_op jit(solution)/shard_map/kj,jrc->krc/dot_general | solution.py:120
  146.1 23.3 %fusion = f32[49,32,256]{2,1,0:T(8,128)S(1)} fusion(f32[49,286,256]{2,0,1:T(8,128)} %fusion.2, f32[49,32,286]{2,0,1:T(8,128)S(1)} %fusion.7), kind=kOutput, calls=%fused_computation.1 | convolution fusion | flops 1377632256 | bytes 17749760 | tf_op jit(solution)/shard_map/krs,kso->kro/dot_general | solution.py:127
  169.4 0.6 broadcast_multiply_fusion
  170.0 0.7 slice_bitcast_fusion
  170.8 5.2 %fusion.3 = f32[16,32,256]{2,0,1:T(8,128)S(1)} fusion(f32[32,256,147]{1,0,2:T(8,128)S(1)} %slice_bitcast_fusion, f32[16,147]{0,1:T(8,128)S(1)} %reshape.229), kind=kOutput, calls=%fused_computation.5 | convolution fusion | flops 231211008 | bytes 5350592 | tf_op jit(solution)/shard_map/dot_general | solution.py:132
  175.9 0.3 copy.25
  176.2 21.0 %all_to_all.18 = f32[16,32,256]{2,1,0:T(8,128)S(1)} all-to-all(f32[16,32,256]{2,1,0:T(8,128)S(1)} %copy.25), channel_id=1, replica_groups=mesh['patch'=2,'epoch'=16] {'epoch'}, dimensions={0} | all-to-all | bytes 1048576 | tf_op jit(solution)/shard_map/all_to_all | solution.py:138
  197.3 0.9 subtract_multiply_fusion
  (81 shorter events, 1.2 us)
Async XLA Ops:
  6.5 132.9 %copy-start = (f32[16,49,3]{1,0,2:T(8,128)S(1)}, f32[16,49,3]{1,0,2:T(8,128)}, u32[]{:S(2)}) copy-start(f32[16,49,3]{1,0,2:T(8,128)} %param.8) | copy-start | bytes 28228
  6.5 5.5 %copy-start.3 = (f32[49]{0:T(128)S(1)}, f32[49]{0:T(128)}, u32[]{:S(2)}) copy-start(f32[49]{0:T(128)} %constant.101) | copy-start | bytes 592
  6.5 5.5 %copy-start.4 = (f32[49]{0:T(128)S(1)}, f32[49]{0:T(128)}, u32[]{:S(2)}) copy-start(f32[49]{0:T(128)} %constant.73) | copy-start | bytes 592
  6.5 5.6 %copy-start.5 = (f32[49]{0:T(128)S(1)}, f32[49]{0:T(128)}, u32[]{:S(2)}) copy-start(f32[49]{0:T(128)} %constant.75) | copy-start | bytes 592
  6.5 5.6 %copy-start.6 = (f32[49]{0:T(128)S(1)}, f32[49]{0:T(128)}, u32[]{:S(2)}) copy-start(f32[49]{0:T(128)} %constant.77) | copy-start | bytes 592
  6.6 5.6 %copy-start.7 = (f32[49]{0:T(128)S(1)}, f32[49]{0:T(128)}, u32[]{:S(2)}) copy-start(f32[49]{0:T(128)} %constant.79) | copy-start | bytes 592
  6.6 5.6 %copy-start.8 = (f32[49]{0:T(128)S(1)}, f32[49]{0:T(128)}, u32[]{:S(2)}) copy-start(f32[49]{0:T(128)} %constant.81) | copy-start | bytes 592
  6.6 5.6 %copy-start.9 = (f32[49]{0:T(128)S(1)}, f32[49]{0:T(128)}, u32[]{:S(2)}) copy-start(f32[49]{0:T(128)} %constant.83) | copy-start | bytes 592
  6.6 5.6 %copy-start.10 = (f32[49]{0:T(128)S(1)}, f32[49]{0:T(128)}, u32[]{:S(2)}) copy-start(f32[49]{0:T(128)} %constant.85) | copy-start | bytes 592
  6.6 5.6 %copy-start.11 = (f32[49]{0:T(128)S(1)}, f32[49]{0:T(128)}, u32[]{:S(2)}) copy-start(f32[49]{0:T(128)} %constant.87) | copy-start | bytes 592
  6.6 5.6 %copy-start.12 = (f32[49]{0:T(128)S(1)}, f32[49]{0:T(128)}, u32[]{:S(2)}) copy-start(f32[49]{0:T(128)} %constant.89) | copy-start | bytes 592
  6.6 5.6 %copy-start.13 = (f32[49]{0:T(128)S(1)}, f32[49]{0:T(128)}, u32[]{:S(2)}) copy-start(f32[49]{0:T(128)} %constant.91) | copy-start | bytes 592
  6.6 5.5 %copy-start.14 = (f32[49]{0:T(128)S(1)}, f32[49]{0:T(128)}, u32[]{:S(2)}) copy-start(f32[49]{0:T(128)} %constant.93) | copy-start | bytes 592
  6.7 5.5 %copy-start.15 = (f32[49]{0:T(128)S(1)}, f32[49]{0:T(128)}, u32[]{:S(2)}) copy-start(f32[49]{0:T(128)} %constant.95) | copy-start | bytes 592
  6.7 5.5 %copy-start.16 = (f32[49]{0:T(128)S(1)}, f32[49]{0:T(128)}, u32[]{:S(2)}) copy-start(f32[49]{0:T(128)} %constant.97) | copy-start | bytes 592
  6.7 5.5 %copy-start.17 = (f32[49]{0:T(128)S(1)}, f32[49]{0:T(128)}, u32[]{:S(2)}) copy-start(f32[49]{0:T(128)} %constant.99) | copy-start | bytes 592
  6.7 3.4 %copy-start.1 = (f32[1,64,4096]{2,1,0:T(8,128)S(1)}, f32[1,64,4096]{2,1,0:T(8,128)}, u32[]{:S(2)}) copy-start(f32[1,64,4096]{2,1,0:T(8,128)} %param.6) | copy-start | bytes 3145732
  6.7 4.9 %copy-start.18 = (s32[16]{0:T(128)S(1)}, s32[16]{0:T(128)}, u32[]{:S(2)}) copy-start(s32[16]{0:T(128)} %param.9) | copy-start | bytes 196
  6.7 69.1 %reduce-scatter.7.cloned.1.call-start = ((), (), s32[]{:S(2)}) async-start(), calls=%async_computation.4 | async-start | bytes 2228224
  9.9 126.0 %reduce-scatter.5.cloned.1.call-start = ((), (), s32[]{:S(2)}) async-start(), calls=%async_computation.3 | async-start | bytes 1114112 | tf_op jit(solution)/shard_map/reduce_scatter | solution.py:113
  22.1 121.5 %copy-start.2 = (f32[49,15,1]{0,1,2:T(8,128)S(1)}, f32[49,15,1]{0,1,2:T(8,128)}, u32[]{:S(2)}) copy-start(f32[49,15,1]{0,1,2:T(8,128)} %constant.102) | copy-start | bytes 8824
  136.8 3.4 %collective-permute-start = (f32[64,15]{1,0:T(8,128)S(1)}, f32[64,15]{1,0:T(8,128)S(1)}, u32[]{:S(2)}, u32[]{:S(2)}) collective-permute-start(f32[64,15]{1,0:T(8,128)S(1)} %get-tuple-element.5), channel_id=1, source_target_pairs={{0,1},{1,2},{2,3},{3,4},{4,5},{5,6},{6,7},{7,8},{8,9},{9,10},{10,1... | collective-permute-start | bytes 11528 | tf_op jit(solution)/shard_map/ppermute | solution.py:26
  138.1 4.7 %collective-permute-start.1 = (f32[64,15]{1,0:T(8,128)S(1)}, f32[64,15]{1,0:T(8,128)S(1)}, u32[]{:S(2)}, u32[]{:S(2)}) collective-permute-start(f32[64,15]{1,0:T(8,128)S(1)} %get-tuple-element.6), channel_id=1, source_target_pairs={{1,0},{2,1},{3,2},{4,3},{5,4},{6,5},{7,6},{8,7},{9,8},{10,9},{11,1... | collective-permute-start | bytes 11528 | tf_op jit(solution)/shard_map/ppermute | solution.py:28
Sparse Core Ops, SparseCore 0:
  11.3 64.5 reduce-scatter.6
  79.4 56.4 reduce-scatter.4
where the time goes:
time: 205 us
  waiting for transfers between devices  115 us (56%)
  matrix products  41.8 us (20%)
  blocking collectives  21 us (10%)
  between operations  13.9 us (7%)
  local copies, waits for them, and re-layouts  5.4 us (3%)
  other arithmetic  4.66 us (2%)
  starting transfers between devices  2.66 us (1%)
    reduce_scatter x1, waiting for transfers between devices, shards(): lax.psum_scatter(part_total, 'epoch', scatter_dimension=1, tiled=True)  59.1 us
    unnamed x3, waiting for transfers between devices  53.8 us
    dot_general x1, matrix products, shards(): jnp.einsum('krs,kso->kro', picked, horiz_mats, precision=lax.Precision.HI...  23.3 us
    all_to_all x1, blocking collectives, shards(): lax.all_to_all(models, 'epoch', split_axis=0, concat_axis=2, tiled=True)  21 us
    dot_general x1, matrix products, shards(): jnp.einsum('kd,dso->kso', horiz_filters, shift_table(horiz_filters.shape[...  9.86 us
    dot_general x1, matrix products, shards(): jnp.dot(coef_table, basis_images, precision=lax.Precision.HIGHEST, prefer...  5.15 us
  transfers between devices with their start and end apart: 4, of which 3 were waited for; matrix products, arithmetic and copies ran while one was open for 7% of the time, Pallas kernels for 0%

commit v1 on v0

v1 whole, which is shorter than its diff:
```python
import functools
import math

import jax
import jax.numpy as jnp
import numpy as np
from jax import lax
from jax.experimental import pallas as pl
from jax.experimental.pallas import tpu as pltpu
from jax.sharding import PartitionSpec as P

HALF = 15
MARGIN = 16
BAND = 64
LANES = 128
SHIFTS = 4
GROUPS = 8

gauss_widths = (1.5, 3.0, 6.0)
gauss_degrees = (6, 4, 2)


def basis_filters():
    offsets = np.arange(-HALF, HALF + 1).astype(np.float64)
    result = []
    for width, degree in zip(gauss_widths, gauss_degrees):
        envelope = np.exp(-offsets * offsets / (2.0 * width * width)) / (math.sqrt(2.0 * math.pi) * width)
        for power in range(degree + 1):
            result.append(envelope * (offsets / width) ** power)
    return np.stack(result)


def kernel_pairs():
    result = []
    first_index = 0
    for degree in gauss_degrees:
        for vert_power in range(degree + 1):
            for horiz_power in range(degree + 1 - vert_power):
                result.append((first_index + vert_power, first_index + horiz_power))
        first_index = first_index + degree + 1
    return result


def tables(rows, padded_rows):
    filters = basis_filters()
    count, taps = filters.shape
    pairs = kernel_pairs()
    vert_pick = np.zeros((len(pairs), count + 1), np.float32)
    horiz_pick = np.zeros((len(pairs), count + 1), np.float32)
    for index, (vert, horiz) in enumerate(pairs):
        vert_pick[index, vert] = 1.0
        horiz_pick[index, horiz] = 1.0
    span = SHIFTS * GROUPS
    horiz = np.zeros((count + 1, span), np.float64)
    horiz[:count, :taps] = filters
    horiz_lanes = np.repeat(horiz, padded_rows, axis=1).astype(np.float32)
    vert = np.zeros((count, rows, padded_rows), np.float64)
    for row in range(rows):
        start = row + MARGIN - HALF
        vert[:, row, start : start + taps] = filters
    vert_lanes = np.tile(vert, (1, 1, SHIFTS)).astype(np.float32)
    return vert_pick, horiz_pick, horiz_lanes, vert_lanes


def valid_lanes(words, first_column, columns):
    word_count = words.shape[1]
    byte_row = lax.broadcasted_iota(jnp.int32, (8, word_count), 0)
    octets = jnp.right_shift(jnp.broadcast_to(words, (8, word_count)), 8 * (byte_row & 3)) & 255
    octets = octets.astype(jnp.float32).astype(jnp.bfloat16)
    word_row = lax.broadcasted_iota(jnp.int32, (word_count, columns), 0)
    word_col = jnp.right_shift(lax.broadcasted_iota(jnp.int32, (word_count, columns), 1) + first_column, 5)
    spread = jnp.where(word_row == word_col, 1.0, 0.0).astype(jnp.bfloat16)
    wide = jnp.dot(octets, spread, preferred_element_type=jnp.float32).astype(jnp.int32)
    lane = lax.broadcasted_iota(jnp.int32, (8, columns), 1)
    row = lax.broadcasted_iota(jnp.int32, (8, columns), 0)
    bit = jnp.right_shift(wide, lane & 7) & 1
    bit = jnp.where(row == (jnp.right_shift(lane, 3) & 3), bit, 0).astype(jnp.float32)
    return jnp.sum(bit, axis=0, keepdims=True)


def mask_kernel(words_ref, image_ref, masked_ref, valid_ref):
    columns = image_ref.shape[1]
    valid = valid_lanes(words_ref[...], pl.program_id(0) * columns, columns)
    valid_ref[...] = valid
    row = lax.broadcasted_iota(jnp.int32, image_ref.shape, 0)
    masked_ref[...] = jnp.where(row == 0, valid, valid * image_ref[...])


def masked_image(words, image, blocks):
    rows, columns = image.shape
    width = columns // blocks
    return pl.pallas_call(
        mask_kernel,
        grid=(blocks,),
        in_specs=[
            pl.BlockSpec(words.shape, lambda i: (0, 0)),
            pl.BlockSpec((rows, width), lambda i: (0, i)),
        ],
        out_specs=[
            pl.BlockSpec((rows, width), lambda i: (0, i)),
            pl.BlockSpec((1, width), lambda i: (0, i)),
        ],
        out_shape=[
            jax.ShapeDtypeStruct((rows, columns), jnp.float32),
            jax.ShapeDtypeStruct((1, columns), jnp.float32),
        ],
        name="mask_image",
    )(words, image)


def weight_kernel(place_ref, order_ref, coef_ref, vert_pick_ref, horiz_pick_ref, horiz_ref, vert_ref, high_ref, low_ref):
    count, rows, lanes = vert_ref.shape
    coef = coef_ref[0]
    terms = []
    for term in range(3):
        table = lax.dot_general(
            vert_pick_ref[...] * coef[:, term : term + 1],
            horiz_pick_ref[...],
            (((0,), (0,)), ((), ())),
            precision=lax.Precision.HIGHEST,
            preferred_element_type=jnp.float32,
        )
        terms.append(
            jnp.dot(table, horiz_ref[...], precision=lax.Precision.HIGHEST, preferred_element_type=jnp.float32)
        )
    row = lax.broadcasted_iota(jnp.int32, (rows, lanes), 0).astype(jnp.float32)
    row_pos = (2.0 * row + 1.0) / rows - 1.0
    for group in range(GROUPS):
        sums = []
        for term in range(3):
            total = jnp.zeros((rows, lanes), jnp.float32)
            for index in range(count):
                taps = terms[term][index : index + 1, group * lanes : (group + 1) * lanes]
                total = total + taps * vert_ref[index]
            sums.append(total)
        for place, weight in enumerate((sums[0] + row_pos * sums[2], sums[1])):
            high = weight.astype(jnp.bfloat16)
            low = (weight - high.astype(jnp.float32)).astype(jnp.bfloat16)
            first = (2 * group + place) * rows
            high_ref[first : first + rows] = high
            low_ref[first : first + rows] = low


def weights(coefficients, epoch_order, slot, rows, padded_rows):
    vert_pick, horiz_pick, horiz_lanes, vert_lanes = tables(rows, padded_rows)
    kernels, poly = coefficients.shape[1:]
    shape = (2 * GROUPS * rows, SHIFTS * padded_rows)
    whole = lambda array: pl.BlockSpec(array.shape, lambda i, place, order: (0,) * array.ndim)
    return pl.pallas_call(
        weight_kernel,
        grid_spec=pltpu.PrefetchScalarGridSpec(
            num_scalar_prefetch=2,
            grid=(1,),
            in_specs=[
                pl.BlockSpec((1, kernels, poly), lambda i, place, order: (order[place[0]], 0, 0)),
                whole(vert_pick),
                whole(horiz_pick),
                whole(horiz_lanes),
                whole(vert_lanes),
            ],
            out_specs=[pl.BlockSpec(shape, lambda i, place, order: (0, 0))] * 2,
        ),
        out_shape=[jax.ShapeDtypeStruct(shape, jnp.bfloat16)] * 2,
        name="kernel_weights",
    )(slot, epoch_order, coefficients, vert_pick, horiz_pick, horiz_lanes, vert_lanes)


def difference_kernel(
    high_ref, low_ref, template_ref, image_ref, valid_ref, out_ref, wide_high, wide_low, partial
):
    padded_rows, columns = template_ref.shape
    rows = out_ref.shape[0]
    domain = wide_high.shape[1]
    template = jnp.concatenate(
        [template_ref[...], jnp.zeros((padded_rows, domain - columns), jnp.float32)], axis=1
    )
    for shift in range(SHIFTS):
        moved = template if shift == 0 else pltpu.roll(template, domain - shift, 1)
        high = moved.astype(jnp.bfloat16)
        low = (moved - high.astype(jnp.float32)).astype(jnp.bfloat16)
        wide_high[shift * padded_rows : (shift + 1) * padded_rows] = high
        wide_low[shift * padded_rows : (shift + 1) * padded_rows] = low

    tile = 384

    def product(index, carry):
        lanes = pl.ds(pl.multiple_of(index * tile, tile), tile)
        high = wide_high[:, lanes]
        total = jnp.dot(high_ref[...], high, preferred_element_type=jnp.float32)
        total += jnp.dot(low_ref[...], high, preferred_element_type=jnp.float32)
        total += jnp.dot(high_ref[...], wide_low[:, lanes], preferred_element_type=jnp.float32)
        partial[:, lanes] = total
        return carry

    lax.fori_loop(0, domain // tile, product, 0)
    size = 2 * rows
    total = jnp.zeros((size, domain), jnp.float32)
    for group in range(GROUPS):
        amount = (HALF - SHIFTS * group) % domain
        total = total + pltpu.roll(partial[group * size : (group + 1) * size], amount, 1)
    column = lax.broadcasted_iota(jnp.int32, (rows, columns), 1).astype(jnp.float32)
    column = (2.0 * column + 1.0) / columns - 1.0
    model = total[:rows, :columns] + column * total[rows:, :columns]
    out_ref[...] = valid_ref[...] * (image_ref[...] - model)


def difference(high, low, template, centre, valid):
    padded_rows, columns = template.shape
    rows = centre.shape[0]
    domain = columns + LANES
    vmem = pl.BlockSpec(memory_space=pltpu.VMEM)
    return pl.pallas_call(
        difference_kernel,
        in_specs=[vmem] * 5,
        out_specs=vmem,
        out_shape=jax.ShapeDtypeStruct((rows, columns), jnp.float32),
        scratch_shapes=[
            pltpu.VMEM((SHIFTS * padded_rows, domain), jnp.bfloat16),
            pltpu.VMEM((SHIFTS * padded_rows, domain), jnp.bfloat16),
            pltpu.VMEM((2 * GROUPS * rows, domain), jnp.float32),
        ],
        name="difference",
    )(high, low, template, centre, valid)


def exchange(cells, bit):
    count = lax.axis_size("epoch")
    return lax.ppermute(cells, "epoch", [(i, i ^ (1 << bit)) for i in range(count)])


def shards(epoch_images, mask_words, coefficients, epoch_order):
    padded_rows, columns = epoch_images.shape[1:]
    rows = padded_rows - 2 * MARGIN
    place = lax.axis_index("epoch")
    bits = lax.axis_size("epoch").bit_length() - 1
    image = epoch_images[0]
    cells, valid = masked_image(mask_words[0], image, 2)
    high, low = weights(coefficients, epoch_order, place[None].astype(jnp.int32), rows, padded_rows)
    for bit in range(bits):
        width = cells.shape[1] // 2
        side = jnp.right_shift(place, bit) & 1
        keep = lax.dynamic_slice_in_dim(cells, side * width, width, 1)
        send = lax.dynamic_slice_in_dim(cells, (1 - side) * width, width, 1)
        cells = keep + exchange(send, bit)
    cells = cells / jnp.maximum(cells[:1], 1.0)
    for bit in reversed(range(bits)):
        other = exchange(cells, bit)
        side = jnp.right_shift(place, bit) & 1
        cells = jnp.where(
            side == 0, jnp.concatenate([cells, other], axis=1), jnp.concatenate([other, cells], axis=1)
        )
    centre = image[MARGIN : MARGIN + rows]
    return difference(high, low, cells, centre, valid)[None]


def solution(mesh):
    placed = (
        P(("patch", "epoch"), None, None),
        P(("patch", "epoch"), None, None),
        P("patch", None, None),
        P("patch"),
    )
    return jax.shard_map(
        shards,
        mesh=mesh,
        in_specs=placed,
        out_specs=P(("patch", "epoch"), None, None),
        check_vma=False,
    )
```

time: 205 us -> 58.9 us (0.29)
  waiting for transfers between devices: 115 us -> 20.1 us
  matrix products: 41.8 us -> 0 us
  blocking collectives: 21 us -> 0 us
  Pallas kernels: 0 us -> 18.9 us
  between operations: 13.9 us -> 0.1 us
  starting transfers between devices: 2.66 us -> 15 us
  other arithmetic: 4.66 us -> 1.33 us
  local copies, waits for them, and re-layouts: 5.4 us -> 3.11 us
    reduce_scatter x1 -> x0, waiting for transfers between devices: 59.1 us -> none  [shards(): lax.psum_scatter(part_total, 'epoch', scatter_dimension=1, tiled=True)]
    unnamed x3 -> x0, waiting for transfers between devices: 53.8 us -> none
    dot_general x6 -> x0, matrix products: 41.8 us -> none  [the longest x1 23.3 us: shards(): jnp.einsum('krs,kso->kro', picked, horiz_mats, precision=lax.Precision.HI...]
    all_to_all x1 -> x0, blocking collectives: 21 us -> none  [shards(): lax.all_to_all(models, 'epoch', split_axis=0, concat_axis=2, tiled=True)]
    pallas_call x0 -> x3, Pallas kernels: none -> 18.9 us  [the longest x1 12.1 us: difference(): pl.pallas_call(difference_kernel, in_specs=[vmem] * 5, out_specs=vmem, ou...]
    ppermute x2 -> x8, waiting for transfers between devices: 2.62 us -> 20.1 us  [exchange(): lax.ppermute(cells, 'epoch', [(i, i ^ 1 << bit) for i in range(count)])]
    ppermute x2 -> x8, starting transfers between devices: 2.58 us -> 15 us  [exchange(): lax.ppermute(cells, 'epoch', [(i, i ^ 1 << bit) for i in range(count)])]
  transfers between devices with their start and end apart: 4 -> 8, of which waited for: 3 -> 7; matrix products, arithmetic and copies ran while one was open for 7% -> 3% of each run, Pallas kernels for 0% -> 8%
where the time goes in v1:
time: 58.9 us; the launch traced here: 58.6 us
  waiting for transfers between devices  20.1 us (34%)
  Pallas kernels  18.9 us (32%)
  starting transfers between devices  15 us (25%)
  local copies, waits for them, and re-layouts  3.11 us (5%)
  other arithmetic  1.33 us (2%)
    ppermute x8, waiting for transfers between devices, exchange(): lax.ppermute(cells, 'epoch', [(i, i ^ 1 << bit) for i in range(count)])  20.1 us
    ppermute x8, starting transfers between devices, exchange(): lax.ppermute(cells, 'epoch', [(i, i ^ 1 << bit) for i in range(count)])  15 us
    pallas_call x1, Pallas kernels, difference(): pl.pallas_call(difference_kernel, in_specs=[vmem] * 5, out_specs=vmem, ou...  12.1 us
    pallas_call x1, Pallas kernels, weights(): pl.pallas_call(weight_kernel, grid_spec=pltpu.PrefetchScalarGridSpec(num_...  4.48 us
    pallas_call x1, Pallas kernels, masked_image(): pl.pallas_call(mask_kernel, grid=(blocks,), in_specs=[pl.BlockSpec(words....  2.32 us
    dynamic_slice x4, local copies, waits for them, and re-layouts, shards(): send = lax.dynamic_slice_in_dim(cells, (1 - side) * width, width, 1)  1.22 us
    select_n x4, other arithmetic, shards(): jnp.where(side == 0, jnp.concatenate([cells, other], axis=1), jnp.concate...  1.2 us
  transfers between devices with their start and end apart: 8, of which 7 were waited for; matrix products, arithmetic and copies ran while one was open for 3% of the time, Pallas kernels for 8%

profile of v1, /device:TPU:0, one launch (start us, length us, event | category | flops | bytes accessed | tf_op | source)
XLA Modules:
  0.0 58.6 jit_solution(1498096691439570318)
XLA Ops:
  0.0 2.3 %mask_image.1 = (f32[64,4096]{1,0:T(8,128)}, f32[1,4096]{1,0:T(1,128)}) custom-call(s32[1,128]{1,0:T(1,128)} %bitcast.9, f32[64,4096]{1,0:T(8,128)} %bitcast.7), custom_call_target="tpu_custom_call" | custom-call | tf_op jit(solution)/shard_map/mask_image/pallas_call | solution.py:92
  2.3 1.2 %constant_dynamic-slice_fusion.3 = f32[64,2048]{1,0:T(8,128)S(1)} fusion(f32[64,4096]{1,0:T(8,128)} %get-tuple-element.11, s32[]{:T(128)S(6)} %select_n.61), kind=kLoop, calls=%fused_computation.13 | loop fusion | bytes 1048580 | tf_op jit(solution)/shard_map/dynamic_slice | solution.py:243
  3.5 0.6 collective-permute-start
  4.1 1.5 %collective-permute-done = f32[64,2048]{1,0:T(8,128)S(1)} collective-permute-done((f32[64,2048]{1,0:T(8,128)S(1)}, f32[64,2048]{1,0:T(8,128)S(1)}, u32[]{:S(2)}, u32[]{:S(2)}) %collective-permute-start) | collective-permute-done | bytes 524320 | tf_op jit(solution)/shard_map/ppermute | solution.py:228
  5.6 0.1 dynamic-slice_add_fusion
  5.7 2.9 %collective-permute-start.1 = (f32[64,1024]{1,0:T(8,128)S(1)}, f32[64,1024]{1,0:T(8,128)S(1)}, u32[]{:S(2)}, u32[]{:S(2)}) collective-permute-start(f32[64,1024]{1,0:T(8,128)S(1)} %constant_dynamic-slice_fusion.2), channel_id=1, source_target_pairs={{0,2},{1,3},{2,0},{3,1},{4,6},{5,7},{6,4},{7,5},{8,10},{9,11},{10,... | collective-permute-start | bytes 786440 | tf_op jit(solution)/shard_map/ppermute | solution.py:228
  8.6 6.6 %collective-permute-done.1 = f32[64,1024]{1,0:T(8,128)S(1)} collective-permute-done((f32[64,1024]{1,0:T(8,128)S(1)}, f32[64,1024]{1,0:T(8,128)S(1)}, u32[]{:S(2)}, u32[]{:S(2)}) %collective-permute-start.1) | collective-permute-done | bytes 262176 | tf_op jit(solution)/shard_map/ppermute | solution.py:228
  15.3 1.9 %collective-permute-start.2 = (f32[64,512]{1,0:T(8,128)S(1)}, f32[64,512]{1,0:T(8,128)S(1)}, u32[]{:S(2)}, u32[]{:S(2)}) collective-permute-start(f32[64,512]{1,0:T(8,128)S(1)} %constant_dynamic-slice_fusion.1), channel_id=1, source_target_pairs={{0,4},{1,5},{2,6},{3,7},{4,0},{5,1},{6,2},{7,3},{8,12},{9,13},{10,... | collective-permute-start | bytes 393224 | tf_op jit(solution)/shard_map/ppermute | solution.py:228
  17.2 3.2 %collective-permute-done.2 = f32[64,512]{1,0:T(8,128)S(1)} collective-permute-done((f32[64,512]{1,0:T(8,128)S(1)}, f32[64,512]{1,0:T(8,128)S(1)}, u32[]{:S(2)}, u32[]{:S(2)}) %collective-permute-start.2) | collective-permute-done | bytes 131104 | tf_op jit(solution)/shard_map/ppermute | solution.py:228
  20.4 2.9 %collective-permute-start.3 = (f32[64,256]{1,0:T(8,128)S(1)}, f32[64,256]{1,0:T(8,128)S(1)}, u32[]{:S(2)}, u32[]{:S(2)}) collective-permute-start(f32[64,256]{1,0:T(8,128)S(1)} %constant_dynamic-slice_fusion), channel_id=1, source_target_pairs={{0,8},{1,9},{2,10},{3,11},{4,12},{5,13},{6,14},{7,15},{8,0},{9,1},... | collective-permute-start | bytes 196616 | tf_op jit(solution)/shard_map/ppermute | solution.py:228
  23.2 2.4 %collective-permute-done.3 = f32[64,256]{1,0:T(8,128)S(1)} collective-permute-done((f32[64,256]{1,0:T(8,128)S(1)}, f32[64,256]{1,0:T(8,128)S(1)}, u32[]{:S(2)}, u32[]{:S(2)}) %collective-permute-start.3) | collective-permute-done | bytes 65568 | tf_op jit(solution)/shard_map/ppermute | solution.py:228
  25.6 2.9 %collective-permute-start.4 = (f32[64,256]{1,0:T(8,128)S(1)}, f32[64,256]{1,0:T(8,128)S(1)}, u32[]{:S(2)}, u32[]{:S(2)}) collective-permute-start(f32[64,256]{1,0:T(8,128)S(1)} %broadcast_divide_fusion), channel_id=1, source_target_pairs={{0,8},{1,9},{2,10},{3,11},{4,12},{5,13},{6,14},{7,15},{8,0},{9,1},... | collective-permute-start | bytes 196616 | tf_op jit(solution)/shard_map/ppermute | solution.py:228
  28.6 2.5 %collective-permute-done.4 = f32[64,256]{1,0:T(8,128)S(1)} collective-permute-done((f32[64,256]{1,0:T(8,128)S(1)}, f32[64,256]{1,0:T(8,128)S(1)}, u32[]{:S(2)}, u32[]{:S(2)}) %collective-permute-start.4) | collective-permute-done | bytes 65568 | tf_op jit(solution)/shard_map/ppermute | solution.py:228
  31.1 2.1 %collective-permute-start.5 = (f32[64,512]{1,0:T(8,128)S(1)}, f32[64,512]{1,0:T(8,128)S(1)}, u32[]{:S(2)}, u32[]{:S(2)}) collective-permute-start(f32[64,512]{1,0:T(8,128)S(1)} %maximum_select_fusion.3), channel_id=1, source_target_pairs={{0,4},{1,5},{2,6},{3,7},{4,0},{5,1},{6,2},{7,3},{8,12},{9,13},{10,... | collective-permute-start | bytes 393224 | tf_op jit(solution)/shard_map/ppermute | solution.py:228
  33.2 2.9 %collective-permute-done.5 = f32[64,512]{1,0:T(8,128)S(1)} collective-permute-done((f32[64,512]{1,0:T(8,128)S(1)}, f32[64,512]{1,0:T(8,128)S(1)}, u32[]{:S(2)}, u32[]{:S(2)}) %collective-permute-start.5) | collective-permute-done | bytes 131104 | tf_op jit(solution)/shard_map/ppermute | solution.py:228
  36.2 1.7 %collective-permute-start.6 = (f32[64,1024]{1,0:T(8,128)S(1)}, f32[64,1024]{1,0:T(8,128)S(1)}, u32[]{:S(2)}, u32[]{:S(2)}) collective-permute-start(f32[64,1024]{1,0:T(8,128)S(1)} %maximum_select_fusion.2), channel_id=1, source_target_pairs={{0,2},{1,3},{2,0},{3,1},{4,6},{5,7},{6,4},{7,5},{8,10},{9,11},{10,... | collective-permute-start | bytes 786440 | tf_op jit(solution)/shard_map/ppermute | solution.py:228
  37.9 1.0 %copy.9.coef_ref = f32[16,49,3]{2,1,0:T(8,128)} copy(f32[16,49,3]{1,0,2:T(8,128)S(1)} %copy-done.2) | data formatting | bytes 18816 | tf_op args[2]
  38.9 4.5 %kernel_weights.1 = (bf16[512,256]{1,0:T(8,128)(2,1)}, bf16[512,256]{1,0:T(8,128)(2,1)}) custom-call(s32[1]{0:T(128)} %bitcast.place_ref, s32[16]{0:T(128)} %order_ref.1, f32[16,49,3]{2,1,0:T(8,128)} %copy.9.coef_ref, f32[49,16]{1,0:T(8,128)} %constant.32.clone.vert_pick_ref, f32[49,16]{1,0:T(8,128)} %constant.33.clone.horiz_pick_ref, ...), custom_call_target="tpu_custom_call" | custom-call | tf_op jit(solution)/shard_map/kernel_weights/pallas_call | solution.py:149
  43.4 0.0 collective-permute-done.6
  43.4 0.1 collective-permute-start.7
  43.5 0.8 %slice_bitcast_fusion.image_ref = f32[32,4096]{1,0:T(8,128)} fusion(f32[1,64,4096]{2,1,0:T(8,128)S(1)} %copy-done), kind=kLoop, calls=%fused_computation.2 | loop fusion | bytes 1048576 | tf_op jit(solution)/shard_map/slice | solution.py:252
  44.4 1.0 %collective-permute-done.7 = f32[64,2048]{1,0:T(8,128)S(1)} collective-permute-done((f32[64,2048]{1,0:T(8,128)S(1)}, f32[64,2048]{1,0:T(8,128)S(1)}, u32[]{:S(2)}, u32[]{:S(2)}) %collective-permute-start.7) | collective-permute-done | bytes 524320 | tf_op jit(solution)/shard_map/ppermute | solution.py:228
  45.4 1.1 %maximum_select_fusion.template_ref = f32[64,4096]{1,0:T(8,128)} fusion(f32[64,2048]{1,0:T(8,128)S(1)} %collective-permute-done.7, f32[64,2048]{1,0:T(8,128)S(1)} %maximum_select_fusion.1, pred[]{:T(512)S(6)} %eq.12), kind=kLoop, calls=%fused_computation | loop fusion | flops 786432 | bytes 2097153 | tf_op jit(solution)/shard_map/jit(_where)/select_n | solution.py:249
  46.5 12.1 %difference.1 = f32[32,4096]{1,0:T(8,128)} custom-call(bf16[512,256]{1,0:T(8,128)(2,1)} %get-tuple-element.9.high_ref, bf16[512,256]{1,0:T(8,128)(2,1)} %get-tuple-element.10.low_ref, f32[64,4096]{1,0:T(8,128)} %maximum_select_fusion.template_ref, f32[32,4096]{1,0:T(8,128)} %slice_bitcast_fusion.image_ref, f32[1,4096]{1,0:T(1,128)} %get-tuple-element.12.valid_ref), custom_call_target="tpu_custom_call" | custom-call | tf_op jit(solution)/shard_map/difference/pallas_call | solution.py:212
  (17 shorter events, 0.2 us)
Async XLA Ops:
  2.3 3.3 %copy-start.1 = (f32[64,4096]{1,0:T(8,128)S(1)}, f32[64,4096]{1,0:T(8,128)}, u32[]{:S(2)}) copy-start(f32[64,4096]{1,0:T(8,128)} %get-tuple-element.11) | copy-start | bytes 3145732
  3.5 2.1 %collective-permute-start = (f32[64,2048]{1,0:T(8,128)S(1)}, f32[64,2048]{1,0:T(8,128)S(1)}, u32[]{:S(2)}, u32[]{:S(2)}) collective-permute-start(f32[64,2048]{1,0:T(8,128)S(1)} %constant_dynamic-slice_fusion.3), channel_id=1, source_target_pairs={{0,1},{1,0},{2,3},{3,2},{4,5},{5,4},{6,7},{7,6},{8,9},{9,8},{10,11... | collective-permute-start | bytes 1572872 | tf_op jit(solution)/shard_map/ppermute | solution.py:228
  5.7 9.5 %collective-permute-start.1 = (f32[64,1024]{1,0:T(8,128)S(1)}, f32[64,1024]{1,0:T(8,128)S(1)}, u32[]{:S(2)}, u32[]{:S(2)}) collective-permute-start(f32[64,1024]{1,0:T(8,128)S(1)} %constant_dynamic-slice_fusion.2), channel_id=1, source_target_pairs={{0,2},{1,3},{2,0},{3,1},{4,6},{5,7},{6,4},{7,5},{8,10},{9,11},{10,... | collective-permute-start | bytes 786440 | tf_op jit(solution)/shard_map/ppermute | solution.py:228
  15.3 5.0 %collective-permute-start.2 = (f32[64,512]{1,0:T(8,128)S(1)}, f32[64,512]{1,0:T(8,128)S(1)}, u32[]{:S(2)}, u32[]{:S(2)}) collective-permute-start(f32[64,512]{1,0:T(8,128)S(1)} %constant_dynamic-slice_fusion.1), channel_id=1, source_target_pairs={{0,4},{1,5},{2,6},{3,7},{4,0},{5,1},{6,2},{7,3},{8,12},{9,13},{10,... | collective-permute-start | bytes 393224 | tf_op jit(solution)/shard_map/ppermute | solution.py:228
  20.4 5.2 %collective-permute-start.3 = (f32[64,256]{1,0:T(8,128)S(1)}, f32[64,256]{1,0:T(8,128)S(1)}, u32[]{:S(2)}, u32[]{:S(2)}) collective-permute-start(f32[64,256]{1,0:T(8,128)S(1)} %constant_dynamic-slice_fusion), channel_id=1, source_target_pairs={{0,8},{1,9},{2,10},{3,11},{4,12},{5,13},{6,14},{7,15},{8,0},{9,1},... | collective-permute-start | bytes 196616 | tf_op jit(solution)/shard_map/ppermute | solution.py:228
  25.6 5.4 %collective-permute-start.4 = (f32[64,256]{1,0:T(8,128)S(1)}, f32[64,256]{1,0:T(8,128)S(1)}, u32[]{:S(2)}, u32[]{:S(2)}) collective-permute-start(f32[64,256]{1,0:T(8,128)S(1)} %broadcast_divide_fusion), channel_id=1, source_target_pairs={{0,8},{1,9},{2,10},{3,11},{4,12},{5,13},{6,14},{7,15},{8,0},{9,1},... | collective-permute-start | bytes 196616 | tf_op jit(solution)/shard_map/ppermute | solution.py:228
  31.1 5.1 %collective-permute-start.5 = (f32[64,512]{1,0:T(8,128)S(1)}, f32[64,512]{1,0:T(8,128)S(1)}, u32[]{:S(2)}, u32[]{:S(2)}) collective-permute-start(f32[64,512]{1,0:T(8,128)S(1)} %maximum_select_fusion.3), channel_id=1, source_target_pairs={{0,4},{1,5},{2,6},{3,7},{4,0},{5,1},{6,2},{7,3},{8,12},{9,13},{10,... | collective-permute-start | bytes 393224 | tf_op jit(solution)/shard_map/ppermute | solution.py:228
  33.2 4.6 %copy-start.2 = (f32[16,49,3]{1,0,2:T(8,128)S(1)}, f32[16,49,3]{1,0,2:T(8,128)}, u32[]{:S(2)}) copy-start(f32[16,49,3]{1,0,2:T(8,128)} %param.10) | copy-start | bytes 28228
  36.2 7.2 %collective-permute-start.6 = (f32[64,1024]{1,0:T(8,128)S(1)}, f32[64,1024]{1,0:T(8,128)S(1)}, u32[]{:S(2)}, u32[]{:S(2)}) collective-permute-start(f32[64,1024]{1,0:T(8,128)S(1)} %maximum_select_fusion.2), channel_id=1, source_target_pairs={{0,2},{1,3},{2,0},{3,1},{4,6},{5,7},{6,4},{7,5},{8,10},{9,11},{10,... | collective-permute-start | bytes 786440 | tf_op jit(solution)/shard_map/ppermute | solution.py:228
  38.9 4.6 %copy-start = (f32[1,64,4096]{2,1,0:T(8,128)S(1)}, f32[1,64,4096]{2,1,0:T(8,128)}, u32[]{:S(2)}) copy-start(f32[1,64,4096]{2,1,0:T(8,128)} %param.8) | copy-start | bytes 3145732
  43.4 2.0 %collective-permute-start.7 = (f32[64,2048]{1,0:T(8,128)S(1)}, f32[64,2048]{1,0:T(8,128)S(1)}, u32[]{:S(2)}, u32[]{:S(2)}) collective-permute-start(f32[64,2048]{1,0:T(8,128)S(1)} %maximum_select_fusion.1), channel_id=1, source_target_pairs={{0,1},{1,0},{2,3},{3,2},{4,5},{5,4},{6,7},{7,6},{8,9},{9,8},{10,11... | collective-permute-start | bytes 1572872 | tf_op jit(solution)/shard_map/ppermute | solution.py:228

commit v2 on v1

v2 whole, which is shorter than its diff:
```python
import math

import jax
import jax.numpy as jnp
import numpy as np
from jax import lax
from jax.experimental import pallas as pl
from jax.experimental.pallas import tpu as pltpu
from jax.sharding import PartitionSpec as P

HALF = 15
MARGIN = 16
BAND = 64
LANES = 128
SHIFTS = 8
GROUPS = 4
GRANT = 20 << 20

gauss_widths = (1.5, 3.0, 6.0)
gauss_degrees = (6, 4, 2)


def basis_filters():
    offsets = np.arange(-HALF, HALF + 1).astype(np.float64)
    result = []
    for width, degree in zip(gauss_widths, gauss_degrees):
        envelope = np.exp(-offsets * offsets / (2.0 * width * width)) / (math.sqrt(2.0 * math.pi) * width)
        for power in range(degree + 1):
            result.append(envelope * (offsets / width) ** power)
    return np.stack(result)


def kernel_pairs():
    result = []
    first_index = 0
    for degree in gauss_degrees:
        for vert_power in range(degree + 1):
            for horiz_power in range(degree + 1 - vert_power):
                result.append((first_index + vert_power, first_index + horiz_power))
        first_index = first_index + degree + 1
    return result


def tables(rows, padded_rows):
    filters = basis_filters()
    count, taps = filters.shape
    pairs = kernel_pairs()
    vert_pick = np.zeros((count + 1, len(pairs)), np.float32)
    horiz_pick = np.zeros((len(pairs), count + 1), np.float32)
    for index, (vert, horiz) in enumerate(pairs):
        vert_pick[vert, index] = 1.0
        horiz_pick[index, horiz] = 1.0
    span = SHIFTS * GROUPS
    horiz = np.zeros((count + 1, span), np.float64)
    horiz[:count, :taps] = filters
    horiz_lanes = np.repeat(horiz, padded_rows, axis=1).astype(np.float32)
    vert = np.zeros((count, rows, padded_rows), np.float64)
    for row in range(rows):
        start = row + MARGIN - HALF
        vert[:, row, start : start + taps] = filters
    vert_lanes = np.tile(vert, (1, 1, SHIFTS)).astype(np.float32)
    return vert_pick, horiz_pick, horiz_lanes, vert_lanes


def valid_lanes(words, first_column, columns):
    word_count = words.shape[1]
    byte_row = lax.broadcasted_iota(jnp.int32, (8, word_count), 0)
    octets = jnp.right_shift(jnp.broadcast_to(words, (8, word_count)), 8 * (byte_row & 3)) & 255
    octets = octets.astype(jnp.float32).astype(jnp.bfloat16)
    word_row = lax.broadcasted_iota(jnp.int32, (word_count, columns), 0)
    word_col = jnp.right_shift(lax.broadcasted_iota(jnp.int32, (word_count, columns), 1) + first_column, 5)
    spread = jnp.where(word_row == word_col, 1.0, 0.0).astype(jnp.bfloat16)
    wide = jnp.dot(octets, spread, preferred_element_type=jnp.float32).astype(jnp.int32)
    lane = lax.broadcasted_iota(jnp.int32, (8, columns), 1)
    row = lax.broadcasted_iota(jnp.int32, (8, columns), 0)
    bit = jnp.right_shift(wide, lane & 7) & 1
    bit = jnp.where(row == (jnp.right_shift(lane, 3) & 3), bit, 0).astype(jnp.float32)
    return jnp.sum(bit, axis=0, keepdims=True)


def mask_kernel(side_ref, words_ref, image_ref, masked_ref, valid_ref):
    columns = image_ref.shape[1]
    valid = valid_lanes(words_ref[...], side_ref[0] * columns, columns)
    valid_ref[...] = valid
    row = lax.broadcasted_iota(jnp.int32, image_ref.shape, 0)
    masked_ref[...] = jnp.where(row == 0, valid, valid * image_ref[...])


def masked_half(side, words, image):
    rows, columns = image.shape
    half = columns // 2
    return pl.pallas_call(
        mask_kernel,
        grid_spec=pltpu.PrefetchScalarGridSpec(
            num_scalar_prefetch=1,
            grid=(1,),
            in_specs=[
                pl.BlockSpec(words.shape, lambda i, side: (0, 0)),
                pl.BlockSpec((rows, half), lambda i, side: (0, side[0])),
            ],
            out_specs=[
                pl.BlockSpec((rows, half), lambda i, side: (0, 0)),
                pl.BlockSpec((1, half), lambda i, side: (0, 0)),
            ],
        ),
        out_shape=[
            jax.ShapeDtypeStruct((rows, half), jnp.float32),
            jax.ShapeDtypeStruct((1, half), jnp.float32),
        ],
        compiler_params=pltpu.CompilerParams(vmem_limit_bytes=GRANT),
        cost_estimate=pl.CostEstimate(flops=rows * half, bytes_accessed=8 * rows * half, transcendentals=0),
        name="mask_half",
    )(side[None], words, image)


def weight_kernel(place_ref, order_ref, coef_ref, vert_pick_ref, horiz_pick_ref, horiz_ref, vert_ref, high_ref, low_ref):
    count, rows, lanes = vert_ref.shape
    exact = dict(precision=lax.Precision.HIGHEST, preferred_element_type=jnp.float32)
    catalog = order_ref[place_ref[0]]
    picked = [vert_pick_ref[...] * coef_ref[term, pl.ds(catalog, 1), :] for term in range(3)]
    table = jnp.dot(jnp.concatenate(picked, axis=0), horiz_pick_ref[...], **exact)
    taps = jnp.dot(table, horiz_ref[...], **exact)
    step = count + 1
    row = lax.broadcasted_iota(jnp.int32, (rows, lanes), 0).astype(jnp.float32)
    row_pos = (2.0 * row + 1.0) / rows - 1.0
    for group in range(GROUPS):
        sums = []
        for term in range(3):
            total = jnp.zeros((rows, lanes), jnp.float32)
            for index in range(count):
                line = term * step + index
                total = total + taps[line : line + 1, group * lanes : (group + 1) * lanes] * vert_ref[index]
            sums.append(total)
        for place, weight in enumerate((sums[0] + row_pos * sums[2], sums[1])):
            high = weight.astype(jnp.bfloat16)
            low = (weight - high.astype(jnp.float32)).astype(jnp.bfloat16)
            first = (2 * group + place) * rows
            high_ref[first : first + rows] = high
            low_ref[first : first + rows] = low


def weights(coefficients, epoch_order, slot, rows, padded_rows):
    arrays = (jnp.transpose(coefficients, (2, 0, 1)),) + tables(rows, padded_rows)
    shape = (2 * GROUPS * rows, SHIFTS * padded_rows)
    smem = pl.BlockSpec(memory_space=pltpu.SMEM)
    vmem = pl.BlockSpec(memory_space=pltpu.VMEM)
    return pl.pallas_call(
        weight_kernel,
        in_specs=[smem, smem] + [vmem] * len(arrays),
        out_specs=[vmem, vmem],
        out_shape=[jax.ShapeDtypeStruct(shape, jnp.bfloat16)] * 2,
        compiler_params=pltpu.CompilerParams(vmem_limit_bytes=GRANT),
        cost_estimate=pl.CostEstimate(flops=10**8, bytes_accessed=2 * 10**6, transcendentals=0),
        name="kernel_weights",
    )(slot[None], epoch_order, *arrays)


def half_model(high_ref, low_ref, template_ref, first_column, total_columns, wide_high, wide_low, partial):
    padded_rows, columns = template_ref.shape
    domain = wide_high.shape[1]
    size = partial.shape[0] // GROUPS
    rows = size // 2
    template = jnp.concatenate(
        [template_ref[...], jnp.zeros((padded_rows, domain - columns), jnp.float32)], axis=1
    )
    for shift in range(SHIFTS):
        moved = template if shift == 0 else pltpu.roll(template, domain - shift, 1)
        high = moved.astype(jnp.bfloat16)
        low = (moved - high.astype(jnp.float32)).astype(jnp.bfloat16)
        wide_high[shift * padded_rows : (shift + 1) * padded_rows] = high
        wide_low[shift * padded_rows : (shift + 1) * padded_rows] = low
    for lanes in (slice(0, columns // 2), slice(columns // 2, domain)):
        high = wide_high[:, lanes]
        total = jnp.dot(high_ref[...], high, preferred_element_type=jnp.float32)
        total += jnp.dot(low_ref[...], high, preferred_element_type=jnp.float32)
        total += jnp.dot(high_ref[...], wide_low[:, lanes], preferred_element_type=jnp.float32)
        partial[:, lanes] = total
    total = jnp.zeros((size, domain), jnp.float32)
    for group in range(GROUPS):
        amount = (HALF - SHIFTS * group) % domain
        total = total + pltpu.roll(partial[group * size : (group + 1) * size], amount, 1)
    lane = lax.broadcasted_iota(jnp.int32, (rows, domain), 1)
    column = first_column + jnp.where(lane < columns + LANES // 2, lane, lane - domain)
    position = (2.0 * column.astype(jnp.float32) + 1.0) / total_columns - 1.0
    return total[:rows] + position * total[rows:]


def near_kernel(side_ref, high_ref, low_ref, template_ref, model_ref, wide_high, wide_low, partial):
    half = template_ref.shape[1]
    model_ref[...] = half_model(
        high_ref, low_ref, template_ref, side_ref[0] * half, 2 * half, wide_high, wide_low, partial
    )


def far_kernel(
    side_ref, high_ref, low_ref, template_ref, near_ref, image_ref, near_valid_ref, far_valid_ref, out_ref,
    wide_high, wide_low, partial,
):
    half = template_ref.shape[1]
    rows = out_ref.shape[0]
    side = side_ref[0]
    far = half_model(
        high_ref, low_ref, template_ref, (1 - side) * half, 2 * half, wide_high, wide_low, partial
    )
    near = near_ref[...]
    lane = lax.broadcasted_iota(jnp.int32, (rows, LANES), 1)
    centre = slice(MARGIN, MARGIN + rows)
    for model, other, valid_ref, place in ((near, far, near_valid_ref, side), (far, near, far_valid_ref, 1 - side)):
        spill = other[:, half:]
        left = jnp.where((place == 1) & (lane < LANES // 2), spill, 0.0)
        right = jnp.where((place == 0) & (lane >= LANES // 2), spill, 0.0)
        whole = jnp.concatenate(
            [model[:, :LANES] + left, model[:, LANES : half - LANES], model[:, half - LANES : half] + right], axis=1
        )
        lanes = pl.ds(pl.multiple_of(place * half, half), half)
        out_ref[:, lanes] = valid_ref[...] * (image_ref[centre, lanes] - whole)


def model_scratch(rows, padded_rows, half):
    domain = half + LANES
    return [
        pltpu.VMEM((SHIFTS * padded_rows, domain), jnp.bfloat16),
        pltpu.VMEM((SHIFTS * padded_rows, domain), jnp.bfloat16),
        pltpu.VMEM((2 * GROUPS * rows, domain), jnp.float32),
    ]


def model_cost(rows, padded_rows, half):
    flops = 12 * GROUPS * rows * SHIFTS * padded_rows * (half + LANES)
    return pl.CostEstimate(flops=flops, bytes_accessed=10 * padded_rows * half, transcendentals=0)


def near_model(side, high, low, template, rows):
    padded_rows, half = template.shape
    vmem = pl.BlockSpec(memory_space=pltpu.VMEM)
    return pl.pallas_call(
        near_kernel,
        in_specs=[pl.BlockSpec(memory_space=pltpu.SMEM)] + [vmem] * 3,
        out_specs=vmem,
        out_shape=jax.ShapeDtypeStruct((rows, half + LANES), jnp.float32),
        scratch_shapes=model_scratch(rows, padded_rows, half),
        compiler_params=pltpu.CompilerParams(vmem_limit_bytes=GRANT),
        cost_estimate=model_cost(rows, padded_rows, half),
        name="near_model",
    )(side[None], high, low, template)


def difference(side, high, low, template, near, image, near_valid, far_valid):
    padded_rows, half = template.shape
    rows = near.shape[0]
    vmem = pl.BlockSpec(memory_space=pltpu.VMEM)
    return pl.pallas_call(
        far_kernel,
        in_specs=[pl.BlockSpec(memory_space=pltpu.SMEM)] + [vmem] * 7,
        out_specs=vmem,
        out_shape=jax.ShapeDtypeStruct((rows, 2 * half), jnp.float32),
        scratch_shapes=model_scratch(rows, padded_rows, half),
        compiler_params=pltpu.CompilerParams(vmem_limit_bytes=GRANT),
        cost_estimate=model_cost(rows, padded_rows, half),
        name="difference",
    )(side[None], high, low, template, near, image, near_valid, far_valid)


def exchange(cells, bit):
    count = lax.axis_size("epoch")
    return lax.ppermute(cells, "epoch", [(i, i ^ (1 << bit)) for i in range(count)])


def halves(cells, side):
    width = cells.shape[1] // 2
    keep = lax.dynamic_slice_in_dim(cells, side * width, width, 1)
    send = lax.dynamic_slice_in_dim(cells, (1 - side) * width, width, 1)
    return keep, send


def shards(epoch_images, mask_words, coefficients, epoch_order):
    padded_rows, columns = epoch_images.shape[1:]
    rows = padded_rows - 2 * MARGIN
    place = lax.axis_index("epoch").astype(jnp.int32)
    bits = lax.axis_size("epoch").bit_length() - 1
    sides = [jnp.right_shift(place, bit) & 1 for bit in range(bits)]
    image, words = epoch_images[0], mask_words[0]

    send, far_valid = masked_half(1 - sides[0], words, image)
    other = exchange(send, 0)
    keep, near_valid = masked_half(sides[0], words, image)
    cells = keep + other
    keep, send = halves(cells, sides[1])
    other = exchange(send, 1)
    high, low = weights(coefficients, epoch_order, place, rows, padded_rows)
    cells = keep + other
    cells, high, low = lax.optimization_barrier((cells, high, low))
    for bit in range(2, bits - 1):
        keep, send = halves(cells, sides[bit])
        cells = keep + exchange(send, bit)
    cells = cells + exchange(cells, bits - 1)
    cells = cells / jnp.maximum(cells[:1], 1.0)
    for bit in reversed(range(1, bits - 1)):
        other = exchange(cells, bit)
        cells = jnp.where(
            sides[bit] == 0, jnp.concatenate([cells, other], axis=1), jnp.concatenate([other, cells], axis=1)
        )
    other = exchange(cells, 0)
    near = near_model(sides[0], high, low, cells, rows)
    return difference(sides[0], high, low, other, near, image, near_valid, far_valid)[None]


def solution(mesh):
    placed = (
        P(("patch", "epoch"), None, None),
        P(("patch", "epoch"), None, None),
        P("patch", None, None),
        P("patch"),
    )
    return jax.shard_map(
        shards,
        mesh=mesh,
        in_specs=placed,
        out_specs=P(("patch", "epoch"), None, None),
        check_vma=False,
    )
```

time: 58.9 us -> 47.2 us (0.80)
  Pallas kernels: 18.9 us -> 8.64 us
  starting transfers between devices: 15 us -> 10.7 us
  waiting for transfers between devices: 20.1 us -> 22.1 us
  other arithmetic: 1.33 us -> 2.3 us
    pallas_call x3 -> x5, Pallas kernels: 18.9 us -> 8.64 us  [the longest x1 3.57 us: difference(): pl.pallas_call(far_kernel, in_specs=[pl.BlockSpec(memory_space=pltpu.SMEM...]
    ppermute x8 -> x7, starting transfers between devices: 15 us -> 10.7 us  [exchange(): lax.ppermute(cells, 'epoch', [(i, i ^ 1 << bit) for i in range(count)])]
    add x0 -> x3, other arithmetic: none -> 2.19 us  [the longest x2 2.17 us: shards(): cells = keep + other]
    ppermute x8 -> x7, waiting for transfers between devices: 20.1 us -> 22.1 us  [exchange(): lax.ppermute(cells, 'epoch', [(i, i ^ 1 << bit) for i in range(count)])]
    unnamed x7 -> x18, local copies, waits for them, and re-layouts: 1.04 us -> 2.98 us
    dynamic_slice x4 -> x2, local copies, waits for them, and re-layouts: 1.22 us -> 0.04 us  [halves(): send = lax.dynamic_slice_in_dim(cells, (1 - side) * width, width, 1)]
    select_n x4 -> x2, other arithmetic: 1.2 us -> 0.07 us  [shards(): jnp.where(sides[bit] == 0, jnp.concatenate([cells, other], axis=1), jnp.c...]
    slice x1 -> x0, local copies, waits for them, and re-layouts: 0.85 us -> none  [shards(): centre = image[MARGIN:MARGIN + rows]]
  transfers between devices with their start and end apart: 8 -> 7, of which waited for: 7 -> 6; matrix products, arithmetic and copies ran while one was open for 3% -> 0% of each run, Pallas kernels for 8% -> 10%
where the time goes in v2:
time: 47.2 us; the launch traced here: 46.9 us
  waiting for transfers between devices  22.1 us (47%)
  starting transfers between devices  10.7 us (23%)
  Pallas kernels  8.64 us (18%)
  local copies, waits for them, and re-layouts  3.03 us (6%)
  other arithmetic  2.3 us (5%)
    ppermute x7, waiting for transfers between devices, exchange(): lax.ppermute(cells, 'epoch', [(i, i ^ 1 << bit) for i in range(count)])  22.1 us
    ppermute x7, starting transfers between devices, exchange(): lax.ppermute(cells, 'epoch', [(i, i ^ 1 << bit) for i in range(count)])  10.7 us
    pallas_call x1, Pallas kernels, difference(): pl.pallas_call(far_kernel, in_specs=[pl.BlockSpec(memory_space=pltpu.SMEM...  3.57 us
    unnamed x18, local copies, waits for them, and re-layouts  2.98 us
    pallas_call x1, Pallas kernels, near_model(): pl.pallas_call(near_kernel, in_specs=[pl.BlockSpec(memory_space=pltpu.SME...  2.7 us
    add x2, other arithmetic, shards(): cells = keep + other  2.17 us
    pallas_call x1, Pallas kernels, weights(): pl.pallas_call(weight_kernel, in_specs=[smem, smem] + [vmem] * len(arrays...  1.94 us
  transfers between devices with their start and end apart: 7, of which 6 were waited for; matrix products, arithmetic and copies ran while one was open for 0% of the time, Pallas kernels for 10%

profile of v2, /device:TPU:0, one launch (start us, length us, event | category | flops | bytes accessed | tf_op | source)
XLA Modules:
  0.0 46.9 jit_solution(2165122595419248498)
XLA Ops:
  0.0 0.7 %copy-done.7 = s32[1,1,128]{2,1,0:T(1,128)S(1)} copy-done((s32[1,1,128]{2,1,0:T(1,128)S(1)}, s32[1,1,128]{2,1,0:T(1,128)}, u32[]{:S(2)}) %copy-start.7) | copy-done | bytes 536
  0.7 1.2 %copy-done = f32[1,64,4096]{2,1,0:T(8,128)S(1)} copy-done((f32[1,64,4096]{2,1,0:T(8,128)S(1)}, f32[1,64,4096]{2,1,0:T(8,128)}, u32[]{:S(2)}) %copy-start) | copy-done | bytes 1048600
  1.9 0.2 mask_half.3
  2.1 0.6 %collective-permute-start = (f32[64,2048]{1,0:T(8,128)S(1)}, f32[64,2048]{1,0:T(8,128)}, u32[]{:S(2)}, u32[]{:S(2)}) collective-permute-start(f32[64,2048]{1,0:T(8,128)S(1)} %get-tuple-element.15), channel_id=1, source_target_pairs={{0,1},{1,0},{2,3},{3,2},{4,5},{5,4},{6,7},{7,6},{8,9},{9,8},{10,11... | collective-permute-start | bytes 1572872 | tf_op jit(solution)/shard_map/ppermute | solution.py:266
  2.7 0.4 copy-done.1
  3.1 0.2 mask_half.2
  3.3 1.0 %collective-permute-done = f32[64,2048]{1,0:T(8,128)} collective-permute-done((f32[64,2048]{1,0:T(8,128)S(1)}, f32[64,2048]{1,0:T(8,128)}, u32[]{:S(2)}, u32[]{:S(2)}) %collective-permute-start) | collective-permute-done | bytes 524320 | tf_op jit(solution)/shard_map/ppermute | solution.py:266
  4.3 1.2 %add.24 = f32[64,2048]{1,0:T(8,128)S(1)} add(f32[64,2048]{1,0:T(8,128)S(1)} %get-tuple-element.14, f32[64,2048]{1,0:T(8,128)} %collective-permute-done) | non-fusion elementwise | flops 131072 | bytes 1572864 | tf_op jit(solution)/shard_map/add | solution.py:287
  5.6 2.9 %collective-permute-start.1 = (f32[64,1024]{1,0:T(8,128)S(1)}, f32[64,1024]{1,0:T(8,128)}, u32[]{:S(2)}, u32[]{:S(2)}) collective-permute-start(f32[64,1024]{1,0:T(8,128)S(1)} %constant_dynamic-slice_fusion.1), channel_id=1, source_target_pairs={{0,2},{1,3},{2,0},{3,1},{4,6},{5,7},{6,4},{7,5},{8,10},{9,11},{10,... | collective-permute-start | bytes 786440 | tf_op jit(solution)/shard_map/ppermute | solution.py:266
  8.6 0.6 %copy-done.8 = s32[16]{0:T(128)S(1)} copy-done((s32[16]{0:T(128)S(1)}, s32[16]{0:T(128)}, u32[]{:S(2)}) %copy-start.8) | copy-done | bytes 88
  9.2 1.9 %kernel_weights.1 = (bf16[256,512]{1,0:T(8,128)(2,1)S(1)}, bf16[256,512]{1,0:T(8,128)(2,1)S(1)}) custom-call(s32[1]{0:T(128)} %bitcast.4.place_ref, s32[16]{0:T(128)S(1)} %copy-done.8, f32[3,16,49]{2,1,0:T(8,128)S(1)} %bitcast.11, f32[16,49]{1,0:T(8,128)S(1)} %copy-done.6, f32[49,16]{1,0:T(8,128)S(1)} %copy-done.4, f32[16,2048]{1,0:T(8,128)S(1)} %copy-done.3, ...), custom_call_target="tpu_custom_call" | custom-call | flops 100000000 | bytes 2000000 | tf_op jit(solution)/shard_map/kernel_weights/pallas_call | solution.py:147
  11.1 4.1 %collective-permute-done.1 = f32[64,1024]{1,0:T(8,128)} collective-permute-done((f32[64,1024]{1,0:T(8,128)S(1)}, f32[64,1024]{1,0:T(8,128)}, u32[]{:S(2)}, u32[]{:S(2)}) %collective-permute-start.1) | collective-permute-done | bytes 262176 | tf_op jit(solution)/shard_map/ppermute | solution.py:266
  15.3 1.0 %dynamic-slice_add_fusion = f32[64,1024]{1,0:T(8,128)S(1)} fusion(f32[64,1024]{1,0:T(8,128)} %collective-permute-done.1, f32[64,2048]{1,0:T(8,128)S(1)} %add.24, s32[]{:T(128)S(6)} %select_n.28), kind=kLoop, calls=%fused_computation.2 | loop fusion | flops 65536 | bytes 786436 | tf_op jit(solution)/shard_map/add | solution.py:291
  16.3 1.9 %collective-permute-start.2 = (f32[64,512]{1,0:T(8,128)S(1)}, f32[64,512]{1,0:T(8,128)S(1)}, u32[]{:S(2)}, u32[]{:S(2)}) collective-permute-start(f32[64,512]{1,0:T(8,128)S(1)} %constant_dynamic-slice_fusion), channel_id=1, source_target_pairs={{0,4},{1,5},{2,6},{3,7},{4,0},{5,1},{6,2},{7,3},{8,12},{9,13},{10,... | collective-permute-start | bytes 393224 | tf_op jit(solution)/shard_map/ppermute | solution.py:266
  18.1 3.2 %collective-permute-done.2 = f32[64,512]{1,0:T(8,128)S(1)} collective-permute-done((f32[64,512]{1,0:T(8,128)S(1)}, f32[64,512]{1,0:T(8,128)S(1)}, u32[]{:S(2)}, u32[]{:S(2)}) %collective-permute-start.2) | collective-permute-done | bytes 131104 | tf_op jit(solution)/shard_map/ppermute | solution.py:266
  21.3 2.9 %collective-permute-start.3 = (f32[64,512]{1,0:T(8,128)S(1)}, f32[64,512]{1,0:T(8,128)S(1)}, u32[]{:S(2)}, u32[]{:S(2)}) collective-permute-start(f32[64,512]{1,0:T(8,128)S(1)} %dynamic-slice_add_fusion.1), channel_id=1, source_target_pairs={{0,8},{1,9},{2,10},{3,11},{4,12},{5,13},{6,14},{7,15},{8,0},{9,1},... | collective-permute-start | bytes 393224 | tf_op jit(solution)/shard_map/ppermute | solution.py:266
  24.2 4.7 %collective-permute-done.3 = f32[64,512]{1,0:T(8,128)S(1)} collective-permute-done((f32[64,512]{1,0:T(8,128)S(1)}, f32[64,512]{1,0:T(8,128)S(1)}, u32[]{:S(2)}, u32[]{:S(2)}) %collective-permute-start.3) | collective-permute-done | bytes 131104 | tf_op jit(solution)/shard_map/ppermute | solution.py:266
  29.0 0.7 %collective-permute-start.4 = (f32[64,512]{1,0:T(8,128)S(1)}, f32[64,512]{1,0:T(8,128)S(1)}, u32[]{:S(2)}, u32[]{:S(2)}) collective-permute-start(f32[64,512]{1,0:T(8,128)S(1)} %broadcast_divide_fusion), channel_id=1, source_target_pairs={{0,4},{1,5},{2,6},{3,7},{4,0},{5,1},{6,2},{7,3},{8,12},{9,13},{10,... | collective-permute-start | bytes 393224 | tf_op jit(solution)/shard_map/ppermute | solution.py:266
  29.7 4.3 %collective-permute-done.4 = f32[64,512]{1,0:T(8,128)S(1)} collective-permute-done((f32[64,512]{1,0:T(8,128)S(1)}, f32[64,512]{1,0:T(8,128)S(1)}, u32[]{:S(2)}, u32[]{:S(2)}) %collective-permute-start.4) | collective-permute-done | bytes 131104 | tf_op jit(solution)/shard_map/ppermute | solution.py:266
  34.0 1.7 %collective-permute-start.5 = (f32[64,1024]{1,0:T(8,128)S(1)}, f32[64,1024]{1,0:T(8,128)S(1)}, u32[]{:S(2)}, u32[]{:S(2)}) collective-permute-start(f32[64,1024]{1,0:T(8,128)S(1)} %maximum_select_fusion.1), channel_id=1, source_target_pairs={{0,2},{1,3},{2,0},{3,1},{4,6},{5,7},{6,4},{7,5},{8,10},{9,11},{10,... | collective-permute-start | bytes 786440 | tf_op jit(solution)/shard_map/ppermute | solution.py:266
  35.7 4.8 %collective-permute-done.5 = f32[64,1024]{1,0:T(8,128)S(1)} collective-permute-done((f32[64,1024]{1,0:T(8,128)S(1)}, f32[64,1024]{1,0:T(8,128)S(1)}, u32[]{:S(2)}, u32[]{:S(2)}) %collective-permute-start.5) | collective-permute-done | bytes 262176 | tf_op jit(solution)/shard_map/ppermute | solution.py:266
  40.5 0.1 collective-permute-start.6
  40.6 2.7 %near_model.1.near_ref = f32[32,2176]{1,0:T(8,128)S(1)} custom-call(s32[1]{0:T(128)} %bitcast.side_ref, bf16[256,512]{1,0:T(8,128)(2,1)S(1)} %get-tuple-element.18.high_ref, bf16[256,512]{1,0:T(8,128)(2,1)S(1)} %get-tuple-element.19.low_ref, f32[64,2048]{1,0:T(8,128)S(1)} %maximum_select_fusion.template_ref), custom_call_target="tpu_custom_call" | custom-call | flops 1711276032 | bytes 1310720 | tf_op jit(solution)/shard_map/near_model/pallas_call | solution.py:236
  43.3 3.6 %difference.1 = f32[32,4096]{1,0:T(8,128)} custom-call(s32[1]{0:T(128)} %bitcast.side_ref, bf16[256,512]{1,0:T(8,128)(2,1)S(1)} %get-tuple-element.18.high_ref, bf16[256,512]{1,0:T(8,128)(2,1)S(1)} %get-tuple-element.19.low_ref, f32[64,2048]{1,0:T(8,128)S(1)} %collective-permute-done.6.template_ref, f32[32,2176]{1,0:T(8,128)S(1)} %near_model.1.near_ref, ...), custom_call_target="tpu_custom_call" | custom-call | flops 1711276032 | bytes 1310720 | tf_op jit(solution)/shard_map/difference/pallas_call | solution.py:252
  (23 shorter events, 0.2 us)
Async XLA Ops:
  0.0 0.7 %copy-start.7 = (s32[1,1,128]{2,1,0:T(1,128)S(1)}, s32[1,1,128]{2,1,0:T(1,128)}, u32[]{:S(2)}) copy-start(s32[1,1,128]{2,1,0:T(1,128)} %param.9) | copy-start | bytes 1540
  0.7 1.2 %copy-start = (f32[1,64,4096]{2,1,0:T(8,128)S(1)}, f32[1,64,4096]{2,1,0:T(8,128)}, u32[]{:S(2)}) copy-start(f32[1,64,4096]{2,1,0:T(8,128)} %param.8) | copy-start | bytes 3145732
  1.9 1.2 %copy-start.1 = (f32[1,64,4096]{2,1,0:T(8,128)S(1)}, f32[1,64,4096]{2,1,0:T(8,128)}, u32[]{:S(2)}) copy-start(f32[1,64,4096]{2,1,0:T(8,128)} %param.8) | copy-start | bytes 3145732
  2.1 2.2 %collective-permute-start = (f32[64,2048]{1,0:T(8,128)S(1)}, f32[64,2048]{1,0:T(8,128)}, u32[]{:S(2)}, u32[]{:S(2)}) collective-permute-start(f32[64,2048]{1,0:T(8,128)S(1)} %get-tuple-element.15), channel_id=1, source_target_pairs={{0,1},{1,0},{2,3},{3,2},{4,5},{5,4},{6,7},{7,6},{8,9},{9,8},{10,11... | collective-permute-start | bytes 1572872 | tf_op jit(solution)/shard_map/ppermute | solution.py:266
  4.3 4.2 %copy-start.2 = (f32[15,32,512]{2,1,0:T(8,128)S(1)}, f32[15,32,512]{2,1,0:T(8,128)}, u32[]{:S(2)}) copy-start(f32[15,32,512]{2,1,0:T(8,128)} %constant.29.clone.vert_ref) | copy-start | bytes 2949124
  5.5 3.0 %copy-start.3 = (f32[16,2048]{1,0:T(8,128)S(1)}, f32[16,2048]{1,0:T(8,128)}, u32[]{:S(2)}) copy-start(f32[16,2048]{1,0:T(8,128)} %constant.28.clone.horiz_ref) | copy-start | bytes 393220
  5.5 3.0 %copy-start.4 = (f32[49,16]{1,0:T(8,128)S(1)}, f32[49,16]{1,0:T(8,128)}, u32[]{:S(2)}) copy-start(f32[49,16]{1,0:T(8,128)} %constant.27.clone.horiz_pick_ref) | copy-start | bytes 9412
  5.5 3.0 %copy-start.6 = (f32[16,49]{1,0:T(8,128)S(1)}, f32[16,49]{1,0:T(8,128)}, u32[]{:S(2)}) copy-start(f32[16,49]{1,0:T(8,128)} %constant.26.clone.vert_pick_ref) | copy-start | bytes 9412
  5.6 3.0 %copy-start.5 = (f32[16,49,3]{1,0,2:T(8,128)S(1)}, f32[16,49,3]{1,0,2:T(8,128)}, u32[]{:S(2)}) copy-start(f32[16,49,3]{1,0,2:T(8,128)} %param.10) | copy-start | bytes 28228
  5.6 9.7 %collective-permute-start.1 = (f32[64,1024]{1,0:T(8,128)S(1)}, f32[64,1024]{1,0:T(8,128)}, u32[]{:S(2)}, u32[]{:S(2)}) collective-permute-start(f32[64,1024]{1,0:T(8,128)S(1)} %constant_dynamic-slice_fusion.1), channel_id=1, source_target_pairs={{0,2},{1,3},{2,0},{3,1},{4,6},{5,7},{6,4},{7,5},{8,10},{9,11},{10,... | collective-permute-start | bytes 786440 | tf_op jit(solution)/shard_map/ppermute | solution.py:266
  8.5 0.7 %copy-start.8 = (s32[16]{0:T(128)S(1)}, s32[16]{0:T(128)}, u32[]{:S(2)}) copy-start(s32[16]{0:T(128)} %order_ref.1) | copy-start | bytes 196
  16.3 5.0 %collective-permute-start.2 = (f32[64,512]{1,0:T(8,128)S(1)}, f32[64,512]{1,0:T(8,128)S(1)}, u32[]{:S(2)}, u32[]{:S(2)}) collective-permute-start(f32[64,512]{1,0:T(8,128)S(1)} %constant_dynamic-slice_fusion), channel_id=1, source_target_pairs={{0,4},{1,5},{2,6},{3,7},{4,0},{5,1},{6,2},{7,3},{8,12},{9,13},{10,... | collective-permute-start | bytes 393224 | tf_op jit(solution)/shard_map/ppermute | solution.py:266
  21.3 7.6 %collective-permute-start.3 = (f32[64,512]{1,0:T(8,128)S(1)}, f32[64,512]{1,0:T(8,128)S(1)}, u32[]{:S(2)}, u32[]{:S(2)}) collective-permute-start(f32[64,512]{1,0:T(8,128)S(1)} %dynamic-slice_add_fusion.1), channel_id=1, source_target_pairs={{0,8},{1,9},{2,10},{3,11},{4,12},{5,13},{6,14},{7,15},{8,0},{9,1},... | collective-permute-start | bytes 393224 | tf_op jit(solution)/shard_map/ppermute | solution.py:266
  29.0 5.0 %collective-permute-start.4 = (f32[64,512]{1,0:T(8,128)S(1)}, f32[64,512]{1,0:T(8,128)S(1)}, u32[]{:S(2)}, u32[]{:S(2)}) collective-permute-start(f32[64,512]{1,0:T(8,128)S(1)} %broadcast_divide_fusion), channel_id=1, source_target_pairs={{0,4},{1,5},{2,6},{3,7},{4,0},{5,1},{6,2},{7,3},{8,12},{9,13},{10,... | collective-permute-start | bytes 393224 | tf_op jit(solution)/shard_map/ppermute | solution.py:266
  34.0 6.4 %collective-permute-start.5 = (f32[64,1024]{1,0:T(8,128)S(1)}, f32[64,1024]{1,0:T(8,128)S(1)}, u32[]{:S(2)}, u32[]{:S(2)}) collective-permute-start(f32[64,1024]{1,0:T(8,128)S(1)} %maximum_select_fusion.1), channel_id=1, source_target_pairs={{0,2},{1,3},{2,0},{3,1},{4,6},{5,7},{6,4},{7,5},{8,10},{9,11},{10,... | collective-permute-start | bytes 786440 | tf_op jit(solution)/shard_map/ppermute | solution.py:266
  40.5 2.8 %collective-permute-start.6 = (f32[64,2048]{1,0:T(8,128)S(1)}, f32[64,2048]{1,0:T(8,128)S(1)}, u32[]{:S(2)}, u32[]{:S(2)}) collective-permute-start(f32[64,2048]{1,0:T(8,128)S(1)} %maximum_select_fusion.template_ref), channel_id=1, source_target_pairs={{0,1},{1,0},{2,3},{3,2},{4,5},{5,4},{6,7},{7,6},{8,9},{9,8},{10,11... | collective-permute-start | bytes 1572872 | tf_op jit(solution)/shard_map/ppermute | solution.py:266

commit v3 on v2

v3 whole, which is shorter than its diff:
```python
import functools
import math

import jax
import jax.numpy as jnp
import numpy as np
from jax import lax
from jax.experimental import pallas as pl
from jax.experimental.pallas import tpu as pltpu
from jax.sharding import PartitionSpec as P

HALF = 15
MARGIN = 16
LANES = 128
SHIFTS = 8
GROUPS = 4
GRANT = 12 << 20
STREAMS = 2

gauss_widths = (1.5, 3.0, 6.0)
gauss_degrees = (6, 4, 2)


def basis_filters():
    offsets = np.arange(-HALF, HALF + 1).astype(np.float64)
    result = []
    for width, degree in zip(gauss_widths, gauss_degrees):
        envelope = np.exp(-offsets * offsets / (2.0 * width * width)) / (math.sqrt(2.0 * math.pi) * width)
        for power in range(degree + 1):
            result.append(envelope * (offsets / width) ** power)
    return np.stack(result)


def kernel_pairs():
    result = []
    first_index = 0
    for degree in gauss_degrees:
        for vert_power in range(degree + 1):
            for horiz_power in range(degree + 1 - vert_power):
                result.append((first_index + vert_power, first_index + horiz_power))
        first_index = first_index + degree + 1
    return result


def tables(rows, padded_rows):
    filters = basis_filters()
    count, taps = filters.shape
    pairs = kernel_pairs()
    vert_pick = np.zeros((count + 1, len(pairs)), np.float32)
    horiz_pick = np.zeros((len(pairs), count + 1), np.float32)
    for index, (vert, horiz) in enumerate(pairs):
        vert_pick[vert, index] = 1.0
        horiz_pick[index, horiz] = 1.0
    span = SHIFTS * GROUPS
    horiz = np.zeros((count + 1, span), np.float64)
    horiz[:count, :taps] = filters
    horiz_lanes = np.repeat(horiz, padded_rows, axis=1).astype(np.float32)
    vert = np.zeros((count, rows, padded_rows), np.float64)
    for row in range(rows):
        start = row + MARGIN - HALF
        vert[:, row, start : start + taps] = filters
    vert_lanes = np.tile(vert, (1, 1, LANES // padded_rows)).astype(np.float32)
    return vert_pick, horiz_pick, horiz_lanes, vert_lanes


def mask_kernel(twin, stream, place_ref, octets_ref, image_ref, masked_ref, valid_ref):
    width = masked_ref.shape[1]
    word_count, piece_words = octets_ref.shape[1], width // 32
    piece = ((place_ref[0] & 1) ^ twin) * STREAMS + stream
    word_row = lax.broadcasted_iota(jnp.int32, (piece_words, width), 0)
    lane = lax.broadcasted_iota(jnp.int32, (piece_words, width), 1)
    spread = jnp.where(word_row == jnp.right_shift(lane, 5), 1.0, 0.0).astype(jnp.bfloat16)
    octets = pltpu.roll(octets_ref[...], lax.rem(word_count - piece * piece_words, word_count), 1)
    octets = octets[:, :piece_words].astype(jnp.bfloat16)
    wide = jnp.dot(octets, spread, preferred_element_type=jnp.float32).astype(jnp.int32)
    lane = lax.broadcasted_iota(jnp.int32, wide.shape, 1)
    byte_row = lax.broadcasted_iota(jnp.int32, wide.shape, 0)
    bit = jnp.right_shift(wide, lane & 7) & 1
    bit = jnp.where(byte_row == (jnp.right_shift(lane, 3) & 3), bit, 0).astype(jnp.float32)
    valid = jnp.sum(bit, axis=0, keepdims=True)
    valid_ref[...] = valid
    row = lax.broadcasted_iota(jnp.int32, masked_ref.shape, 0)
    cells = image_ref[:, pl.ds(pl.multiple_of(piece * width, width), width)]
    masked_ref[...] = jnp.where(row == 0, valid, valid * cells)


def masked_piece(place, octets, image, twin, stream):
    rows, columns = image.shape
    width = columns // (2 * STREAMS)
    vmem = pl.BlockSpec(memory_space=pltpu.VMEM)
    return pl.pallas_call(
        functools.partial(mask_kernel, twin, stream),
        in_specs=[pl.BlockSpec(memory_space=pltpu.SMEM), vmem, vmem],
        out_specs=[vmem, vmem],
        out_shape=[
            jax.ShapeDtypeStruct((rows, width), jnp.float32),
            jax.ShapeDtypeStruct((1, width), jnp.float32),
        ],
        compiler_params=pltpu.CompilerParams(vmem_limit_bytes=GRANT),
        cost_estimate=pl.CostEstimate(flops=rows * width, bytes_accessed=8 * rows * width, transcendentals=0),
        name="mask_piece",
    )(place, octets, image)


def part_kernel(bit, place_ref, kept_ref, arrived_ref, keep_ref, send_ref):
    width = keep_ref.shape[1]
    side = jnp.right_shift(place_ref[0], bit) & 1
    for target_ref, part in ((keep_ref, side), (send_ref, 1 - side)):
        lanes = pl.ds(pl.multiple_of(part * width, width), width)
        target_ref[...] = kept_ref[:, lanes] + arrived_ref[:, lanes]


def add_and_part(place, bit, kept, arrived):
    rows, width = kept.shape
    if width % (2 * LANES):
        return halves(kept + arrived, jnp.right_shift(place[0], bit) & 1)
    vmem = pl.BlockSpec(memory_space=pltpu.VMEM)
    return pl.pallas_call(
        functools.partial(part_kernel, bit),
        in_specs=[pl.BlockSpec(memory_space=pltpu.SMEM), vmem, vmem],
        out_specs=[vmem, vmem],
        out_shape=[jax.ShapeDtypeStruct((rows, width // 2), jnp.float32)] * 2,
        compiler_params=pltpu.CompilerParams(vmem_limit_bytes=GRANT),
        cost_estimate=pl.CostEstimate(flops=rows * width, bytes_accessed=12 * rows * width, transcendentals=0),
        name="add_and_part",
    )(place, kept, arrived)


def weight_kernel(place_ref, order_ref, coef_ref, vert_pick_ref, horiz_pick_ref, horiz_ref, vert_ref, high_ref, low_ref):
    count, rows, lanes = vert_ref.shape
    exact = dict(precision=lax.Precision.HIGHEST, preferred_element_type=jnp.float32)
    order = order_ref[...]
    slot = lax.broadcasted_iota(jnp.int32, order.shape, 1)
    catalog = jnp.sum(jnp.where(slot == place_ref[0], order, 0), axis=1, keepdims=True)
    chosen = lax.broadcasted_iota(jnp.int32, coef_ref.shape[1:], 0) == catalog
    picked = [
        vert_pick_ref[...] * jnp.sum(jnp.where(chosen, coef_ref[term], 0.0), axis=0, keepdims=True)
        for term in range(3)
    ]
    table = jnp.dot(jnp.concatenate(picked, axis=0), horiz_pick_ref[...], **exact)
    taps = jnp.dot(table, horiz_ref[...], **exact)
    step = count + 1
    row = lax.broadcasted_iota(jnp.int32, (rows, lanes), 0).astype(jnp.float32)
    row_pos = (2.0 * row + 1.0) / rows - 1.0
    width = high_ref.shape[1]
    for group in range(GROUPS):
        for start in range(0, width, lanes):
            sums = []
            for term in range(3):
                total = jnp.zeros((rows, lanes), jnp.float32)
                for index in range(count):
                    line = term * step + index
                    first = group * width + start
                    total = total + taps[line : line + 1, first : first + lanes] * vert_ref[index]
                sums.append(total)
            for place, weight in enumerate((sums[0] + row_pos * sums[2], sums[1])):
                high = weight.astype(jnp.bfloat16)
                low = (weight - high.astype(jnp.float32)).astype(jnp.bfloat16)
                first = (2 * group + place) * rows
                high_ref[first : first + rows, start : start + lanes] = high
                low_ref[first : first + rows, start : start + lanes] = low


def weights(place, coefficients, epoch_order, rows, padded_rows):
    arrays = (epoch_order[None], jnp.transpose(coefficients, (2, 0, 1)),) + tables(rows, padded_rows)
    shape = (2 * GROUPS * rows, SHIFTS * padded_rows)
    smem = pl.BlockSpec(memory_space=pltpu.SMEM)
    vmem = pl.BlockSpec(memory_space=pltpu.VMEM)
    return pl.pallas_call(
        weight_kernel,
        in_specs=[smem] + [vmem] * len(arrays),
        out_specs=[vmem, vmem],
        out_shape=[jax.ShapeDtypeStruct(shape, jnp.bfloat16)] * 2,
        compiler_params=pltpu.CompilerParams(vmem_limit_bytes=GRANT),
        cost_estimate=pl.CostEstimate(flops=10**8, bytes_accessed=2 * 10**6, transcendentals=0),
        name="kernel_weights",
    )(place, *arrays)


def piece_model(high_ref, low_ref, template_ref, first_column, total_columns, wide_high, wide_low, partial):
    padded_rows, columns = template_ref.shape
    domain = wide_high.shape[1]
    size = partial.shape[0] // GROUPS
    rows = size // 2
    template = jnp.concatenate(
        [template_ref[...], jnp.zeros((padded_rows, domain - columns), jnp.float32)], axis=1
    )
    for shift in range(SHIFTS):
        moved = template if shift == 0 else pltpu.roll(template, domain - shift, 1)
        high = moved.astype(jnp.bfloat16)
        low = (moved - high.astype(jnp.float32)).astype(jnp.bfloat16)
        wide_high[shift * padded_rows : (shift + 1) * padded_rows] = high
        wide_low[shift * padded_rows : (shift + 1) * padded_rows] = low
    high = wide_high[...]
    total = jnp.dot(high_ref[...], high, preferred_element_type=jnp.float32)
    total += jnp.dot(low_ref[...], high, preferred_element_type=jnp.float32)
    total += jnp.dot(high_ref[...], wide_low[...], preferred_element_type=jnp.float32)
    partial[...] = total
    total = jnp.zeros((size, domain), jnp.float32)
    for group in range(GROUPS):
        amount = (HALF - SHIFTS * group) % domain
        total = total + pltpu.roll(partial[group * size : (group + 1) * size], amount, 1)
    lane = lax.broadcasted_iota(jnp.int32, (rows, domain), 1)
    column = first_column + jnp.where(lane < columns + LANES // 2, lane, lane - domain)
    position = (2.0 * column.astype(jnp.float32) + 1.0) / total_columns - 1.0
    return total[:rows] + position * total[rows:]


def piece_column(place, bit, stream, other, twin, width):
    side = (place & 1) ^ twin
    part = (jnp.right_shift(place, bit) & 1) ^ other
    return pl.multiple_of(side * (2 * STREAMS * width) + stream * (2 * width) + part * width, LANES)


def add_pieces(pieces, place, high_ref, low_ref, template_refs, total_columns, model_ref, scratch):
    lane = lax.broadcasted_iota(jnp.int32, (model_ref.shape[0], LANES), 1)
    for index, (piece, template_ref) in enumerate(zip(pieces, template_refs)):
        width = template_ref.shape[1]
        first = piece_column(place, *piece, width)
        model = piece_model(
            high_ref, low_ref, template_ref, first, total_columns, *scratch[3 * index : 3 * index + 3]
        )
        spill = model[:, width:]
        body = pl.ds(first + LANES, width)
        model_ref[:, body] = model_ref[:, body] + model[:, :width]
        before = pl.ds(first, LANES)
        model_ref[:, before] = model_ref[:, before] + jnp.where(lane < LANES // 2, 0.0, spill)
        after = pl.ds(pl.multiple_of(first + (LANES + width), LANES), LANES)
        model_ref[:, after] = model_ref[:, after] + jnp.where(lane < LANES // 2, spill, 0.0)


def model_kernel(pieces, total_columns, fresh, place_ref, high_ref, low_ref, *refs):
    count = len(pieces)
    templates, refs = refs[:count], refs[count:]
    if fresh:
        model_ref, scratch = refs[0], refs[1:]
        model_ref[...] = jnp.zeros_like(model_ref)
    else:
        model_ref, scratch = refs[1], refs[2:]
    add_pieces(pieces, place_ref[0], high_ref, low_ref, templates, total_columns, model_ref, scratch)


def difference_kernel(pieces, place_ref, high_ref, low_ref, *refs):
    count, parts = len(pieces), 2 * STREAMS
    templates, refs = refs[:count], refs[count:]
    model_ref, image_ref, valid_refs = refs[0], refs[1], refs[2 : 2 + parts]
    out_ref, total_ref = refs[2 + parts : 4 + parts]
    rows, columns = out_ref.shape
    width = columns // parts
    total_ref[...] = model_ref[...]
    add_pieces(pieces, place_ref[0], high_ref, low_ref, templates, columns, total_ref, refs[4 + parts :])
    for part, valid_ref in enumerate(valid_refs):
        side = (place_ref[0] & 1) ^ (part // STREAMS)
        first = pl.multiple_of((side * STREAMS + part % STREAMS) * width, width)
        lanes = pl.ds(first, width)
        model = total_ref[:, pl.ds(pl.multiple_of(first + LANES, LANES), width)]
        out_ref[:, lanes] = valid_ref[...] * (image_ref[MARGIN : MARGIN + rows, lanes] - model)


def model_scratch(rows, padded_rows, width):
    domain = width + LANES
    return [
        pltpu.VMEM((SHIFTS * padded_rows, domain), jnp.bfloat16),
        pltpu.VMEM((SHIFTS * padded_rows, domain), jnp.bfloat16),
        pltpu.VMEM((2 * GROUPS * rows, domain), jnp.float32),
    ]


def model_cost(rows, padded_rows, width, pieces=1):
    flops = 12 * GROUPS * rows * SHIFTS * padded_rows * (width + LANES) * pieces
    return pl.CostEstimate(flops=flops, bytes_accessed=10 * padded_rows * width * pieces, transcendentals=0)


def add_models(place, high, low, pieces, templates, model, rows, total_columns):
    padded_rows, width = templates[0].shape
    count = len(templates)
    fresh = model is None
    vmem = pl.BlockSpec(memory_space=pltpu.VMEM)
    return pl.pallas_call(
        functools.partial(model_kernel, pieces, total_columns, fresh),
        in_specs=[pl.BlockSpec(memory_space=pltpu.SMEM)] + [vmem] * (2 + count + (not fresh)),
        out_specs=vmem,
        out_shape=jax.ShapeDtypeStruct((rows, total_columns + 2 * LANES), jnp.float32),
        scratch_shapes=model_scratch(rows, padded_rows, width) * count,
        input_output_aliases={} if fresh else {3 + count: 0},
        compiler_params=pltpu.CompilerParams(vmem_limit_bytes=GRANT),
        cost_estimate=model_cost(rows, padded_rows, width, count),
        name="add_models",
    )(place, high, low, *templates, *(() if fresh else (model,)))


def difference(place, high, low, pieces, templates, model, image, valids):
    padded_rows, width = templates[0].shape
    count = len(templates)
    rows = model.shape[0]
    vmem = pl.BlockSpec(memory_space=pltpu.VMEM)
    return pl.pallas_call(
        functools.partial(difference_kernel, pieces),
        in_specs=[pl.BlockSpec(memory_space=pltpu.SMEM)] + [vmem] * (4 + count + len(valids)),
        out_specs=vmem,
        out_shape=jax.ShapeDtypeStruct((rows, image.shape[1]), jnp.float32),
        scratch_shapes=[pltpu.VMEM(model.shape, jnp.float32)] + model_scratch(rows, padded_rows, width) * count,
        compiler_params=pltpu.CompilerParams(vmem_limit_bytes=GRANT),
        cost_estimate=model_cost(rows, padded_rows, width, count),
        name="difference",
    )(place, high, low, *templates, model, image, *valids)


def exchange(cells, bit):
    count = lax.axis_size("epoch")
    return lax.ppermute(cells, "epoch", [(i, i ^ (1 << bit)) for i in range(count)])


def halves(cells, side):
    width = cells.shape[1] // 2
    keep = lax.dynamic_slice_in_dim(cells, side * width, width, 1)
    send = lax.dynamic_slice_in_dim(cells, (1 - side) * width, width, 1)
    return keep, send


def joined_columns(cells, other, side):
    return jnp.where(side == 0, jnp.concatenate([cells, other], axis=1), jnp.concatenate([other, cells], axis=1))


def part_of_epoch(epoch_images, mask_words, coefficients, epoch_order):
    padded_rows, columns = epoch_images.shape[1:]
    rows = padded_rows - 2 * MARGIN
    index = lax.axis_index("epoch").astype(jnp.int32)
    place = index[None]
    bits = lax.axis_size("epoch").bit_length() - 1
    image, words = epoch_images[0], mask_words[0]
    orders = list(range(1, bits - 1)), [2, 1] + list(range(3, bits - 1))
    streams = range(STREAMS)

    places = 8 * (lax.broadcasted_iota(jnp.int32, (8, words.shape[1]), 0) & 3)
    octets = (jnp.right_shift(jnp.broadcast_to(words, places.shape), places) & 255).astype(jnp.float32)
    far, near = [], []
    for stream in streams:
        far.append(masked_piece(place, octets, image, 1, stream))
    others = [exchange(far[stream][0], 0) for stream in streams]
    for stream in streams:
        near.append(masked_piece(place, octets, image, 0, stream))
    cells = [near[stream][0] for stream in streams]
    for step in range(bits - 2):
        pairs = [add_and_part(place, orders[stream][step], cells[stream], others[stream]) for stream in streams]
        cells = [pairs[stream][0] for stream in streams]
        others = [exchange(pairs[stream][1], orders[stream][step]) for stream in streams]
    cells = [cells[stream] + others[stream] for stream in streams]
    others = [exchange(cells[stream], bits - 1) for stream in streams]
    high, low = weights(place, coefficients, epoch_order, rows, padded_rows)
    cells = [cells[stream] + others[stream] for stream in streams]
    cells = [part / jnp.maximum(part[:1], 1.0) for part in cells]
    for step in reversed(range(1, bits - 2)):
        others = [exchange(cells[stream], orders[stream][step]) for stream in streams]
        cells = [
            joined_columns(
                cells[stream], others[stream], jnp.right_shift(index, orders[stream][step]) & 1
            )
            for stream in streams
        ]
    kinds = [
        [(orders[stream][0], stream, other, twin) for stream in streams] for other in range(2) for twin in range(2)
    ]
    others = [exchange(cells[stream], orders[stream][0]) for stream in streams]
    twins = [exchange(cells[stream], 0) for stream in streams]
    model = None
    for stream in reversed(streams):
        model = add_models(place, high, low, [kinds[0][stream]], [cells[stream]], model, rows, columns)
    model = add_models(place, high, low, kinds[1], twins, model, rows, columns)
    twins = [exchange(others[stream], 0) for stream in streams]
    model = add_models(place, high, low, kinds[2], others, model, rows, columns)
    valids = [piece[1] for piece in near + far]
    return difference(place, high, low, kinds[3], twins, model, image, valids)[None]


def solution(mesh):
    placed = (
        P(("patch", "epoch"), None, None),
        P(("patch", "epoch"), None, None),
        P("patch", None, None),
        P("patch"),
    )
    return jax.shard_map(
        part_of_epoch,
        mesh=mesh,
        in_specs=placed,
        out_specs=P(("patch", "epoch"), None, None),
        check_vma=False,
    )
```

time: 47.2 us -> 41.3 us (0.87)
  waiting for transfers between devices: 22.1 us -> 8.58 us
  starting transfers between devices: 10.7 us -> 18.5 us
  Pallas kernels: 8.64 us -> 11.1 us
  other arithmetic: 2.3 us -> 0.17 us
  local copies, waits for them, and re-layouts: 3.03 us -> 2.54 us
    ppermute x7 -> x16, waiting for transfers between devices: 22.1 us -> 8.58 us  [exchange(): lax.ppermute(cells, 'epoch', [(i, i ^ 1 << bit) for i in range(count)])]
    ppermute x7 -> x16, starting transfers between devices: 10.7 us -> 18.5 us  [exchange(): lax.ppermute(cells, 'epoch', [(i, i ^ 1 << bit) for i in range(count)])]
    pallas_call x5 -> x14, Pallas kernels: 8.64 us -> 11.1 us  [the longest x4 5.96 us: add_models(): pl.pallas_call(functools.partial(model_kernel, pieces, total_columns, fre...]
    add x4, other arithmetic: 2.21 us -> 0.04 us  [part_of_epoch(): cells = [cells[stream] + others[stream] for stream in streams]]
  transfers between devices with their start and end apart: 7 -> 16, of which waited for: 6 -> 6; matrix products, arithmetic and copies ran while one was open for 0% -> 0% of each run, Pallas kernels for 10% -> 20%
where the time goes in v3:
time: 41.3 us; the launch traced here: 41.1 us
  starting transfers between devices  18.5 us (45%)
  Pallas kernels  11.1 us (27%)
  waiting for transfers between devices  8.58 us (21%)
  local copies, waits for them, and re-layouts  2.54 us (6%)
    ppermute x16, starting transfers between devices, exchange(): lax.ppermute(cells, 'epoch', [(i, i ^ 1 << bit) for i in range(count)])  18.5 us
    ppermute x16, waiting for transfers between devices, exchange(): lax.ppermute(cells, 'epoch', [(i, i ^ 1 << bit) for i in range(count)])  8.58 us
    pallas_call x4, Pallas kernels, add_models(): pl.pallas_call(functools.partial(model_kernel, pieces, total_columns, fre...  5.96 us
    pallas_call x1, Pallas kernels, difference(): pl.pallas_call(functools.partial(difference_kernel, pieces), in_specs=[pl...  2.71 us
    unnamed x18, local copies, waits for them, and re-layouts  2.54 us
    pallas_call x1, Pallas kernels, weights(): pl.pallas_call(weight_kernel, in_specs=[smem] + [vmem] * len(arrays), out...  1.46 us
    pallas_call x4, Pallas kernels, masked_piece(): pl.pallas_call(functools.partial(mask_kernel, twin, stream), in_specs=[pl...  0.88 us
  transfers between devices with their start and end apart: 16, of which 6 were waited for; matrix products, arithmetic and copies ran while one was open for 0% of the time, Pallas kernels for 20%

profile of v3, /device:TPU:0, one launch (start us, length us, event | category | flops | bytes accessed | tf_op | source)
XLA Modules:
  0.0 41.1 jit_solution(6187005100279270707)
XLA Ops:
  0.0 0.7 %copy-done.8 = s32[1,1,128]{2,1,0:T(1,128)S(1)} copy-done((s32[1,1,128]{2,1,0:T(1,128)S(1)}, s32[1,1,128]{2,1,0:T(1,128)}, u32[]{:S(2)}) %copy-start.8) | copy-done | bytes 536
  0.7 1.2 %copy-done = f32[1,64,4096]{2,1,0:T(8,128)S(1)} copy-done((f32[1,64,4096]{2,1,0:T(8,128)S(1)}, f32[1,64,4096]{2,1,0:T(8,128)}, u32[]{:S(2)}) %copy-start) | copy-done | bytes 1048600
  3.3 0.6 %collective-permute-done.7.arrived_ref = f32[64,1024]{1,0:T(8,128)S(1)} collective-permute-done((f32[64,1024]{1,0:T(8,128)S(1)}, f32[64,1024]{1,0:T(8,128)S(1)}, u32[]{:S(2)}, u32[]{:S(2)}) %collective-permute-start.7) | collective-permute-done | bytes 262176 | tf_op jit(solution)/shard_map/ppermute | solution.py:311
  3.9 3.0 %collective-permute-start.8 = (f32[64,512]{1,0:T(8,128)S(1)}, f32[64,512]{1,0:T(8,128)S(1)}, u32[]{:S(2)}, u32[]{:S(2)}) collective-permute-start(f32[64,512]{1,0:T(8,128)S(1)} %get-tuple-element.34), channel_id=1, source_target_pairs={{0,4},{1,5},{2,6},{3,7},{4,0},{5,1},{6,2},{7,3},{8,12},{9,13},{10,... | collective-permute-start | bytes 393224 | tf_op jit(solution)/shard_map/ppermute | solution.py:311
  7.2 1.6 %collective-permute-start.1 = (f32[64,512]{1,0:T(8,128)S(1)}, f32[64,512]{1,0:T(8,128)S(1)}, u32[]{:S(2)}, u32[]{:S(2)}) collective-permute-start(f32[64,512]{1,0:T(8,128)S(1)} %get-tuple-element.28), channel_id=1, source_target_pairs={{0,2},{1,3},{2,0},{3,1},{4,6},{5,7},{6,4},{7,5},{8,10},{9,11},{10,... | collective-permute-start | bytes 393224 | tf_op jit(solution)/shard_map/ppermute | solution.py:311
  8.8 1.9 %collective-permute-done.8.arrived_ref = f32[64,512]{1,0:T(8,128)S(1)} collective-permute-done((f32[64,512]{1,0:T(8,128)S(1)}, f32[64,512]{1,0:T(8,128)S(1)}, u32[]{:S(2)}, u32[]{:S(2)}) %collective-permute-start.8) | collective-permute-done | bytes 131104 | tf_op jit(solution)/shard_map/ppermute | solution.py:311
  10.8 1.7 %collective-permute-start.9 = (f32[64,256]{1,0:T(8,128)S(1)}, f32[64,256]{1,0:T(8,128)S(1)}, u32[]{:S(2)}, u32[]{:S(2)}) collective-permute-start(f32[64,256]{1,0:T(8,128)S(1)} %get-tuple-element.36), channel_id=1, source_target_pairs={{0,2},{1,3},{2,0},{3,1},{4,6},{5,7},{6,4},{7,5},{8,10},{9,11},{10,... | collective-permute-start | bytes 196616 | tf_op jit(solution)/shard_map/ppermute | solution.py:311
  12.6 1.6 %collective-permute-start.2 = (f32[64,256]{1,0:T(8,128)S(1)}, f32[64,256]{1,0:T(8,128)S(1)}, u32[]{:S(2)}, u32[]{:S(2)}) collective-permute-start(f32[64,256]{1,0:T(8,128)S(1)} %get-tuple-element.30), channel_id=1, source_target_pairs={{0,4},{1,5},{2,6},{3,7},{4,0},{5,1},{6,2},{7,3},{8,12},{9,13},{10,... | collective-permute-start | bytes 196616 | tf_op jit(solution)/shard_map/ppermute | solution.py:311
  14.2 0.9 %collective-permute-done.9 = f32[64,256]{1,0:T(8,128)S(1)} collective-permute-done((f32[64,256]{1,0:T(8,128)S(1)}, f32[64,256]{1,0:T(8,128)S(1)}, u32[]{:S(2)}, u32[]{:S(2)}) %collective-permute-start.9) | collective-permute-done | bytes 65568 | tf_op jit(solution)/shard_map/ppermute | solution.py:311
  15.1 2.8 %collective-permute-start.10 = (f32[64,256]{1,0:T(8,128)S(1)}, f32[64,256]{1,0:T(8,128)S(1)}, u32[]{:S(2)}, u32[]{:S(2)}) collective-permute-start(f32[64,256]{1,0:T(8,128)S(1)} %add.14), channel_id=1, source_target_pairs={{0,8},{1,9},{2,10},{3,11},{4,12},{5,13},{6,14},{7,15},{8,0},{9,1},... | collective-permute-start | bytes 196616 | tf_op jit(solution)/shard_map/ppermute | solution.py:311
  17.9 2.1 %collective-permute-start.3 = (f32[64,256]{1,0:T(8,128)S(1)}, f32[64,256]{1,0:T(8,128)S(1)}, u32[]{:S(2)}, u32[]{:S(2)}) collective-permute-start(f32[64,256]{1,0:T(8,128)S(1)} %add.12), channel_id=1, source_target_pairs={{0,8},{1,9},{2,10},{3,11},{4,12},{5,13},{6,14},{7,15},{8,0},{9,1},... | collective-permute-start | bytes 196616 | tf_op jit(solution)/shard_map/ppermute | solution.py:311
  20.0 2.1 %collective-permute-done.10 = f32[64,256]{1,0:T(8,128)S(1)} collective-permute-done((f32[64,256]{1,0:T(8,128)S(1)}, f32[64,256]{1,0:T(8,128)S(1)}, u32[]{:S(2)}, u32[]{:S(2)}) %collective-permute-start.10) | collective-permute-done | bytes 65568 | tf_op jit(solution)/shard_map/ppermute | solution.py:311
  22.2 1.6 %collective-permute-start.11 = (f32[64,256]{1,0:T(8,128)S(1)}, f32[64,256]{1,0:T(8,128)S(1)}, u32[]{:S(2)}, u32[]{:S(2)}) collective-permute-start(f32[64,256]{1,0:T(8,128)S(1)} %broadcast_divide_fusion), channel_id=1, source_target_pairs={{0,2},{1,3},{2,0},{3,1},{4,6},{5,7},{6,4},{7,5},{8,10},{9,11},{10,... | collective-permute-start | bytes 196616 | tf_op jit(solution)/shard_map/ppermute | solution.py:311
  23.8 1.0 %collective-permute-start.4 = (f32[64,256]{1,0:T(8,128)S(1)}, f32[64,256]{1,0:T(8,128)S(1)}, u32[]{:S(2)}, u32[]{:S(2)}) collective-permute-start(f32[64,256]{1,0:T(8,128)S(1)} %broadcast_divide_fusion.1), channel_id=1, source_target_pairs={{0,4},{1,5},{2,6},{3,7},{4,0},{5,1},{6,2},{7,3},{8,12},{9,13},{10,... | collective-permute-start | bytes 196616 | tf_op jit(solution)/shard_map/ppermute | solution.py:311
  24.9 1.7 %collective-permute-done.11 = f32[64,256]{1,0:T(8,128)S(1)} collective-permute-done((f32[64,256]{1,0:T(8,128)S(1)}, f32[64,256]{1,0:T(8,128)S(1)}, u32[]{:S(2)}, u32[]{:S(2)}) %collective-permute-start.11) | collective-permute-done | bytes 65568 | tf_op jit(solution)/shard_map/ppermute | solution.py:311
  26.9 1.3 %collective-permute-done.4 = f32[64,256]{1,0:T(8,128)S(1)} collective-permute-done((f32[64,256]{1,0:T(8,128)S(1)}, f32[64,256]{1,0:T(8,128)S(1)}, u32[]{:S(2)}, u32[]{:S(2)}) %collective-permute-start.4) | collective-permute-done | bytes 65568 | tf_op jit(solution)/shard_map/ppermute | solution.py:311
  28.2 1.0 %collective-permute-start.5 = (f32[64,512]{1,0:T(8,128)S(1)}, f32[64,512]{1,0:T(8,128)S(1)}, u32[]{:S(2)}, u32[]{:S(2)}) collective-permute-start(f32[64,512]{1,0:T(8,128)S(1)} %maximum_select_fusion.refs_0_), channel_id=1, source_target_pairs={{0,2},{1,3},{2,0},{3,1},{4,6},{5,7},{6,4},{7,5},{8,10},{9,11},{10,... | collective-permute-start | bytes 393224 | tf_op jit(solution)/shard_map/ppermute | solution.py:311
  29.7 0.6 %copy-done.7 = s32[16]{0:T(128)S(1)} copy-done((s32[16]{0:T(128)S(1)}, s32[16]{0:T(128)}, u32[]{:S(2)}) %copy-start.7) | copy-done | bytes 88
  30.3 1.5 %kernel_weights.1 = (bf16[256,512]{1,0:T(8,128)(2,1)S(1)}, bf16[256,512]{1,0:T(8,128)(2,1)S(1)}) custom-call(s32[1]{0:T(128)} %bitcast.place_ref, s32[1,16]{1,0:T(1,128)S(1)} %bitcast.14, f32[3,16,49]{2,1,0:T(8,128)S(1)} %bitcast.13, f32[16,49]{1,0:T(8,128)S(1)} %copy-done.6, f32[49,16]{1,0:T(8,128)S(1)} %copy-done.4, f32[16,2048]{1,0:T(8,128)S(1)} %copy-done.3, ...), custom_call_target="tpu_custom_call" | custom-call | flops 100000000 | bytes 2000000 | tf_op jit(solution)/shard_map/kernel_weights/pallas_call | solution.py:169
  31.8 1.2 %add_models.4.refs_1_ = f32[32,4352]{1,0:T(8,128)S(1)} custom-call(s32[1]{0:T(128)} %bitcast.place_ref, bf16[256,512]{1,0:T(8,128)(2,1)S(1)} %get-tuple-element.23.high_ref, bf16[256,512]{1,0:T(8,128)(2,1)S(1)} %get-tuple-element.24.low_ref, f32[64,512]{1,0:T(8,128)S(1)} %maximum_select_fusion.1.refs_0_), custom_call_target="tpu_custom_call" | custom-call | flops 503316480 | bytes 327680 | tf_op jit(solution)/shard_map/add_models/pallas_call | solution.py:279
  33.0 1.1 %add_models.5.refs_2_ = f32[32,4352]{1,0:T(8,128)S(1)} custom-call(s32[1]{0:T(128)} %bitcast.place_ref, bf16[256,512]{1,0:T(8,128)(2,1)S(1)} %get-tuple-element.23.high_ref, bf16[256,512]{1,0:T(8,128)(2,1)S(1)} %get-tuple-element.24.low_ref, f32[64,512]{1,0:T(8,128)S(1)} %maximum_select_fusion.refs_0_, ...), custom_call_target="tpu_custom_call", output_to_operand_aliasing={{}: (4, {})} | custom-call | flops 503316480 | bytes 327680 | tf_op jit(solution)/shard_map/add_models/pallas_call | solution.py:279
  34.7 1.8 %add_models.6.refs_2_ = f32[32,4352]{1,0:T(8,128)S(1)} custom-call(s32[1]{0:T(128)} %bitcast.place_ref, bf16[256,512]{1,0:T(8,128)(2,1)S(1)} %get-tuple-element.23.high_ref, bf16[256,512]{1,0:T(8,128)(2,1)S(1)} %get-tuple-element.24.low_ref, f32[64,512]{1,0:T(8,128)S(1)} %collective-permute-done.14.refs_0_, ...), custom_call_target="tpu_custom_call", output_to_operand_aliasing={{}: (5, {})} | custom-call | flops 1006632960 | bytes 655360 | tf_op jit(solution)/shard_map/add_models/pallas_call | solution.py:279
  36.5 1.8 %add_models.7.refs_2_ = f32[32,4352]{1,0:T(8,128)S(1)} custom-call(s32[1]{0:T(128)} %bitcast.place_ref, bf16[256,512]{1,0:T(8,128)(2,1)S(1)} %get-tuple-element.23.high_ref, bf16[256,512]{1,0:T(8,128)(2,1)S(1)} %get-tuple-element.24.low_ref, f32[64,512]{1,0:T(8,128)S(1)} %collective-permute-done.5.refs_0_, ...), custom_call_target="tpu_custom_call", output_to_operand_aliasing={{}: (5, {})} | custom-call | flops 1006632960 | bytes 655360 | tf_op jit(solution)/shard_map/add_models/pallas_call | solution.py:279
  38.4 2.7 %difference.1 = f32[32,4096]{1,0:T(8,128)} custom-call(s32[1]{0:T(128)} %bitcast.place_ref, bf16[256,512]{1,0:T(8,128)(2,1)S(1)} %get-tuple-element.23.high_ref, bf16[256,512]{1,0:T(8,128)(2,1)S(1)} %get-tuple-element.24.low_ref, f32[64,512]{1,0:T(8,128)S(1)} %collective-permute-done.6.refs_0_, f32[64,512]{1,0:T(8,128)S(1)} %collective-permute-done.13.refs_1_, ...), custom_call_target="tpu_custom_call" | custom-call | flops 1006632960 | bytes 655360 | tf_op jit(solution)/shard_map/difference/pallas_call | solution.py:297
  (52 shorter events, 3.3 us)
Async XLA Ops:
  0.7 1.2 %copy-start = (f32[1,64,4096]{2,1,0:T(8,128)S(1)}, f32[1,64,4096]{2,1,0:T(8,128)}, u32[]{:S(2)}) copy-start(f32[1,64,4096]{2,1,0:T(8,128)} %param.8) | copy-start | bytes 3145732
  2.2 1.7 %collective-permute-start.7 = (f32[64,1024]{1,0:T(8,128)S(1)}, f32[64,1024]{1,0:T(8,128)S(1)}, u32[]{:S(2)}, u32[]{:S(2)}) collective-permute-start(f32[64,1024]{1,0:T(8,128)S(1)} %get-tuple-element.32), channel_id=1, source_target_pairs={{0,1},{1,0},{2,3},{3,2},{4,5},{5,4},{6,7},{7,6},{8,9},{9,8},{10,11... | collective-permute-start | bytes 786440 | tf_op jit(solution)/shard_map/ppermute | solution.py:311
  3.0 4.0 %copy-start.1 = (f32[1,64,4096]{2,1,0:T(8,128)S(1)}, f32[1,64,4096]{2,1,0:T(8,128)}, u32[]{:S(2)}) copy-start(f32[1,64,4096]{2,1,0:T(8,128)} %param.8) | copy-start | bytes 3145732
  3.0 4.2 %collective-permute-start = (f32[64,1024]{1,0:T(8,128)S(1)}, f32[64,1024]{1,0:T(8,128)S(1)}, u32[]{:S(2)}, u32[]{:S(2)}) collective-permute-start(f32[64,1024]{1,0:T(8,128)S(1)} %get-tuple-element.26), channel_id=1, source_target_pairs={{0,1},{1,0},{2,3},{3,2},{4,5},{5,4},{6,7},{7,6},{8,9},{9,8},{10,11... | collective-permute-start | bytes 786440 | tf_op jit(solution)/shard_map/ppermute | solution.py:311
  3.9 6.8 %collective-permute-start.8 = (f32[64,512]{1,0:T(8,128)S(1)}, f32[64,512]{1,0:T(8,128)S(1)}, u32[]{:S(2)}, u32[]{:S(2)}) collective-permute-start(f32[64,512]{1,0:T(8,128)S(1)} %get-tuple-element.34), channel_id=1, source_target_pairs={{0,4},{1,5},{2,6},{3,7},{4,0},{5,1},{6,2},{7,3},{8,12},{9,13},{10,... | collective-permute-start | bytes 393224 | tf_op jit(solution)/shard_map/ppermute | solution.py:311
  7.2 5.3 %collective-permute-start.1 = (f32[64,512]{1,0:T(8,128)S(1)}, f32[64,512]{1,0:T(8,128)S(1)}, u32[]{:S(2)}, u32[]{:S(2)}) collective-permute-start(f32[64,512]{1,0:T(8,128)S(1)} %get-tuple-element.28), channel_id=1, source_target_pairs={{0,2},{1,3},{2,0},{3,1},{4,6},{5,7},{6,4},{7,5},{8,10},{9,11},{10,... | collective-permute-start | bytes 393224 | tf_op jit(solution)/shard_map/ppermute | solution.py:311
  10.8 4.3 %collective-permute-start.9 = (f32[64,256]{1,0:T(8,128)S(1)}, f32[64,256]{1,0:T(8,128)S(1)}, u32[]{:S(2)}, u32[]{:S(2)}) collective-permute-start(f32[64,256]{1,0:T(8,128)S(1)} %get-tuple-element.36), channel_id=1, source_target_pairs={{0,2},{1,3},{2,0},{3,1},{4,6},{5,7},{6,4},{7,5},{8,10},{9,11},{10,... | collective-permute-start | bytes 196616 | tf_op jit(solution)/shard_map/ppermute | solution.py:311
  12.6 5.4 %collective-permute-start.2 = (f32[64,256]{1,0:T(8,128)S(1)}, f32[64,256]{1,0:T(8,128)S(1)}, u32[]{:S(2)}, u32[]{:S(2)}) collective-permute-start(f32[64,256]{1,0:T(8,128)S(1)} %get-tuple-element.30), channel_id=1, source_target_pairs={{0,4},{1,5},{2,6},{3,7},{4,0},{5,1},{6,2},{7,3},{8,12},{9,13},{10,... | collective-permute-start | bytes 196616 | tf_op jit(solution)/shard_map/ppermute | solution.py:311
  15.1 7.1 %collective-permute-start.10 = (f32[64,256]{1,0:T(8,128)S(1)}, f32[64,256]{1,0:T(8,128)S(1)}, u32[]{:S(2)}, u32[]{:S(2)}) collective-permute-start(f32[64,256]{1,0:T(8,128)S(1)} %add.14), channel_id=1, source_target_pairs={{0,8},{1,9},{2,10},{3,11},{4,12},{5,13},{6,14},{7,15},{8,0},{9,1},... | collective-permute-start | bytes 196616 | tf_op jit(solution)/shard_map/ppermute | solution.py:311
  17.9 5.8 %collective-permute-start.3 = (f32[64,256]{1,0:T(8,128)S(1)}, f32[64,256]{1,0:T(8,128)S(1)}, u32[]{:S(2)}, u32[]{:S(2)}) collective-permute-start(f32[64,256]{1,0:T(8,128)S(1)} %add.12), channel_id=1, source_target_pairs={{0,8},{1,9},{2,10},{3,11},{4,12},{5,13},{6,14},{7,15},{8,0},{9,1},... | collective-permute-start | bytes 196616 | tf_op jit(solution)/shard_map/ppermute | solution.py:311
  22.2 4.3 %collective-permute-start.11 = (f32[64,256]{1,0:T(8,128)S(1)}, f32[64,256]{1,0:T(8,128)S(1)}, u32[]{:S(2)}, u32[]{:S(2)}) collective-permute-start(f32[64,256]{1,0:T(8,128)S(1)} %broadcast_divide_fusion), channel_id=1, source_target_pairs={{0,2},{1,3},{2,0},{3,1},{4,6},{5,7},{6,4},{7,5},{8,10},{9,11},{10,... | collective-permute-start | bytes 196616 | tf_op jit(solution)/shard_map/ppermute | solution.py:311
  23.8 5.8 %copy-start.2 = (f32[15,32,128]{2,1,0:T(8,128)S(1)}, f32[15,32,128]{2,1,0:T(8,128)}, u32[]{:S(2)}) copy-start(f32[15,32,128]{2,1,0:T(8,128)} %constant.29.clone.vert_ref) | copy-start | bytes 737284
  23.8 4.3 %collective-permute-start.4 = (f32[64,256]{1,0:T(8,128)S(1)}, f32[64,256]{1,0:T(8,128)S(1)}, u32[]{:S(2)}, u32[]{:S(2)}) collective-permute-start(f32[64,256]{1,0:T(8,128)S(1)} %broadcast_divide_fusion.1), channel_id=1, source_target_pairs={{0,4},{1,5},{2,6},{3,7},{4,0},{5,1},{6,2},{7,3},{8,12},{9,13},{10,... | collective-permute-start | bytes 196616 | tf_op jit(solution)/shard_map/ppermute | solution.py:311
  26.6 3.1 %copy-start.3 = (f32[16,2048]{1,0:T(8,128)S(1)}, f32[16,2048]{1,0:T(8,128)}, u32[]{:S(2)}) copy-start(f32[16,2048]{1,0:T(8,128)} %constant.28.clone.horiz_ref) | copy-start | bytes 393220
  26.6 3.1 %copy-start.4 = (f32[49,16]{1,0:T(8,128)S(1)}, f32[49,16]{1,0:T(8,128)}, u32[]{:S(2)}) copy-start(f32[49,16]{1,0:T(8,128)} %constant.27.clone.horiz_pick_ref) | copy-start | bytes 9412
  26.6 3.1 %copy-start.5 = (f32[16,49,3]{1,0,2:T(8,128)S(1)}, f32[16,49,3]{1,0,2:T(8,128)}, u32[]{:S(2)}) copy-start(f32[16,49,3]{1,0,2:T(8,128)} %param.10) | copy-start | bytes 28228
  26.6 7.5 %collective-permute-start.12 = (f32[64,512]{1,0:T(8,128)S(1)}, f32[64,512]{1,0:T(8,128)S(1)}, u32[]{:S(2)}, u32[]{:S(2)}) collective-permute-start(f32[64,512]{1,0:T(8,128)S(1)} %maximum_select_fusion.1.refs_0_), channel_id=1, source_target_pairs={{0,4},{1,5},{2,6},{3,7},{4,0},{5,1},{6,2},{7,3},{8,12},{9,13},{10,... | collective-permute-start | bytes 393224 | tf_op jit(solution)/shard_map/ppermute | solution.py:311
  28.2 1.5 %copy-start.6 = (f32[16,49]{1,0:T(8,128)S(1)}, f32[16,49]{1,0:T(8,128)}, u32[]{:S(2)}) copy-start(f32[16,49]{1,0:T(8,128)} %constant.26.clone.vert_pick_ref) | copy-start | bytes 9412
  28.2 6.0 %collective-permute-start.5 = (f32[64,512]{1,0:T(8,128)S(1)}, f32[64,512]{1,0:T(8,128)S(1)}, u32[]{:S(2)}, u32[]{:S(2)}) collective-permute-start(f32[64,512]{1,0:T(8,128)S(1)} %maximum_select_fusion.refs_0_), channel_id=1, source_target_pairs={{0,2},{1,3},{2,0},{3,1},{4,6},{5,7},{6,4},{7,5},{8,10},{9,11},{10,... | collective-permute-start | bytes 393224 | tf_op jit(solution)/shard_map/ppermute | solution.py:311
  29.2 5.5 %collective-permute-start.15 = (f32[64,512]{1,0:T(8,128)S(1)}, f32[64,512]{1,0:T(8,128)S(1)}, u32[]{:S(2)}, u32[]{:S(2)}) collective-permute-start(f32[64,512]{1,0:T(8,128)S(1)} %maximum_select_fusion.1.refs_0_), channel_id=1, source_target_pairs={{0,1},{1,0},{2,3},{3,2},{4,5},{5,4},{6,7},{7,6},{8,9},{9,8},{10,11... | collective-permute-start | bytes 393224 | tf_op jit(solution)/shard_map/ppermute | solution.py:311
  29.2 5.5 %collective-permute-start.14 = (f32[64,512]{1,0:T(8,128)S(1)}, f32[64,512]{1,0:T(8,128)S(1)}, u32[]{:S(2)}, u32[]{:S(2)}) collective-permute-start(f32[64,512]{1,0:T(8,128)S(1)} %maximum_select_fusion.refs_0_), channel_id=1, source_target_pairs={{0,1},{1,0},{2,3},{3,2},{4,5},{5,4},{6,7},{7,6},{8,9},{9,8},{10,11... | collective-permute-start | bytes 393224 | tf_op jit(solution)/shard_map/ppermute | solution.py:311
  29.7 0.7 %copy-start.7 = (s32[16]{0:T(128)S(1)}, s32[16]{0:T(128)}, u32[]{:S(2)}) copy-start(s32[16]{0:T(128)} %param.11) | copy-start | bytes 196
  34.1 4.3 %collective-permute-start.13 = (f32[64,512]{1,0:T(8,128)S(1)}, f32[64,512]{1,0:T(8,128)S(1)}, u32[]{:S(2)}, u32[]{:S(2)}) collective-permute-start(f32[64,512]{1,0:T(8,128)S(1)} %collective-permute-done.12.refs_1_), channel_id=1, source_target_pairs={{0,1},{1,0},{2,3},{3,2},{4,5},{5,4},{6,7},{7,6},{8,9},{9,8},{10,11... | collective-permute-start | bytes 393224 | tf_op jit(solution)/shard_map/ppermute | solution.py:311
  34.2 4.2 %collective-permute-start.6 = (f32[64,512]{1,0:T(8,128)S(1)}, f32[64,512]{1,0:T(8,128)S(1)}, u32[]{:S(2)}, u32[]{:S(2)}) collective-permute-start(f32[64,512]{1,0:T(8,128)S(1)} %collective-permute-done.5.refs_0_), channel_id=1, source_target_pairs={{0,1},{1,0},{2,3},{3,2},{4,5},{5,4},{6,7},{7,6},{8,9},{9,8},{10,11... | collective-permute-start | bytes 393224 | tf_op jit(solution)/shard_map/ppermute | solution.py:311
  (1 other events, 0.7 us)

commit v4 on v3

--- a/solution.py
+++ b/solution.py
@@ -16,6 +16,7 @@
 GROUPS = 4
 GRANT = 12 << 20
 STREAMS = 2
+PRODUCT = 1280
 
 gauss_widths = (1.5, 3.0, 6.0)
 gauss_degrees = (6, 4, 2)
@@ -177,51 +178,69 @@
     )(place, *arrays)
 
 
-def piece_model(high_ref, low_ref, template_ref, first_column, total_columns, wide_high, wide_low, partial):
-    padded_rows, columns = template_ref.shape
-    domain = wide_high.shape[1]
-    size = partial.shape[0] // GROUPS
-    rows = size // 2
-    template = jnp.concatenate(
-        [template_ref[...], jnp.zeros((padded_rows, domain - columns), jnp.float32)], axis=1
-    )
+def widen(template, lanes, wide_high, wide_low):
+    padded_rows, columns = template.shape
+    domain = columns + LANES
+    template = jnp.concatenate([template, jnp.zeros((padded_rows, LANES), jnp.float32)], axis=1)
     for shift in range(SHIFTS):
         moved = template if shift == 0 else pltpu.roll(template, domain - shift, 1)
         high = moved.astype(jnp.bfloat16)
         low = (moved - high.astype(jnp.float32)).astype(jnp.bfloat16)
-        wide_high[shift * padded_rows : (shift + 1) * padded_rows] = high
-        wide_low[shift * padded_rows : (shift + 1) * padded_rows] = low
-    high = wide_high[...]
-    total = jnp.dot(high_ref[...], high, preferred_element_type=jnp.float32)
-    total += jnp.dot(low_ref[...], high, preferred_element_type=jnp.float32)
-    total += jnp.dot(high_ref[...], wide_low[...], preferred_element_type=jnp.float32)
-    partial[...] = total
+        wide_high[shift * padded_rows : (shift + 1) * padded_rows, lanes] = high
+        wide_low[shift * padded_rows : (shift + 1) * padded_rows, lanes] = low
+
+
+def multiply(high_ref, low_ref, wide_high, wide_low, partial):
+    lanes = partial.shape[1]
+    block = PRODUCT if lanes % PRODUCT == 0 else lanes
+    for start in range(0, lanes, block):
+        here = slice(start, start + block)
+        high = wide_high[:, here]
+        total = jnp.dot(high_ref[...], high, preferred_element_type=jnp.float32)
+        total += jnp.dot(low_ref[...], high, preferred_element_type=jnp.float32)
+        total += jnp.dot(high_ref[...], wide_low[:, here], preferred_element_type=jnp.float32)
+        partial[:, here] = total
+
+
+def gathered(partial, lanes, first_column, total_columns):
+    size = partial.shape[0] // GROUPS
+    rows = size // 2
+    domain = lanes.stop - lanes.start
     total = jnp.zeros((size, domain), jnp.float32)
     for group in range(GROUPS):
         amount = (HALF - SHIFTS * group) % domain
-        total = total + pltpu.roll(partial[group * size : (group + 1) * size], amount, 1)
+        total = total + pltpu.roll(partial[group * size : (group + 1) * size, lanes], amount, 1)
     lane = lax.broadcasted_iota(jnp.int32, (rows, domain), 1)
-    column = first_column + jnp.where(lane < columns + LANES // 2, lane, lane - domain)
+    column = first_column + jnp.where(lane < domain - LANES // 2, lane, lane - domain)
     position = (2.0 * column.astype(jnp.float32) + 1.0) / total_columns - 1.0
     return total[:rows] + position * total[rows:]
 
 
-def piece_column(place, bit, stream, other, twin, width):
-    side = (place & 1) ^ twin
-    part = (jnp.right_shift(place, bit) & 1) ^ other
-    return pl.multiple_of(side * (2 * STREAMS * width) + stream * (2 * width) + part * width, LANES)
+def piece_column(place, twin, stream, choices, half):
+    width = half // STREAMS
+    first = ((place & 1) ^ twin) * half + stream * width
+    for bit, other in choices:
+        width = width // 2
+        first = first + ((jnp.right_shift(place, bit) & 1) ^ other) * width
+    return pl.multiple_of(first, LANES)
 
 
 def add_pieces(pieces, place, high_ref, low_ref, template_refs, total_columns, model_ref, scratch):
+    wide_high, wide_low, partial = scratch
     lane = lax.broadcasted_iota(jnp.int32, (model_ref.shape[0], LANES), 1)
-    for index, (piece, template_ref) in enumerate(zip(pieces, template_refs)):
-        width = template_ref.shape[1]
-        first = piece_column(place, *piece, width)
-        model = piece_model(
-            high_ref, low_ref, template_ref, first, total_columns, *scratch[3 * index : 3 * index + 3]
-        )
+    spans, stop = [], 0
+    for template_ref in template_refs:
+        start, stop = stop, stop + template_ref.shape[1] + LANES
+        spans.append(slice(start, stop))
+    for span, template_ref in zip(spans, template_refs):
+        widen(template_ref[...], span, wide_high, wide_low)
+    multiply(high_ref, low_ref, wide_high, wide_low, partial)
+    for span, piece in zip(spans, pieces):
+        width = span.stop - span.start - LANES
+        first = piece_column(place, *piece, total_columns // 2)
+        model = gathered(partial, span, first, total_columns)
         spill = model[:, width:]
-        body = pl.ds(first + LANES, width)
+        body = pl.ds(pl.multiple_of(first + LANES, LANES), width)
         model_ref[:, body] = model_ref[:, body] + model[:, :width]
         before = pl.ds(first, LANES)
         model_ref[:, before] = model_ref[:, before] + jnp.where(lane < LANES // 2, 0.0, spill)
@@ -244,35 +263,67 @@
     count, parts = len(pieces), 2 * STREAMS
     templates, refs = refs[:count], refs[count:]
     model_ref, image_ref, valid_refs = refs[0], refs[1], refs[2 : 2 + parts]
-    out_ref, total_ref = refs[2 + parts : 4 + parts]
+    out_ref, total_ref, valid_all, ready, early_sem, late_sem = refs[2 + parts : 8 + parts]
     rows, columns = out_ref.shape
-    width = columns // parts
+    half, width = columns // 2, columns // parts
+    side = place_ref[0] & 1
+    for part, valid_ref in enumerate(valid_refs):
+        first = ((side ^ (part // STREAMS)) * STREAMS + part % STREAMS) * width
+        valid_all[:, pl.ds(pl.multiple_of(first, width), width)] = valid_ref[...]
+
+    def finish(first, size, model, sem):
+        first = pl.multiple_of(first, LANES)
+        lanes = pl.ds(first, size)
+        centre = image_ref[MARGIN : MARGIN + rows, lanes]
+        ready[:, lanes] = valid_all[:, lanes] * (centre - model[:, pl.ds(pl.multiple_of(first + LANES, LANES), size)])
+        copy = pltpu.make_async_copy(ready.at[:, lanes], out_ref.at[:, lanes], sem)
+        copy.start()
+        return copy
+
+    early = finish(side * (half + LANES), half - LANES, model_ref, early_sem)
     total_ref[...] = model_ref[...]
-    add_pieces(pieces, place_ref[0], high_ref, low_ref, templates, columns, total_ref, refs[4 + parts :])
-    for part, valid_ref in enumerate(valid_refs):
-        side = (place_ref[0] & 1) ^ (part // STREAMS)
-        first = pl.multiple_of((side * STREAMS + part % STREAMS) * width, width)
-        lanes = pl.ds(first, width)
-        model = total_ref[:, pl.ds(pl.multiple_of(first + LANES, LANES), width)]
-        out_ref[:, lanes] = valid_ref[...] * (image_ref[MARGIN : MARGIN + rows, lanes] - model)
-
-
-def model_scratch(rows, padded_rows, width):
-    domain = width + LANES
+    add_pieces(pieces, place_ref[0], high_ref, low_ref, templates, columns, total_ref, refs[8 + parts :])
+    late = finish((1 - side) * (half - LANES), half + LANES, total_ref, late_sem)
+    early.wait()
+    late.wait()
+
+
+def model_scratch(rows, templates):
+    padded_rows = templates[0].shape[0]
+    lanes = sum(template.shape[1] + LANES for template in templates)
     return [
-        pltpu.VMEM((SHIFTS * padded_rows, domain), jnp.bfloat16),
-        pltpu.VMEM((SHIFTS * padded_rows, domain), jnp.bfloat16),
-        pltpu.VMEM((2 * GROUPS * rows, domain), jnp.float32),
+        pltpu.VMEM((SHIFTS * padded_rows, lanes), jnp.bfloat16),
+        pltpu.VMEM((SHIFTS * padded_rows, lanes), jnp.bfloat16),
+        pltpu.VMEM((2 * GROUPS * rows, lanes), jnp.float32),
     ]
 
 
-def model_cost(rows, padded_rows, width, pieces=1):
-    flops = 12 * GROUPS * rows * SHIFTS * padded_rows * (width + LANES) * pieces
-    return pl.CostEstimate(flops=flops, bytes_accessed=10 * padded_rows * width * pieces, transcendentals=0)
+def model_cost(rows, templates):
+    padded_rows = templates[0].shape[0]
+    lanes = sum(template.shape[1] + LANES for template in templates)
+    flops = 12 * GROUPS * rows * SHIFTS * padded_rows * lanes
+    return pl.CostEstimate(flops=flops, bytes_accessed=10 * padded_rows * lanes, transcendentals=0)
+
+
+def norm_kernel(kept_ref, arrived_ref, out_ref):
+    total = kept_ref[...] + arrived_ref[...]
+    out_ref[...] = total / jnp.maximum(total[:1], 1.0)
+
+
+def template_of(kept, arrived):
+    vmem = pl.BlockSpec(memory_space=pltpu.VMEM)
+    return pl.pallas_call(
+        norm_kernel,
+        in_specs=[vmem, vmem],
+        out_specs=vmem,
+        out_shape=jax.ShapeDtypeStruct(kept.shape, jnp.float32),
+        compiler_params=pltpu.CompilerParams(vmem_limit_bytes=GRANT),
+        cost_estimate=pl.CostEstimate(flops=4 * kept.size, bytes_accessed=12 * kept.size, transcendentals=0),
+        name="template",
+    )(kept, arrived)
 
 
 def add_models(place, high, low, pieces, templates, model, rows, total_columns):
-    padded_rows, width = templates[0].shape
     count = len(templates)
     fresh = model is None
     vmem = pl.BlockSpec(memory_space=pltpu.VMEM)
@@ -281,27 +332,32 @@
         in_specs=[pl.BlockSpec(memory_space=pltpu.SMEM)] + [vmem] * (2 + count + (not fresh)),
         out_specs=vmem,
         out_shape=jax.ShapeDtypeStruct((rows, total_columns + 2 * LANES), jnp.float32),
-        scratch_shapes=model_scratch(rows, padded_rows, width) * count,
+        scratch_shapes=model_scratch(rows, templates),
         input_output_aliases={} if fresh else {3 + count: 0},
         compiler_params=pltpu.CompilerParams(vmem_limit_bytes=GRANT),
-        cost_estimate=model_cost(rows, padded_rows, width, count),
+        cost_estimate=model_cost(rows, templates),
         name="add_models",
     )(place, high, low, *templates, *(() if fresh else (model,)))
 
 
 def difference(place, high, low, pieces, templates, model, image, valids):
-    padded_rows, width = templates[0].shape
-    count = len(templates)
-    rows = model.shape[0]
+    rows, columns = model.shape[0], image.shape[1]
     vmem = pl.BlockSpec(memory_space=pltpu.VMEM)
     return pl.pallas_call(
         functools.partial(difference_kernel, pieces),
-        in_specs=[pl.BlockSpec(memory_space=pltpu.SMEM)] + [vmem] * (4 + count + len(valids)),
-        out_specs=vmem,
-        out_shape=jax.ShapeDtypeStruct((rows, image.shape[1]), jnp.float32),
-        scratch_shapes=[pltpu.VMEM(model.shape, jnp.float32)] + model_scratch(rows, padded_rows, width) * count,
-        compiler_params=pltpu.CompilerParams(vmem_limit_bytes=GRANT),
-        cost_estimate=model_cost(rows, padded_rows, width, count),
+        in_specs=[pl.BlockSpec(memory_space=pltpu.SMEM)] + [vmem] * (4 + len(templates) + len(valids)),
+        out_specs=pl.BlockSpec(memory_space=pl.ANY),
+        out_shape=jax.ShapeDtypeStruct((rows, columns), jnp.float32),
+        scratch_shapes=[
+            pltpu.VMEM(model.shape, jnp.float32),
+            pltpu.VMEM((1, columns), jnp.float32),
+            pltpu.VMEM((rows, columns), jnp.float32),
+            pltpu.SemaphoreType.DMA,
+            pltpu.SemaphoreType.DMA,
+        ]
+        + model_scratch(rows, templates),
+        compiler_params=pltpu.CompilerParams(vmem_limit_bytes=GRANT),
+        cost_estimate=model_cost(rows, templates),
         name="difference",
     )(place, high, low, *templates, model, image, *valids)
 
@@ -348,29 +404,38 @@
     cells = [cells[stream] + others[stream] for stream in streams]
     others = [exchange(cells[stream], bits - 1) for stream in streams]
     high, low = weights(place, coefficients, epoch_order, rows, padded_rows)
-    cells = [cells[stream] + others[stream] for stream in streams]
-    cells = [part / jnp.maximum(part[:1], 1.0) for part in cells]
-    for step in reversed(range(1, bits - 2)):
-        others = [exchange(cells[stream], orders[stream][step]) for stream in streams]
-        cells = [
-            joined_columns(
-                cells[stream], others[stream], jnp.right_shift(index, orders[stream][step]) & 1
-            )
+    for stream in streams:
+        cells[stream] = template_of(cells[stream], others[stream])
+
+    def joined(cells, others, step):
+        return [
+            joined_columns(cells[stream], others[stream], jnp.right_shift(index, orders[stream][step]) & 1)
             for stream in streams
         ]
-    kinds = [
-        [(orders[stream][0], stream, other, twin) for stream in streams] for other in range(2) for twin in range(2)
-    ]
-    others = [exchange(cells[stream], orders[stream][0]) for stream in streams]
+
+    def gather_step(cells, step):
+        return [exchange(cells[stream], orders[stream][step]) for stream in streams]
+
+    def pieces(twin, others):
+        return [
+            (twin, stream, tuple((orders[stream][level], other) for level, other in enumerate(others)))
+            for stream in streams
+        ]
+
+    for step in reversed(range(2, bits - 2)):
+        cells = joined(cells, gather_step(cells, step), step)
+    others = gather_step(cells, 1)
     twins = [exchange(cells[stream], 0) for stream in streams]
-    model = None
-    for stream in reversed(streams):
-        model = add_models(place, high, low, [kinds[0][stream]], [cells[stream]], model, rows, columns)
-    model = add_models(place, high, low, kinds[1], twins, model, rows, columns)
-    twins = [exchange(others[stream], 0) for stream in streams]
-    model = add_models(place, high, low, kinds[2], others, model, rows, columns)
+    model = add_models(place, high, low, pieces(0, (0, 0)), cells, None, rows, columns)
+    cells, quarter = joined(cells, others, 1), others
+    others = gather_step(cells, 0)
+    model = add_models(place, high, low, pieces(0, (0, 1)) + pieces(1, (0, 0)), quarter + twins, model, rows, columns)
+    twins = [exchange(quarter[stream], 0) for stream in streams]
+    ends = [exchange(others[stream], 0) for stream in streams]
+    model = add_models(place, high, low, pieces(1, (0, 1)), twins, model, rows, columns)
+    model = add_models(place, high, low, pieces(0, (1,)), others, model, rows, columns)
     valids = [piece[1] for piece in near + far]
-    return difference(place, high, low, kinds[3], twins, model, image, valids)[None]
+    return difference(place, high, low, pieces(1, (1,)), ends, model, image, valids)[None]
 
 
 def solution(mesh):

time: 41.3 us -> 42.3 us (1.024)
  starting transfers between devices: 18.5 us -> 19.1 us
  waiting for transfers between devices: 8.58 us -> 9.17 us
    ppermute x16 -> x18, starting transfers between devices: 18.5 us -> 19.1 us  [exchange(): lax.ppermute(cells, 'epoch', [(i, i ^ 1 << bit) for i in range(count)])]
    ppermute x16 -> x18, waiting for transfers between devices: 8.58 us -> 9.17 us  [exchange(): lax.ppermute(cells, 'epoch', [(i, i ^ 1 << bit) for i in range(count)])]
  transfers between devices with their start and end apart: 16 -> 18, of which waited for: 6 -> 6; matrix products, arithmetic and copies ran while one was open for 0% -> 0% of each run, Pallas kernels for 20% -> 19%
where the time goes in v4:
time: 42.3 us; the launch traced here: 42.1 us
  starting transfers between devices  19.1 us (45%)
  Pallas kernels  11 us (26%)
  waiting for transfers between devices  9.17 us (22%)
  local copies, waits for them, and re-layouts  2.53 us (6%)
    ppermute x18, starting transfers between devices, exchange(): lax.ppermute(cells, 'epoch', [(i, i ^ 1 << bit) for i in range(count)])  19.1 us
    ppermute x18, waiting for transfers between devices, exchange(): lax.ppermute(cells, 'epoch', [(i, i ^ 1 << bit) for i in range(count)])  9.17 us
    pallas_call x4, Pallas kernels, add_models(): pl.pallas_call(functools.partial(model_kernel, pieces, total_columns, fre...  5.96 us
    pallas_call x1, Pallas kernels, difference(): pl.pallas_call(functools.partial(difference_kernel, pieces), in_specs=[pl...  2.59 us
    unnamed x18, local copies, waits for them, and re-layouts  2.53 us
    pallas_call x1, Pallas kernels, weights(): pl.pallas_call(weight_kernel, in_specs=[smem] + [vmem] * len(arrays), out...  1.43 us
    pallas_call x4, Pallas kernels, masked_piece(): pl.pallas_call(functools.partial(mask_kernel, twin, stream), in_specs=[pl...  0.88 us
  transfers between devices with their start and end apart: 18, of which 6 were waited for; matrix products, arithmetic and copies ran while one was open for 0% of the time, Pallas kernels for 19%

profile of v4, /device:TPU:0, one launch (start us, length us, event | category | flops | bytes accessed | tf_op | source)
XLA Modules:
  0.0 42.1 jit_solution(11107405809177378722)
XLA Ops:
  0.0 0.7 %copy-done.8 = s32[1,1,128]{2,1,0:T(1,128)S(1)} copy-done((s32[1,1,128]{2,1,0:T(1,128)S(1)}, s32[1,1,128]{2,1,0:T(1,128)}, u32[]{:S(2)}) %copy-start.8) | copy-done | bytes 536
  0.7 1.2 %copy-done = f32[1,64,4096]{2,1,0:T(8,128)S(1)} copy-done((f32[1,64,4096]{2,1,0:T(8,128)S(1)}, f32[1,64,4096]{2,1,0:T(8,128)}, u32[]{:S(2)}) %copy-start) | copy-done | bytes 1048600
  3.3 0.6 %collective-permute-done.7.arrived_ref = f32[64,1024]{1,0:T(8,128)S(1)} collective-permute-done((f32[64,1024]{1,0:T(8,128)S(1)}, f32[64,1024]{1,0:T(8,128)S(1)}, u32[]{:S(2)}, u32[]{:S(2)}) %collective-permute-start.7) | collective-permute-done | bytes 262176 | tf_op jit(solution)/shard_map/ppermute | solution.py:367
  3.9 3.0 %collective-permute-start.8 = (f32[64,512]{1,0:T(8,128)S(1)}, f32[64,512]{1,0:T(8,128)S(1)}, u32[]{:S(2)}, u32[]{:S(2)}) collective-permute-start(f32[64,512]{1,0:T(8,128)S(1)} %get-tuple-element.34), channel_id=1, source_target_pairs={{0,4},{1,5},{2,6},{3,7},{4,0},{5,1},{6,2},{7,3},{8,12},{9,13},{10,... | collective-permute-start | bytes 393224 | tf_op jit(solution)/shard_map/ppermute | solution.py:367
  7.2 1.6 %collective-permute-start.1 = (f32[64,512]{1,0:T(8,128)S(1)}, f32[64,512]{1,0:T(8,128)S(1)}, u32[]{:S(2)}, u32[]{:S(2)}) collective-permute-start(f32[64,512]{1,0:T(8,128)S(1)} %get-tuple-element.28), channel_id=1, source_target_pairs={{0,2},{1,3},{2,0},{3,1},{4,6},{5,7},{6,4},{7,5},{8,10},{9,11},{10,... | collective-permute-start | bytes 393224 | tf_op jit(solution)/shard_map/ppermute | solution.py:367
  8.8 1.9 %collective-permute-done.8.arrived_ref = f32[64,512]{1,0:T(8,128)S(1)} collective-permute-done((f32[64,512]{1,0:T(8,128)S(1)}, f32[64,512]{1,0:T(8,128)S(1)}, u32[]{:S(2)}, u32[]{:S(2)}) %collective-permute-start.8) | collective-permute-done | bytes 131104 | tf_op jit(solution)/shard_map/ppermute | solution.py:367
  10.8 1.7 %collective-permute-start.9 = (f32[64,256]{1,0:T(8,128)S(1)}, f32[64,256]{1,0:T(8,128)S(1)}, u32[]{:S(2)}, u32[]{:S(2)}) collective-permute-start(f32[64,256]{1,0:T(8,128)S(1)} %get-tuple-element.36), channel_id=1, source_target_pairs={{0,2},{1,3},{2,0},{3,1},{4,6},{5,7},{6,4},{7,5},{8,10},{9,11},{10,... | collective-permute-start | bytes 196616 | tf_op jit(solution)/shard_map/ppermute | solution.py:367
  12.6 1.6 %collective-permute-start.2 = (f32[64,256]{1,0:T(8,128)S(1)}, f32[64,256]{1,0:T(8,128)S(1)}, u32[]{:S(2)}, u32[]{:S(2)}) collective-permute-start(f32[64,256]{1,0:T(8,128)S(1)} %get-tuple-element.30), channel_id=1, source_target_pairs={{0,4},{1,5},{2,6},{3,7},{4,0},{5,1},{6,2},{7,3},{8,12},{9,13},{10,... | collective-permute-start | bytes 196616 | tf_op jit(solution)/shard_map/ppermute | solution.py:367
  14.2 0.9 %collective-permute-done.9 = f32[64,256]{1,0:T(8,128)S(1)} collective-permute-done((f32[64,256]{1,0:T(8,128)S(1)}, f32[64,256]{1,0:T(8,128)S(1)}, u32[]{:S(2)}, u32[]{:S(2)}) %collective-permute-start.9) | collective-permute-done | bytes 65568 | tf_op jit(solution)/shard_map/ppermute | solution.py:367
  15.1 2.8 %collective-permute-start.10 = (f32[64,256]{1,0:T(8,128)S(1)}, f32[64,256]{1,0:T(8,128)S(1)}, u32[]{:S(2)}, u32[]{:S(2)}) collective-permute-start(f32[64,256]{1,0:T(8,128)S(1)} %add.7.kept_ref), channel_id=1, source_target_pairs={{0,8},{1,9},{2,10},{3,11},{4,12},{5,13},{6,14},{7,15},{8,0},{9,1},... | collective-permute-start | bytes 196616 | tf_op jit(solution)/shard_map/ppermute | solution.py:367
  18.0 2.1 %collective-permute-start.3 = (f32[64,256]{1,0:T(8,128)S(1)}, f32[64,256]{1,0:T(8,128)S(1)}, u32[]{:S(2)}, u32[]{:S(2)}) collective-permute-start(f32[64,256]{1,0:T(8,128)S(1)} %add.6.kept_ref), channel_id=1, source_target_pairs={{0,8},{1,9},{2,10},{3,11},{4,12},{5,13},{6,14},{7,15},{8,0},{9,1},... | collective-permute-start | bytes 196616 | tf_op jit(solution)/shard_map/ppermute | solution.py:367
  20.1 2.1 %collective-permute-done.10.arrived_ref = f32[64,256]{1,0:T(8,128)S(1)} collective-permute-done((f32[64,256]{1,0:T(8,128)S(1)}, f32[64,256]{1,0:T(8,128)S(1)}, u32[]{:S(2)}, u32[]{:S(2)}) %collective-permute-start.10) | collective-permute-done | bytes 65568 | tf_op jit(solution)/shard_map/ppermute | solution.py:367
  22.2 1.6 %collective-permute-start.11 = (f32[64,256]{1,0:T(8,128)S(1)}, f32[64,256]{1,0:T(8,128)S(1)}, u32[]{:S(2)}, u32[]{:S(2)}) collective-permute-start(f32[64,256]{1,0:T(8,128)S(1)} %template.3.refs_1_), channel_id=1, source_target_pairs={{0,2},{1,3},{2,0},{3,1},{4,6},{5,7},{6,4},{7,5},{8,10},{9,11},{10,... | collective-permute-start | bytes 196616 | tf_op jit(solution)/shard_map/ppermute | solution.py:367
  23.8 0.6 %copy-done.7 = s32[16]{0:T(128)S(1)} copy-done((s32[16]{0:T(128)S(1)}, s32[16]{0:T(128)}, u32[]{:S(2)}) %copy-start.7) | copy-done | bytes 88
  24.4 1.4 %kernel_weights.1 = (bf16[256,512]{1,0:T(8,128)(2,1)S(1)}, bf16[256,512]{1,0:T(8,128)(2,1)S(1)}) custom-call(s32[1]{0:T(128)} %bitcast.place_ref, s32[1,16]{1,0:T(1,128)S(1)} %bitcast.12, f32[3,16,49]{2,1,0:T(8,128)S(1)} %bitcast.11, f32[16,49]{1,0:T(8,128)S(1)} %copy-done.6, f32[49,16]{1,0:T(8,128)S(1)} %copy-done.4, f32[16,2048]{1,0:T(8,128)S(1)} %copy-done.3, ...), custom_call_target="tpu_custom_call" | custom-call | flops 100000000 | bytes 2000000 | tf_op jit(solution)/shard_map/kernel_weights/pallas_call | solution.py:170
  26.8 1.8 %collective-permute-start.12 = (f32[64,512]{1,0:T(8,128)S(1)}, f32[64,512]{1,0:T(8,128)S(1)}, u32[]{:S(2)}, u32[]{:S(2)}) collective-permute-start(f32[64,512]{1,0:T(8,128)S(1)} %maximum_select_fusion.1), channel_id=1, source_target_pairs={{0,4},{1,5},{2,6},{3,7},{4,0},{5,1},{6,2},{7,3},{8,12},{9,13},{10,... | collective-permute-start | bytes 393224 | tf_op jit(solution)/shard_map/ppermute | solution.py:367
  28.7 2.9 %collective-permute-done.4.refs_0_ = f32[64,256]{1,0:T(8,128)S(1)} collective-permute-done((f32[64,256]{1,0:T(8,128)S(1)}, f32[64,256]{1,0:T(8,128)S(1)}, u32[]{:S(2)}, u32[]{:S(2)}) %collective-permute-start.4) | collective-permute-done | bytes 65568 | tf_op jit(solution)/shard_map/ppermute | solution.py:367
  31.5 0.6 %collective-permute-start.5 = (f32[64,512]{1,0:T(8,128)S(1)}, f32[64,512]{1,0:T(8,128)S(1)}, u32[]{:S(2)}, u32[]{:S(2)}) collective-permute-start(f32[64,512]{1,0:T(8,128)S(1)} %maximum_select_fusion), channel_id=1, source_target_pairs={{0,2},{1,3},{2,0},{3,1},{4,6},{5,7},{6,4},{7,5},{8,10},{9,11},{10,... | collective-permute-start | bytes 393224 | tf_op jit(solution)/shard_map/ppermute | solution.py:367
  32.1 1.2 %add_models.4.refs_4_ = f32[32,4352]{1,0:T(8,128)S(1)} custom-call(s32[1]{0:T(128)} %bitcast.place_ref, bf16[256,512]{1,0:T(8,128)(2,1)S(1)} %get-tuple-element.23.high_ref, bf16[256,512]{1,0:T(8,128)(2,1)S(1)} %get-tuple-element.24.low_ref, f32[64,256]{1,0:T(8,128)S(1)} %template.2.refs_0_, f32[64,256]{1,0:T(8,128)S(1)} %template.3.refs_1_), custom_call_target="tpu_custom_call" | custom-call | flops 603979776 | bytes 491520 | tf_op jit(solution)/shard_map/add_models/pallas_call | solution.py:330
  33.9 1.9 %add_models.5.refs_2_ = f32[32,4352]{1,0:T(8,128)S(1)} custom-call(s32[1]{0:T(128)} %bitcast.place_ref, bf16[256,512]{1,0:T(8,128)(2,1)S(1)} %get-tuple-element.23.high_ref, bf16[256,512]{1,0:T(8,128)(2,1)S(1)} %get-tuple-element.24.low_ref, f32[64,256]{1,0:T(8,128)S(1)} %collective-permute-done.4.refs_0_, ...), custom_call_target="tpu_custom_call", output_to_operand_aliasing={{}: (7, {})} | custom-call | flops 1207959552 | bytes 983040 | tf_op jit(solution)/shard_map/add_models/pallas_call | solution.py:330
  35.9 0.6 %collective-permute-done.5.refs_0_ = f32[64,512]{1,0:T(8,128)S(1)} collective-permute-done((f32[64,512]{1,0:T(8,128)S(1)}, f32[64,512]{1,0:T(8,128)S(1)}, u32[]{:S(2)}, u32[]{:S(2)}) %collective-permute-start.5) | collective-permute-done | bytes 131104 | tf_op jit(solution)/shard_map/ppermute | solution.py:367
  36.6 1.1 %add_models.6.refs_2_ = f32[32,4352]{1,0:T(8,128)S(1)} custom-call(s32[1]{0:T(128)} %bitcast.place_ref, bf16[256,512]{1,0:T(8,128)(2,1)S(1)} %get-tuple-element.23.high_ref, bf16[256,512]{1,0:T(8,128)(2,1)S(1)} %get-tuple-element.24.low_ref, f32[64,256]{1,0:T(8,128)S(1)} %collective-permute-done.14.refs_0_, ...), custom_call_target="tpu_custom_call", output_to_operand_aliasing={{}: (5, {})} | custom-call | flops 603979776 | bytes 491520 | tf_op jit(solution)/shard_map/add_models/pallas_call | solution.py:330
  37.7 1.8 %add_models.7.refs_2_ = f32[32,4352]{1,0:T(8,128)S(1)} custom-call(s32[1]{0:T(128)} %bitcast.place_ref, bf16[256,512]{1,0:T(8,128)(2,1)S(1)} %get-tuple-element.23.high_ref, bf16[256,512]{1,0:T(8,128)(2,1)S(1)} %get-tuple-element.24.low_ref, f32[64,512]{1,0:T(8,128)S(1)} %collective-permute-done.5.refs_0_, ...), custom_call_target="tpu_custom_call", output_to_operand_aliasing={{}: (5, {})} | custom-call | flops 1006632960 | bytes 819200 | tf_op jit(solution)/shard_map/add_models/pallas_call | solution.py:330
  39.5 2.6 %difference.1 = f32[32,4096]{1,0:T(8,128)} custom-call(s32[1]{0:T(128)} %bitcast.place_ref, bf16[256,512]{1,0:T(8,128)(2,1)S(1)} %get-tuple-element.23.high_ref, bf16[256,512]{1,0:T(8,128)(2,1)S(1)} %get-tuple-element.24.low_ref, f32[64,512]{1,0:T(8,128)S(1)} %collective-permute-done.6.refs_0_, f32[64,512]{1,0:T(8,128)S(1)} %collective-permute-done.13.refs_1_, ...), custom_call_target="tpu_custom_call" | custom-call | flops 1006632960 | bytes 819200 | tf_op jit(solution)/shard_map/difference/pallas_call | solution.py:346
  (52 shorter events, 3.5 us)
Async XLA Ops:
  2.2 1.7 %collective-permute-start.7 = (f32[64,1024]{1,0:T(8,128)S(1)}, f32[64,1024]{1,0:T(8,128)S(1)}, u32[]{:S(2)}, u32[]{:S(2)}) collective-permute-start(f32[64,1024]{1,0:T(8,128)S(1)} %get-tuple-element.32), channel_id=1, source_target_pairs={{0,1},{1,0},{2,3},{3,2},{4,5},{5,4},{6,7},{7,6},{8,9},{9,8},{10,11... | collective-permute-start | bytes 786440 | tf_op jit(solution)/shard_map/ppermute | solution.py:367
  3.0 4.0 %copy-start.1 = (f32[1,64,4096]{2,1,0:T(8,128)S(1)}, f32[1,64,4096]{2,1,0:T(8,128)}, u32[]{:S(2)}) copy-start(f32[1,64,4096]{2,1,0:T(8,128)} %param.8) | copy-start | bytes 3145732
  3.0 4.2 %collective-permute-start = (f32[64,1024]{1,0:T(8,128)S(1)}, f32[64,1024]{1,0:T(8,128)S(1)}, u32[]{:S(2)}, u32[]{:S(2)}) collective-permute-start(f32[64,1024]{1,0:T(8,128)S(1)} %get-tuple-element.26), channel_id=1, source_target_pairs={{0,1},{1,0},{2,3},{3,2},{4,5},{5,4},{6,7},{7,6},{8,9},{9,8},{10,11... | collective-permute-start | bytes 786440 | tf_op jit(solution)/shard_map/ppermute | solution.py:367
  3.9 6.8 %collective-permute-start.8 = (f32[64,512]{1,0:T(8,128)S(1)}, f32[64,512]{1,0:T(8,128)S(1)}, u32[]{:S(2)}, u32[]{:S(2)}) collective-permute-start(f32[64,512]{1,0:T(8,128)S(1)} %get-tuple-element.34), channel_id=1, source_target_pairs={{0,4},{1,5},{2,6},{3,7},{4,0},{5,1},{6,2},{7,3},{8,12},{9,13},{10,... | collective-permute-start | bytes 393224 | tf_op jit(solution)/shard_map/ppermute | solution.py:367
  7.2 5.3 %collective-permute-start.1 = (f32[64,512]{1,0:T(8,128)S(1)}, f32[64,512]{1,0:T(8,128)S(1)}, u32[]{:S(2)}, u32[]{:S(2)}) collective-permute-start(f32[64,512]{1,0:T(8,128)S(1)} %get-tuple-element.28), channel_id=1, source_target_pairs={{0,2},{1,3},{2,0},{3,1},{4,6},{5,7},{6,4},{7,5},{8,10},{9,11},{10,... | collective-permute-start | bytes 393224 | tf_op jit(solution)/shard_map/ppermute | solution.py:367
  10.8 4.3 %collective-permute-start.9 = (f32[64,256]{1,0:T(8,128)S(1)}, f32[64,256]{1,0:T(8,128)S(1)}, u32[]{:S(2)}, u32[]{:S(2)}) collective-permute-start(f32[64,256]{1,0:T(8,128)S(1)} %get-tuple-element.36), channel_id=1, source_target_pairs={{0,2},{1,3},{2,0},{3,1},{4,6},{5,7},{6,4},{7,5},{8,10},{9,11},{10,... | collective-permute-start | bytes 196616 | tf_op jit(solution)/shard_map/ppermute | solution.py:367
  12.6 5.4 %collective-permute-start.2 = (f32[64,256]{1,0:T(8,128)S(1)}, f32[64,256]{1,0:T(8,128)S(1)}, u32[]{:S(2)}, u32[]{:S(2)}) collective-permute-start(f32[64,256]{1,0:T(8,128)S(1)} %get-tuple-element.30), channel_id=1, source_target_pairs={{0,4},{1,5},{2,6},{3,7},{4,0},{5,1},{6,2},{7,3},{8,12},{9,13},{10,... | collective-permute-start | bytes 196616 | tf_op jit(solution)/shard_map/ppermute | solution.py:367
  15.1 8.7 %copy-start.5 = (f32[16,49,3]{1,0,2:T(8,128)S(1)}, f32[16,49,3]{1,0,2:T(8,128)}, u32[]{:S(2)}) copy-start(f32[16,49,3]{1,0,2:T(8,128)} %param.10) | copy-start | bytes 28228
  15.1 8.7 %copy-start.6 = (f32[16,49]{1,0:T(8,128)S(1)}, f32[16,49]{1,0:T(8,128)}, u32[]{:S(2)}) copy-start(f32[16,49]{1,0:T(8,128)} %constant.24.clone.vert_pick_ref) | copy-start | bytes 9412
  15.1 8.7 %copy-start.2 = (f32[15,32,128]{2,1,0:T(8,128)S(1)}, f32[15,32,128]{2,1,0:T(8,128)}, u32[]{:S(2)}) copy-start(f32[15,32,128]{2,1,0:T(8,128)} %constant.27.clone.vert_ref) | copy-start | bytes 737284
  15.1 7.1 %collective-permute-start.10 = (f32[64,256]{1,0:T(8,128)S(1)}, f32[64,256]{1,0:T(8,128)S(1)}, u32[]{:S(2)}, u32[]{:S(2)}) collective-permute-start(f32[64,256]{1,0:T(8,128)S(1)} %add.7.kept_ref), channel_id=1, source_target_pairs={{0,8},{1,9},{2,10},{3,11},{4,12},{5,13},{6,14},{7,15},{8,0},{9,1},... | collective-permute-start | bytes 196616 | tf_op jit(solution)/shard_map/ppermute | solution.py:367
  18.0 5.8 %copy-start.3 = (f32[16,2048]{1,0:T(8,128)S(1)}, f32[16,2048]{1,0:T(8,128)}, u32[]{:S(2)}) copy-start(f32[16,2048]{1,0:T(8,128)} %constant.26.clone.horiz_ref) | copy-start | bytes 393220
  18.0 8.0 %collective-permute-start.3 = (f32[64,256]{1,0:T(8,128)S(1)}, f32[64,256]{1,0:T(8,128)S(1)}, u32[]{:S(2)}, u32[]{:S(2)}) collective-permute-start(f32[64,256]{1,0:T(8,128)S(1)} %add.6.kept_ref), channel_id=1, source_target_pairs={{0,8},{1,9},{2,10},{3,11},{4,12},{5,13},{6,14},{7,15},{8,0},{9,1},... | collective-permute-start | bytes 196616 | tf_op jit(solution)/shard_map/ppermute | solution.py:367
  22.2 1.6 %copy-start.4 = (f32[49,16]{1,0:T(8,128)S(1)}, f32[49,16]{1,0:T(8,128)}, u32[]{:S(2)}) copy-start(f32[49,16]{1,0:T(8,128)} %constant.25.clone.horiz_pick_ref) | copy-start | bytes 9412
  22.2 4.6 %collective-permute-start.11 = (f32[64,256]{1,0:T(8,128)S(1)}, f32[64,256]{1,0:T(8,128)S(1)}, u32[]{:S(2)}, u32[]{:S(2)}) collective-permute-start(f32[64,256]{1,0:T(8,128)S(1)} %template.3.refs_1_), channel_id=1, source_target_pairs={{0,2},{1,3},{2,0},{3,1},{4,6},{5,7},{6,4},{7,5},{8,10},{9,11},{10,... | collective-permute-start | bytes 196616 | tf_op jit(solution)/shard_map/ppermute | solution.py:367
  25.9 7.5 %collective-permute-start.17 = (f32[64,256]{1,0:T(8,128)S(1)}, f32[64,256]{1,0:T(8,128)S(1)}, u32[]{:S(2)}, u32[]{:S(2)}) collective-permute-start(f32[64,256]{1,0:T(8,128)S(1)} %template.3.refs_1_), channel_id=1, source_target_pairs={{0,1},{1,0},{2,3},{3,2},{4,5},{5,4},{6,7},{7,6},{8,9},{9,8},{10,11... | collective-permute-start | bytes 196616 | tf_op jit(solution)/shard_map/ppermute | solution.py:367
  26.0 7.9 %collective-permute-start.16 = (f32[64,256]{1,0:T(8,128)S(1)}, f32[64,256]{1,0:T(8,128)S(1)}, u32[]{:S(2)}, u32[]{:S(2)}) collective-permute-start(f32[64,256]{1,0:T(8,128)S(1)} %template.2.refs_0_), channel_id=1, source_target_pairs={{0,1},{1,0},{2,3},{3,2},{4,5},{5,4},{6,7},{7,6},{8,9},{9,8},{10,11... | collective-permute-start | bytes 196616 | tf_op jit(solution)/shard_map/ppermute | solution.py:367
  26.6 5.0 %collective-permute-start.4 = (f32[64,256]{1,0:T(8,128)S(1)}, f32[64,256]{1,0:T(8,128)S(1)}, u32[]{:S(2)}, u32[]{:S(2)}) collective-permute-start(f32[64,256]{1,0:T(8,128)S(1)} %template.2.refs_0_), channel_id=1, source_target_pairs={{0,4},{1,5},{2,6},{3,7},{4,0},{5,1},{6,2},{7,3},{8,12},{9,13},{10,... | collective-permute-start | bytes 196616 | tf_op jit(solution)/shard_map/ppermute | solution.py:367
  26.8 8.9 %collective-permute-start.12 = (f32[64,512]{1,0:T(8,128)S(1)}, f32[64,512]{1,0:T(8,128)S(1)}, u32[]{:S(2)}, u32[]{:S(2)}) collective-permute-start(f32[64,512]{1,0:T(8,128)S(1)} %maximum_select_fusion.1), channel_id=1, source_target_pairs={{0,4},{1,5},{2,6},{3,7},{4,0},{5,1},{6,2},{7,3},{8,12},{9,13},{10,... | collective-permute-start | bytes 393224 | tf_op jit(solution)/shard_map/ppermute | solution.py:367
  31.5 5.0 %collective-permute-start.5 = (f32[64,512]{1,0:T(8,128)S(1)}, f32[64,512]{1,0:T(8,128)S(1)}, u32[]{:S(2)}, u32[]{:S(2)}) collective-permute-start(f32[64,512]{1,0:T(8,128)S(1)} %maximum_select_fusion), channel_id=1, source_target_pairs={{0,2},{1,3},{2,0},{3,1},{4,6},{5,7},{6,4},{7,5},{8,10},{9,11},{10,... | collective-permute-start | bytes 393224 | tf_op jit(solution)/shard_map/ppermute | solution.py:367
  33.3 3.3 %collective-permute-start.15 = (f32[64,256]{1,0:T(8,128)S(1)}, f32[64,256]{1,0:T(8,128)S(1)}, u32[]{:S(2)}, u32[]{:S(2)}) collective-permute-start(f32[64,256]{1,0:T(8,128)S(1)} %collective-permute-done.11.refs_1_), channel_id=1, source_target_pairs={{0,1},{1,0},{2,3},{3,2},{4,5},{5,4},{6,7},{7,6},{8,9},{9,8},{10,11... | collective-permute-start | bytes 196616 | tf_op jit(solution)/shard_map/ppermute | solution.py:367
  33.4 3.2 %collective-permute-start.14 = (f32[64,256]{1,0:T(8,128)S(1)}, f32[64,256]{1,0:T(8,128)S(1)}, u32[]{:S(2)}, u32[]{:S(2)}) collective-permute-start(f32[64,256]{1,0:T(8,128)S(1)} %collective-permute-done.4.refs_0_), channel_id=1, source_target_pairs={{0,1},{1,0},{2,3},{3,2},{4,5},{5,4},{6,7},{7,6},{8,9},{9,8},{10,11... | collective-permute-start | bytes 196616 | tf_op jit(solution)/shard_map/ppermute | solution.py:367
  35.8 3.7 %collective-permute-start.13 = (f32[64,512]{1,0:T(8,128)S(1)}, f32[64,512]{1,0:T(8,128)S(1)}, u32[]{:S(2)}, u32[]{:S(2)}) collective-permute-start(f32[64,512]{1,0:T(8,128)S(1)} %collective-permute-done.12.refs_1_), channel_id=1, source_target_pairs={{0,1},{1,0},{2,3},{3,2},{4,5},{5,4},{6,7},{7,6},{8,9},{9,8},{10,11... | collective-permute-start | bytes 393224 | tf_op jit(solution)/shard_map/ppermute | solution.py:367
  36.6 2.9 %collective-permute-start.6 = (f32[64,512]{1,0:T(8,128)S(1)}, f32[64,512]{1,0:T(8,128)S(1)}, u32[]{:S(2)}, u32[]{:S(2)}) collective-permute-start(f32[64,512]{1,0:T(8,128)S(1)} %collective-permute-done.5.refs_0_), channel_id=1, source_target_pairs={{0,1},{1,0},{2,3},{3,2},{4,5},{5,4},{6,7},{7,6},{8,9},{9,8},{10,11... | collective-permute-start | bytes 393224 | tf_op jit(solution)/shard_map/ppermute | solution.py:367
  (3 other events, 2.5 us)

commit v5 on v4

--- a/solution.py
+++ b/solution.py
@@ -15,8 +15,9 @@
 SHIFTS = 8
 GROUPS = 4
 GRANT = 12 << 20
+FULL_GRANT = 67043328 - (2000 << 10)
 STREAMS = 2
-PRODUCT = 1280
+PRODUCT = 256
 
 gauss_widths = (1.5, 3.0, 6.0)
 gauss_degrees = (6, 4, 2)
@@ -64,43 +65,93 @@
     return vert_pick, horiz_pick, horiz_lanes, vert_lanes
 
 
-def mask_kernel(twin, stream, place_ref, octets_ref, image_ref, masked_ref, valid_ref):
-    width = masked_ref.shape[1]
-    word_count, piece_words = octets_ref.shape[1], width // 32
-    piece = ((place_ref[0] & 1) ^ twin) * STREAMS + stream
+def octets_of(words):
+    byte_row = lax.broadcasted_iota(jnp.int32, (8, words.shape[1]), 0)
+    octets = jnp.right_shift(jnp.broadcast_to(words, byte_row.shape), 8 * (byte_row & 3)) & 255
+    return octets.astype(jnp.float32)
+
+
+def valid_lanes(octets, piece, width):
+    word_count, piece_words = octets.shape[1], width // 32
     word_row = lax.broadcasted_iota(jnp.int32, (piece_words, width), 0)
     lane = lax.broadcasted_iota(jnp.int32, (piece_words, width), 1)
     spread = jnp.where(word_row == jnp.right_shift(lane, 5), 1.0, 0.0).astype(jnp.bfloat16)
-    octets = pltpu.roll(octets_ref[...], lax.rem(word_count - piece * piece_words, word_count), 1)
+    octets = pltpu.roll(octets, lax.rem(word_count - piece * piece_words, word_count), 1)
     octets = octets[:, :piece_words].astype(jnp.bfloat16)
     wide = jnp.dot(octets, spread, preferred_element_type=jnp.float32).astype(jnp.int32)
     lane = lax.broadcasted_iota(jnp.int32, wide.shape, 1)
     byte_row = lax.broadcasted_iota(jnp.int32, wide.shape, 0)
     bit = jnp.right_shift(wide, lane & 7) & 1
     bit = jnp.where(byte_row == (jnp.right_shift(lane, 3) & 3), bit, 0).astype(jnp.float32)
-    valid = jnp.sum(bit, axis=0, keepdims=True)
-    valid_ref[...] = valid
-    row = lax.broadcasted_iota(jnp.int32, masked_ref.shape, 0)
-    cells = image_ref[:, pl.ds(pl.multiple_of(piece * width, width), width)]
-    masked_ref[...] = jnp.where(row == 0, valid, valid * cells)
-
-
-def masked_piece(place, octets, image, twin, stream):
+    return jnp.sum(bit, axis=0, keepdims=True)
+
+
+def masked(valid, cells):
+    row = lax.broadcasted_iota(jnp.int32, cells.shape, 0)
+    return jnp.where(row == 0, valid, valid * cells)
+
+
+def first_kernel(stream, place_ref, words_ref, image_ref, masked_ref, words, cells, word_sem, cell_sem):
+    width = cells.shape[1]
+    piece = (1 - (place_ref[0] & 1)) * STREAMS + stream
+    lanes = pl.ds(pl.multiple_of(piece * width, width), width)
+    copies = (
+        pltpu.make_async_copy(words_ref, words, word_sem),
+        pltpu.make_async_copy(image_ref.at[:, lanes], cells, cell_sem),
+    )
+    for copy in copies:
+        copy.start()
+    copies[0].wait()
+    valid = valid_lanes(octets_of(words[...]), piece, width)
+    copies[1].wait()
+    masked_ref[...] = masked(valid, cells[...])
+
+
+def first_piece(place, words, image, stream):
+    rows, columns = image.shape
+    width = columns // (2 * STREAMS)
+    anywhere = pl.BlockSpec(memory_space=pl.ANY)
+    return pl.pallas_call(
+        functools.partial(first_kernel, stream),
+        in_specs=[pl.BlockSpec(memory_space=pltpu.SMEM), anywhere, anywhere],
+        out_specs=pl.BlockSpec(memory_space=pltpu.VMEM),
+        out_shape=jax.ShapeDtypeStruct((rows, width), jnp.float32),
+        scratch_shapes=[
+            pltpu.VMEM(words.shape, jnp.int32),
+            pltpu.VMEM((rows, width), jnp.float32),
+            pltpu.SemaphoreType.DMA,
+            pltpu.SemaphoreType.DMA,
+        ],
+        compiler_params=pltpu.CompilerParams(vmem_limit_bytes=FULL_GRANT),
+        cost_estimate=pl.CostEstimate(flops=rows * width, bytes_accessed=8 * rows * width, transcendentals=0),
+        name="first_piece",
+    )(place, words, image)
+
+
+def mask_kernel(twin, stream, place_ref, words_ref, image_ref, masked_ref, *valid_refs):
+    width = masked_ref.shape[1]
+    octets = octets_of(words_ref[...])
+    base = ((place_ref[0] & 1) ^ twin) * STREAMS
+    for index, valid_ref in enumerate(valid_refs):
+        valid_ref[...] = valid_lanes(octets, base + (stream + index) % STREAMS, width)
+    lanes = pl.ds(pl.multiple_of((base + stream) * width, width), width)
+    masked_ref[...] = masked(valid_refs[0][...], image_ref[:, lanes])
+
+
+def masked_piece(place, words, image, twin, stream, valids):
     rows, columns = image.shape
     width = columns // (2 * STREAMS)
     vmem = pl.BlockSpec(memory_space=pltpu.VMEM)
     return pl.pallas_call(
         functools.partial(mask_kernel, twin, stream),
         in_specs=[pl.BlockSpec(memory_space=pltpu.SMEM), vmem, vmem],
-        out_specs=[vmem, vmem],
-        out_shape=[
-            jax.ShapeDtypeStruct((rows, width), jnp.float32),
-            jax.ShapeDtypeStruct((1, width), jnp.float32),
-        ],
+        out_specs=[vmem] * (1 + valids),
+        out_shape=[jax.ShapeDtypeStruct((rows, width), jnp.float32)]
+        + [jax.ShapeDtypeStruct((1, width), jnp.float32)] * valids,
         compiler_params=pltpu.CompilerParams(vmem_limit_bytes=GRANT),
         cost_estimate=pl.CostEstimate(flops=rows * width, bytes_accessed=8 * rows * width, transcendentals=0),
         name="mask_piece",
-    )(place, octets, image)
+    )(place, words, image)
 
 
 def part_kernel(bit, place_ref, kept_ref, arrived_ref, keep_ref, send_ref):
@@ -182,19 +233,17 @@
     padded_rows, columns = template.shape
     domain = columns + LANES
     template = jnp.concatenate([template, jnp.zeros((padded_rows, LANES), jnp.float32)], axis=1)
-    for shift in range(SHIFTS):
-        moved = template if shift == 0 else pltpu.roll(template, domain - shift, 1)
-        high = moved.astype(jnp.bfloat16)
-        low = (moved - high.astype(jnp.float32)).astype(jnp.bfloat16)
-        wide_high[shift * padded_rows : (shift + 1) * padded_rows, lanes] = high
-        wide_low[shift * padded_rows : (shift + 1) * padded_rows, lanes] = low
+    main = template.astype(jnp.bfloat16).astype(jnp.float32)
+    for wide, part in ((wide_high, main), (wide_low, template - main)):
+        for shift in range(SHIFTS):
+            moved = part if shift == 0 else pltpu.roll(part, domain - shift, 1)
+            wide[shift * padded_rows : (shift + 1) * padded_rows, lanes] = moved.astype(jnp.bfloat16)
 
 
 def multiply(high_ref, low_ref, wide_high, wide_low, partial):
     lanes = partial.shape[1]
-    block = PRODUCT if lanes % PRODUCT == 0 else lanes
-    for start in range(0, lanes, block):
-        here = slice(start, start + block)
+    for start in range(0, lanes, PRODUCT):
+        here = slice(start, min(start + PRODUCT, lanes))
         high = wide_high[:, here]
         total = jnp.dot(high_ref[...], high, preferred_element_type=jnp.float32)
         total += jnp.dot(low_ref[...], high, preferred_element_type=jnp.float32)
@@ -388,14 +437,12 @@
     orders = list(range(1, bits - 1)), [2, 1] + list(range(3, bits - 1))
     streams = range(STREAMS)
 
-    places = 8 * (lax.broadcasted_iota(jnp.int32, (8, words.shape[1]), 0) & 3)
-    octets = (jnp.right_shift(jnp.broadcast_to(words, places.shape), places) & 255).astype(jnp.float32)
-    far, near = [], []
+    near = []
+    sent = first_piece(place, words, image, 1)
+    far = masked_piece(place, words, image, 1, 0, 2)
+    others = [exchange(cells, 0) for cells in (far[0], sent)]
     for stream in streams:
-        far.append(masked_piece(place, octets, image, 1, stream))
-    others = [exchange(far[stream][0], 0) for stream in streams]
-    for stream in streams:
-        near.append(masked_piece(place, octets, image, 0, stream))
+        near.append(masked_piece(place, words, image, 0, stream, 1))
     cells = [near[stream][0] for stream in streams]
     for step in range(bits - 2):
         pairs = [add_and_part(place, orders[stream][step], cells[stream], others[stream]) for stream in streams]
@@ -434,7 +481,7 @@
     ends = [exchange(others[stream], 0) for stream in streams]
     model = add_models(place, high, low, pieces(1, (0, 1)), twins, model, rows, columns)
     model = add_models(place, high, low, pieces(0, (1,)), others, model, rows, columns)
-    valids = [piece[1] for piece in near + far]
+    valids = [piece[1] for piece in near] + list(far[1:])
     return difference(place, high, low, pieces(1, (1,)), ends, model, image, valids)[None]
 
 

time: 42.3 us -> 41.5 us (0.981)
  local copies, waits for them, and re-layouts: 2.53 us -> 0.66 us
  Pallas kernels: 11 us -> 11.8 us
  waiting for transfers between devices: 9.17 us -> 9.63 us
    unnamed x18 -> x16, local copies, waits for them, and re-layouts: 2.53 us -> 0.66 us
    pallas_call x0 -> x1, Pallas kernels: none -> 1.79 us  [first_piece(): pl.pallas_call(functools.partial(first_kernel, stream), in_specs=[pl.Bloc...]
    pallas_call x4, Pallas kernels: 5.96 us -> 5.31 us  [add_models(): pl.pallas_call(functools.partial(model_kernel, pieces, total_columns, fre...]
    ppermute x18, waiting for transfers between devices: 9.17 us -> 9.63 us  [exchange(): lax.ppermute(cells, 'epoch', [(i, i ^ 1 << bit) for i in range(count)])]
    pallas_call x4 -> x3, Pallas kernels: 0.88 us -> 0.72 us  [masked_piece(): pl.pallas_call(functools.partial(mask_kernel, twin, stream), in_specs=[pl...]
  transfers between devices with their start and end apart: 18 -> 18, of which waited for: 6 -> 6; matrix products, arithmetic and copies ran while one was open for 0% -> 0% of each run, Pallas kernels for 19% -> 18%
where the time goes in v5:
time: 41.5 us; the launch traced here: 41.4 us
  starting transfers between devices  19.1 us (46%)
  Pallas kernels  11.8 us (28%)
  waiting for transfers between devices  9.63 us (23%)
  local copies, waits for them, and re-layouts  0.66 us (2%)
    ppermute x18, starting transfers between devices, exchange(): lax.ppermute(cells, 'epoch', [(i, i ^ 1 << bit) for i in range(count)])  19.1 us
    ppermute x18, waiting for transfers between devices, exchange(): lax.ppermute(cells, 'epoch', [(i, i ^ 1 << bit) for i in range(count)])  9.63 us
    pallas_call x4, Pallas kernels, add_models(): pl.pallas_call(functools.partial(model_kernel, pieces, total_columns, fre...  5.31 us
    pallas_call x1, Pallas kernels, difference(): pl.pallas_call(functools.partial(difference_kernel, pieces), in_specs=[pl...  2.37 us
    pallas_call x1, Pallas kernels, first_piece(): pl.pallas_call(functools.partial(first_kernel, stream), in_specs=[pl.Bloc...  1.79 us
    pallas_call x1, Pallas kernels, weights(): pl.pallas_call(weight_kernel, in_specs=[smem] + [vmem] * len(arrays), out...  1.43 us
  transfers between devices with their start and end apart: 18, of which 6 were waited for; matrix products, arithmetic and copies ran while one was open for 0% of the time, Pallas kernels for 18%

profile of v5, /device:TPU:0, one launch (start us, length us, event | category | flops | bytes accessed | tf_op | source)
XLA Modules:
  0.0 41.4 jit_solution(7874071816691472913)
XLA Ops:
  0.0 1.8 %first_piece.1 = f32[64,1024]{1,0:T(8,128)} custom-call(s32[1]{0:T(128)} %bitcast.place_ref, s32[1,128]{1,0:T(1,128)} %bitcast.12, f32[64,4096]{1,0:T(8,128)} %bitcast.6), custom_call_target="tpu_custom_call" | custom-call | flops 65536 | bytes 524288 | tf_op jit(solution)/shard_map/first_piece/pallas_call | solution.py:114
  1.8 0.6 %collective-permute-start.7 = (f32[64,1024]{1,0:T(8,128)}, f32[64,1024]{1,0:T(8,128)S(1)}, u32[]{:S(2)}, u32[]{:S(2)}) collective-permute-start(f32[64,1024]{1,0:T(8,128)} %first_piece.1), channel_id=1, source_target_pairs={{0,1},{1,0},{2,3},{3,2},{4,5},{5,4},{6,7},{7,6},{8,9},{9,8},{10,11... | collective-permute-start | bytes 786440 | tf_op jit(solution)/shard_map/ppermute | solution.py:416
  3.0 0.8 %collective-permute-done.7.arrived_ref = f32[64,1024]{1,0:T(8,128)S(1)} collective-permute-done((f32[64,1024]{1,0:T(8,128)}, f32[64,1024]{1,0:T(8,128)S(1)}, u32[]{:S(2)}, u32[]{:S(2)}) %collective-permute-start.7) | collective-permute-done | bytes 262176 | tf_op jit(solution)/shard_map/ppermute | solution.py:416
  3.8 3.0 %collective-permute-start.8 = (f32[64,512]{1,0:T(8,128)S(1)}, f32[64,512]{1,0:T(8,128)S(1)}, u32[]{:S(2)}, u32[]{:S(2)}) collective-permute-start(f32[64,512]{1,0:T(8,128)S(1)} %get-tuple-element.32), channel_id=1, source_target_pairs={{0,4},{1,5},{2,6},{3,7},{4,0},{5,1},{6,2},{7,3},{8,12},{9,13},{10,... | collective-permute-start | bytes 393224 | tf_op jit(solution)/shard_map/ppermute | solution.py:416
  7.1 1.6 %collective-permute-start.1 = (f32[64,512]{1,0:T(8,128)S(1)}, f32[64,512]{1,0:T(8,128)S(1)}, u32[]{:S(2)}, u32[]{:S(2)}) collective-permute-start(f32[64,512]{1,0:T(8,128)S(1)} %get-tuple-element.27), channel_id=1, source_target_pairs={{0,2},{1,3},{2,0},{3,1},{4,6},{5,7},{6,4},{7,5},{8,10},{9,11},{10,... | collective-permute-start | bytes 393224 | tf_op jit(solution)/shard_map/ppermute | solution.py:416
  8.6 1.9 %collective-permute-done.8.arrived_ref = f32[64,512]{1,0:T(8,128)S(1)} collective-permute-done((f32[64,512]{1,0:T(8,128)S(1)}, f32[64,512]{1,0:T(8,128)S(1)}, u32[]{:S(2)}, u32[]{:S(2)}) %collective-permute-start.8) | collective-permute-done | bytes 131104 | tf_op jit(solution)/shard_map/ppermute | solution.py:416
  10.6 1.7 %collective-permute-start.9 = (f32[64,256]{1,0:T(8,128)S(1)}, f32[64,256]{1,0:T(8,128)S(1)}, u32[]{:S(2)}, u32[]{:S(2)}) collective-permute-start(f32[64,256]{1,0:T(8,128)S(1)} %get-tuple-element.34), channel_id=1, source_target_pairs={{0,2},{1,3},{2,0},{3,1},{4,6},{5,7},{6,4},{7,5},{8,10},{9,11},{10,... | collective-permute-start | bytes 196616 | tf_op jit(solution)/shard_map/ppermute | solution.py:416
  12.4 1.6 %collective-permute-start.2 = (f32[64,256]{1,0:T(8,128)S(1)}, f32[64,256]{1,0:T(8,128)S(1)}, u32[]{:S(2)}, u32[]{:S(2)}) collective-permute-start(f32[64,256]{1,0:T(8,128)S(1)} %get-tuple-element.29), channel_id=1, source_target_pairs={{0,4},{1,5},{2,6},{3,7},{4,0},{5,1},{6,2},{7,3},{8,12},{9,13},{10,... | collective-permute-start | bytes 196616 | tf_op jit(solution)/shard_map/ppermute | solution.py:416
  14.0 0.9 %collective-permute-done.9 = f32[64,256]{1,0:T(8,128)S(1)} collective-permute-done((f32[64,256]{1,0:T(8,128)S(1)}, f32[64,256]{1,0:T(8,128)S(1)}, u32[]{:S(2)}, u32[]{:S(2)}) %collective-permute-start.9) | collective-permute-done | bytes 65568 | tf_op jit(solution)/shard_map/ppermute | solution.py:416
  14.9 2.8 %collective-permute-start.10 = (f32[64,256]{1,0:T(8,128)S(1)}, f32[64,256]{1,0:T(8,128)S(1)}, u32[]{:S(2)}, u32[]{:S(2)}) collective-permute-start(f32[64,256]{1,0:T(8,128)S(1)} %add.7.kept_ref), channel_id=1, source_target_pairs={{0,8},{1,9},{2,10},{3,11},{4,12},{5,13},{6,14},{7,15},{8,0},{9,1},... | collective-permute-start | bytes 196616 | tf_op jit(solution)/shard_map/ppermute | solution.py:416
  17.8 2.1 %collective-permute-start.3 = (f32[64,256]{1,0:T(8,128)S(1)}, f32[64,256]{1,0:T(8,128)S(1)}, u32[]{:S(2)}, u32[]{:S(2)}) collective-permute-start(f32[64,256]{1,0:T(8,128)S(1)} %add.6.kept_ref), channel_id=1, source_target_pairs={{0,8},{1,9},{2,10},{3,11},{4,12},{5,13},{6,14},{7,15},{8,0},{9,1},... | collective-permute-start | bytes 196616 | tf_op jit(solution)/shard_map/ppermute | solution.py:416
  19.9 2.1 %collective-permute-done.10.arrived_ref = f32[64,256]{1,0:T(8,128)S(1)} collective-permute-done((f32[64,256]{1,0:T(8,128)S(1)}, f32[64,256]{1,0:T(8,128)S(1)}, u32[]{:S(2)}, u32[]{:S(2)}) %collective-permute-start.10) | collective-permute-done | bytes 65568 | tf_op jit(solution)/shard_map/ppermute | solution.py:416
  22.0 1.6 %collective-permute-start.11 = (f32[64,256]{1,0:T(8,128)S(1)}, f32[64,256]{1,0:T(8,128)S(1)}, u32[]{:S(2)}, u32[]{:S(2)}) collective-permute-start(f32[64,256]{1,0:T(8,128)S(1)} %template.3.refs_1_), channel_id=1, source_target_pairs={{0,2},{1,3},{2,0},{3,1},{4,6},{5,7},{6,4},{7,5},{8,10},{9,11},{10,... | collective-permute-start | bytes 196616 | tf_op jit(solution)/shard_map/ppermute | solution.py:416
  23.6 0.6 %copy-done.7 = s32[16]{0:T(128)S(1)} copy-done((s32[16]{0:T(128)S(1)}, s32[16]{0:T(128)}, u32[]{:S(2)}) %copy-start.7) | copy-done | bytes 88
  24.3 1.4 %kernel_weights.1 = (bf16[256,512]{1,0:T(8,128)(2,1)S(1)}, bf16[256,512]{1,0:T(8,128)(2,1)S(1)}) custom-call(s32[1]{0:T(128)} %bitcast.place_ref, s32[1,16]{1,0:T(1,128)S(1)} %bitcast.16, f32[3,16,49]{2,1,0:T(8,128)S(1)} %bitcast.11, f32[16,49]{1,0:T(8,128)S(1)} %copy-done.6, f32[49,16]{1,0:T(8,128)S(1)} %copy-done.3, f32[16,2048]{1,0:T(8,128)S(1)} %copy-done.2, ...), custom_call_target="tpu_custom_call" | custom-call | flops 100000000 | bytes 2000000 | tf_op jit(solution)/shard_map/kernel_weights/pallas_call | solution.py:221
  26.7 1.8 %collective-permute-start.12 = (f32[64,512]{1,0:T(8,128)S(1)}, f32[64,512]{1,0:T(8,128)S(1)}, u32[]{:S(2)}, u32[]{:S(2)}) collective-permute-start(f32[64,512]{1,0:T(8,128)S(1)} %maximum_select_fusion.1), channel_id=1, source_target_pairs={{0,4},{1,5},{2,6},{3,7},{4,0},{5,1},{6,2},{7,3},{8,12},{9,13},{10,... | collective-permute-start | bytes 393224 | tf_op jit(solution)/shard_map/ppermute | solution.py:416
  28.5 2.9 %collective-permute-done.4.refs_0_ = f32[64,256]{1,0:T(8,128)S(1)} collective-permute-done((f32[64,256]{1,0:T(8,128)S(1)}, f32[64,256]{1,0:T(8,128)S(1)}, u32[]{:S(2)}, u32[]{:S(2)}) %collective-permute-start.4) | collective-permute-done | bytes 65568 | tf_op jit(solution)/shard_map/ppermute | solution.py:416
  31.4 0.6 %collective-permute-start.5 = (f32[64,512]{1,0:T(8,128)S(1)}, f32[64,512]{1,0:T(8,128)S(1)}, u32[]{:S(2)}, u32[]{:S(2)}) collective-permute-start(f32[64,512]{1,0:T(8,128)S(1)} %maximum_select_fusion), channel_id=1, source_target_pairs={{0,2},{1,3},{2,0},{3,1},{4,6},{5,7},{6,4},{7,5},{8,10},{9,11},{10,... | collective-permute-start | bytes 393224 | tf_op jit(solution)/shard_map/ppermute | solution.py:416
  31.9 1.1 %add_models.4.refs_4_ = f32[32,4352]{1,0:T(8,128)S(1)} custom-call(s32[1]{0:T(128)} %bitcast.place_ref, bf16[256,512]{1,0:T(8,128)(2,1)S(1)} %get-tuple-element.22.high_ref, bf16[256,512]{1,0:T(8,128)(2,1)S(1)} %get-tuple-element.23.low_ref, f32[64,256]{1,0:T(8,128)S(1)} %template.2.refs_0_, f32[64,256]{1,0:T(8,128)S(1)} %template.3.refs_1_), custom_call_target="tpu_custom_call" | custom-call | flops 603979776 | bytes 491520 | tf_op jit(solution)/shard_map/add_models/pallas_call | solution.py:379
  33.6 1.7 %add_models.5.refs_2_ = f32[32,4352]{1,0:T(8,128)S(1)} custom-call(s32[1]{0:T(128)} %bitcast.place_ref, bf16[256,512]{1,0:T(8,128)(2,1)S(1)} %get-tuple-element.22.high_ref, bf16[256,512]{1,0:T(8,128)(2,1)S(1)} %get-tuple-element.23.low_ref, f32[64,256]{1,0:T(8,128)S(1)} %collective-permute-done.4.refs_0_, ...), custom_call_target="tpu_custom_call", output_to_operand_aliasing={{}: (7, {})} | custom-call | flops 1207959552 | bytes 983040 | tf_op jit(solution)/shard_map/add_models/pallas_call | solution.py:379
  35.4 0.9 %collective-permute-done.5.refs_0_ = f32[64,512]{1,0:T(8,128)S(1)} collective-permute-done((f32[64,512]{1,0:T(8,128)S(1)}, f32[64,512]{1,0:T(8,128)S(1)}, u32[]{:S(2)}, u32[]{:S(2)}) %collective-permute-start.5) | collective-permute-done | bytes 131104 | tf_op jit(solution)/shard_map/ppermute | solution.py:416
  36.4 1.0 %add_models.6.refs_2_ = f32[32,4352]{1,0:T(8,128)S(1)} custom-call(s32[1]{0:T(128)} %bitcast.place_ref, bf16[256,512]{1,0:T(8,128)(2,1)S(1)} %get-tuple-element.22.high_ref, bf16[256,512]{1,0:T(8,128)(2,1)S(1)} %get-tuple-element.23.low_ref, f32[64,256]{1,0:T(8,128)S(1)} %collective-permute-done.14.refs_0_, ...), custom_call_target="tpu_custom_call", output_to_operand_aliasing={{}: (5, {})} | custom-call | flops 603979776 | bytes 491520 | tf_op jit(solution)/shard_map/add_models/pallas_call | solution.py:379
  37.4 1.5 %add_models.7.refs_2_ = f32[32,4352]{1,0:T(8,128)S(1)} custom-call(s32[1]{0:T(128)} %bitcast.place_ref, bf16[256,512]{1,0:T(8,128)(2,1)S(1)} %get-tuple-element.22.high_ref, bf16[256,512]{1,0:T(8,128)(2,1)S(1)} %get-tuple-element.23.low_ref, f32[64,512]{1,0:T(8,128)S(1)} %collective-permute-done.5.refs_0_, ...), custom_call_target="tpu_custom_call", output_to_operand_aliasing={{}: (5, {})} | custom-call | flops 1006632960 | bytes 819200 | tf_op jit(solution)/shard_map/add_models/pallas_call | solution.py:379
  39.0 2.4 %difference.1 = f32[32,4096]{1,0:T(8,128)} custom-call(s32[1]{0:T(128)} %bitcast.place_ref, bf16[256,512]{1,0:T(8,128)(2,1)S(1)} %get-tuple-element.22.high_ref, bf16[256,512]{1,0:T(8,128)(2,1)S(1)} %get-tuple-element.23.low_ref, f32[64,512]{1,0:T(8,128)S(1)} %collective-permute-done.6.refs_0_, f32[64,512]{1,0:T(8,128)S(1)} %collective-permute-done.13.refs_1_, ...), custom_call_target="tpu_custom_call" | custom-call | flops 1006632960 | bytes 819200 | tf_op jit(solution)/shard_map/difference/pallas_call | solution.py:395
  (48 shorter events, 2.7 us)
Async XLA Ops:
  0.0 2.4 %copy-start = (f32[1,64,4096]{2,1,0:T(8,128)S(1)}, f32[1,64,4096]{2,1,0:T(8,128)}, u32[]{:S(2)}) copy-start(f32[1,64,4096]{2,1,0:T(8,128)} %param.8) | copy-start | bytes 3145732
  0.0 2.4 %copy-start.5 = (s32[1,1,128]{2,1,0:T(1,128)S(1)}, s32[1,1,128]{2,1,0:T(1,128)}, u32[]{:S(2)}) copy-start(s32[1,1,128]{2,1,0:T(1,128)} %param.9) | copy-start | bytes 1540
  1.8 1.9 %collective-permute-start.7 = (f32[64,1024]{1,0:T(8,128)}, f32[64,1024]{1,0:T(8,128)S(1)}, u32[]{:S(2)}, u32[]{:S(2)}) collective-permute-start(f32[64,1024]{1,0:T(8,128)} %first_piece.1), channel_id=1, source_target_pairs={{0,1},{1,0},{2,3},{3,2},{4,5},{5,4},{6,7},{7,6},{8,9},{9,8},{10,11... | collective-permute-start | bytes 786440 | tf_op jit(solution)/shard_map/ppermute | solution.py:416
  2.6 4.4 %collective-permute-start = (f32[64,1024]{1,0:T(8,128)S(1)}, f32[64,1024]{1,0:T(8,128)S(1)}, u32[]{:S(2)}, u32[]{:S(2)}) collective-permute-start(f32[64,1024]{1,0:T(8,128)S(1)} %get-tuple-element.25), channel_id=1, source_target_pairs={{0,1},{1,0},{2,3},{3,2},{4,5},{5,4},{6,7},{7,6},{8,9},{9,8},{10,11... | collective-permute-start | bytes 786440 | tf_op jit(solution)/shard_map/ppermute | solution.py:416
  3.8 6.8 %collective-permute-start.8 = (f32[64,512]{1,0:T(8,128)S(1)}, f32[64,512]{1,0:T(8,128)S(1)}, u32[]{:S(2)}, u32[]{:S(2)}) collective-permute-start(f32[64,512]{1,0:T(8,128)S(1)} %get-tuple-element.32), channel_id=1, source_target_pairs={{0,4},{1,5},{2,6},{3,7},{4,0},{5,1},{6,2},{7,3},{8,12},{9,13},{10,... | collective-permute-start | bytes 393224 | tf_op jit(solution)/shard_map/ppermute | solution.py:416
  7.1 5.3 %collective-permute-start.1 = (f32[64,512]{1,0:T(8,128)S(1)}, f32[64,512]{1,0:T(8,128)S(1)}, u32[]{:S(2)}, u32[]{:S(2)}) collective-permute-start(f32[64,512]{1,0:T(8,128)S(1)} %get-tuple-element.27), channel_id=1, source_target_pairs={{0,2},{1,3},{2,0},{3,1},{4,6},{5,7},{6,4},{7,5},{8,10},{9,11},{10,... | collective-permute-start | bytes 393224 | tf_op jit(solution)/shard_map/ppermute | solution.py:416
  10.6 4.3 %collective-permute-start.9 = (f32[64,256]{1,0:T(8,128)S(1)}, f32[64,256]{1,0:T(8,128)S(1)}, u32[]{:S(2)}, u32[]{:S(2)}) collective-permute-start(f32[64,256]{1,0:T(8,128)S(1)} %get-tuple-element.34), channel_id=1, source_target_pairs={{0,2},{1,3},{2,0},{3,1},{4,6},{5,7},{6,4},{7,5},{8,10},{9,11},{10,... | collective-permute-start | bytes 196616 | tf_op jit(solution)/shard_map/ppermute | solution.py:416
  12.4 5.4 %collective-permute-start.2 = (f32[64,256]{1,0:T(8,128)S(1)}, f32[64,256]{1,0:T(8,128)S(1)}, u32[]{:S(2)}, u32[]{:S(2)}) collective-permute-start(f32[64,256]{1,0:T(8,128)S(1)} %get-tuple-element.29), channel_id=1, source_target_pairs={{0,4},{1,5},{2,6},{3,7},{4,0},{5,1},{6,2},{7,3},{8,12},{9,13},{10,... | collective-permute-start | bytes 196616 | tf_op jit(solution)/shard_map/ppermute | solution.py:416
  14.9 8.7 %copy-start.4 = (f32[16,49,3]{1,0,2:T(8,128)S(1)}, f32[16,49,3]{1,0,2:T(8,128)}, u32[]{:S(2)}) copy-start(f32[16,49,3]{1,0,2:T(8,128)} %param.10) | copy-start | bytes 28228
  14.9 8.7 %copy-start.6 = (f32[16,49]{1,0:T(8,128)S(1)}, f32[16,49]{1,0:T(8,128)}, u32[]{:S(2)}) copy-start(f32[16,49]{1,0:T(8,128)} %constant.18.clone.vert_pick_ref) | copy-start | bytes 9412
  14.9 8.7 %copy-start.1 = (f32[15,32,128]{2,1,0:T(8,128)S(1)}, f32[15,32,128]{2,1,0:T(8,128)}, u32[]{:S(2)}) copy-start(f32[15,32,128]{2,1,0:T(8,128)} %constant.21.clone.vert_ref) | copy-start | bytes 737284
  14.9 7.1 %collective-permute-start.10 = (f32[64,256]{1,0:T(8,128)S(1)}, f32[64,256]{1,0:T(8,128)S(1)}, u32[]{:S(2)}, u32[]{:S(2)}) collective-permute-start(f32[64,256]{1,0:T(8,128)S(1)} %add.7.kept_ref), channel_id=1, source_target_pairs={{0,8},{1,9},{2,10},{3,11},{4,12},{5,13},{6,14},{7,15},{8,0},{9,1},... | collective-permute-start | bytes 196616 | tf_op jit(solution)/shard_map/ppermute | solution.py:416
  17.8 5.8 %copy-start.2 = (f32[16,2048]{1,0:T(8,128)S(1)}, f32[16,2048]{1,0:T(8,128)}, u32[]{:S(2)}) copy-start(f32[16,2048]{1,0:T(8,128)} %constant.20.clone.horiz_ref) | copy-start | bytes 393220
  17.8 8.0 %collective-permute-start.3 = (f32[64,256]{1,0:T(8,128)S(1)}, f32[64,256]{1,0:T(8,128)S(1)}, u32[]{:S(2)}, u32[]{:S(2)}) collective-permute-start(f32[64,256]{1,0:T(8,128)S(1)} %add.6.kept_ref), channel_id=1, source_target_pairs={{0,8},{1,9},{2,10},{3,11},{4,12},{5,13},{6,14},{7,15},{8,0},{9,1},... | collective-permute-start | bytes 196616 | tf_op jit(solution)/shard_map/ppermute | solution.py:416
  22.0 4.6 %collective-permute-start.11 = (f32[64,256]{1,0:T(8,128)S(1)}, f32[64,256]{1,0:T(8,128)S(1)}, u32[]{:S(2)}, u32[]{:S(2)}) collective-permute-start(f32[64,256]{1,0:T(8,128)S(1)} %template.3.refs_1_), channel_id=1, source_target_pairs={{0,2},{1,3},{2,0},{3,1},{4,6},{5,7},{6,4},{7,5},{8,10},{9,11},{10,... | collective-permute-start | bytes 196616 | tf_op jit(solution)/shard_map/ppermute | solution.py:416
  25.7 7.4 %collective-permute-start.17 = (f32[64,256]{1,0:T(8,128)S(1)}, f32[64,256]{1,0:T(8,128)S(1)}, u32[]{:S(2)}, u32[]{:S(2)}) collective-permute-start(f32[64,256]{1,0:T(8,128)S(1)} %template.3.refs_1_), channel_id=1, source_target_pairs={{0,1},{1,0},{2,3},{3,2},{4,5},{5,4},{6,7},{7,6},{8,9},{9,8},{10,11... | collective-permute-start | bytes 196616 | tf_op jit(solution)/shard_map/ppermute | solution.py:416
  25.8 7.8 %collective-permute-start.16 = (f32[64,256]{1,0:T(8,128)S(1)}, f32[64,256]{1,0:T(8,128)S(1)}, u32[]{:S(2)}, u32[]{:S(2)}) collective-permute-start(f32[64,256]{1,0:T(8,128)S(1)} %template.2.refs_0_), channel_id=1, source_target_pairs={{0,1},{1,0},{2,3},{3,2},{4,5},{5,4},{6,7},{7,6},{8,9},{9,8},{10,11... | collective-permute-start | bytes 196616 | tf_op jit(solution)/shard_map/ppermute | solution.py:416
  26.4 5.0 %collective-permute-start.4 = (f32[64,256]{1,0:T(8,128)S(1)}, f32[64,256]{1,0:T(8,128)S(1)}, u32[]{:S(2)}, u32[]{:S(2)}) collective-permute-start(f32[64,256]{1,0:T(8,128)S(1)} %template.2.refs_0_), channel_id=1, source_target_pairs={{0,4},{1,5},{2,6},{3,7},{4,0},{5,1},{6,2},{7,3},{8,12},{9,13},{10,... | collective-permute-start | bytes 196616 | tf_op jit(solution)/shard_map/ppermute | solution.py:416
  26.7 8.6 %collective-permute-start.12 = (f32[64,512]{1,0:T(8,128)S(1)}, f32[64,512]{1,0:T(8,128)S(1)}, u32[]{:S(2)}, u32[]{:S(2)}) collective-permute-start(f32[64,512]{1,0:T(8,128)S(1)} %maximum_select_fusion.1), channel_id=1, source_target_pairs={{0,4},{1,5},{2,6},{3,7},{4,0},{5,1},{6,2},{7,3},{8,12},{9,13},{10,... | collective-permute-start | bytes 393224 | tf_op jit(solution)/shard_map/ppermute | solution.py:416
  31.4 5.0 %collective-permute-start.5 = (f32[64,512]{1,0:T(8,128)S(1)}, f32[64,512]{1,0:T(8,128)S(1)}, u32[]{:S(2)}, u32[]{:S(2)}) collective-permute-start(f32[64,512]{1,0:T(8,128)S(1)} %maximum_select_fusion), channel_id=1, source_target_pairs={{0,2},{1,3},{2,0},{3,1},{4,6},{5,7},{6,4},{7,5},{8,10},{9,11},{10,... | collective-permute-start | bytes 393224 | tf_op jit(solution)/shard_map/ppermute | solution.py:416
  33.0 3.4 %collective-permute-start.15 = (f32[64,256]{1,0:T(8,128)S(1)}, f32[64,256]{1,0:T(8,128)S(1)}, u32[]{:S(2)}, u32[]{:S(2)}) collective-permute-start(f32[64,256]{1,0:T(8,128)S(1)} %collective-permute-done.11.refs_1_), channel_id=1, source_target_pairs={{0,1},{1,0},{2,3},{3,2},{4,5},{5,4},{6,7},{7,6},{8,9},{9,8},{10,11... | collective-permute-start | bytes 196616 | tf_op jit(solution)/shard_map/ppermute | solution.py:416
  33.1 3.3 %collective-permute-start.14 = (f32[64,256]{1,0:T(8,128)S(1)}, f32[64,256]{1,0:T(8,128)S(1)}, u32[]{:S(2)}, u32[]{:S(2)}) collective-permute-start(f32[64,256]{1,0:T(8,128)S(1)} %collective-permute-done.4.refs_0_), channel_id=1, source_target_pairs={{0,1},{1,0},{2,3},{3,2},{4,5},{5,4},{6,7},{7,6},{8,9},{9,8},{10,11... | collective-permute-start | bytes 196616 | tf_op jit(solution)/shard_map/ppermute | solution.py:416
  35.3 3.7 %collective-permute-start.13 = (f32[64,512]{1,0:T(8,128)S(1)}, f32[64,512]{1,0:T(8,128)S(1)}, u32[]{:S(2)}, u32[]{:S(2)}) collective-permute-start(f32[64,512]{1,0:T(8,128)S(1)} %collective-permute-done.12.refs_1_), channel_id=1, source_target_pairs={{0,1},{1,0},{2,3},{3,2},{4,5},{5,4},{6,7},{7,6},{8,9},{9,8},{10,11... | collective-permute-start | bytes 393224 | tf_op jit(solution)/shard_map/ppermute | solution.py:416
  36.4 2.6 %collective-permute-start.6 = (f32[64,512]{1,0:T(8,128)S(1)}, f32[64,512]{1,0:T(8,128)S(1)}, u32[]{:S(2)}, u32[]{:S(2)}) collective-permute-start(f32[64,512]{1,0:T(8,128)S(1)} %collective-permute-done.5.refs_0_), channel_id=1, source_target_pairs={{0,1},{1,0},{2,3},{3,2},{4,5},{5,4},{6,7},{7,6},{8,9},{9,8},{10,11... | collective-permute-start | bytes 393224 | tf_op jit(solution)/shard_map/ppermute | solution.py:416
  (2 other events, 2.3 us)
